TPU v7x, 32 devices: a whole 2x2x4 slice. The times are simulated.
32 devices in a mesh: gx: 8 (over z, x), gy: 4 (over y, core).
Axes of the slice: x: 2, y: 2, z: 4, core: 2. Of those that a mesh axis runs over, the one named last changes fastest.
Arguments:
- fields: float32 [13, 8, 64, 512], P(None, None, 'gx', 'gy'), may hold values from -6 to 6
- density: float32 [8, 64, 512], P(None, 'gx', 'gy'), may hold values from 1.8 to 2.6
- fluid_density: float32 [8, 64, 512], P(None, 'gx', 'gy'), may hold values from 0.8 to 1.2
- mobility: float32 [8, 64, 512], P(None, 'gx', 'gy'), may hold values from 0.5 to 4
- lame_lambda: float32 [8, 64, 512], P(None, 'gx', 'gy'), may hold values from 2.5 to 4
- shear_modulus: float32 [8, 64, 512], P(None, 'gx', 'gy'), may hold values from 0.5 to 1.5
- biot_modulus: float32 [8, 64, 512], P(None, 'gx', 'gy'), may hold values from 1 to 3
- biot_coef: float32 [8, 64, 512], P(None, 'gx', 'gy'), may hold values from 0.3 to 0.9
- region_mask: int32 [8, 64, 512], P(None, 'gx', 'gy'), may hold values 0 or 1
- profile_index: int32 [8, 64, 512], P(None, 'gx', 'gy'), may hold values from 0 to 7
- profile_table: float32 [8], replicated, may hold values from 0.05 to 0.4
- source_cells: int32 [64], replicated, may hold values from 0 to 262143
- source_amp: float32 [4, 64], replicated, may hold values from -6 to 6
- receiver_cells: int32 [512], replicated, may hold values from 0 to 262143
- field_cot: float32 [13, 8, 64, 512], P(None, None, 'gx', 'gy'), may hold values from -6 to 6
- receiver_cot: float32 [4, 512], replicated, may hold values from -6 to 6
Outputs:
- field_grad: float32 [13, 8, 64, 512], P(None, None, 'gx', 'gy')
- param_grad: float32 [7, 8, 64, 512], P(None, None, 'gx', 'gy')
Inputs may be any that keep to these rules, and one draw needn't show every extreme that they name: `source_cells`: flat index z * 64 * 512 + x * 512 + y; cells may repeat. `receiver_cells`: flat index z * 64 * 512 + x * 512 + y; cells may repeat.
All inputs are finite; a program needn't handle non-finite values. No bound on the sum of `region_mask` on one device may be relied on, other than what follows from the above.
Results may differ from a plain program's by a relative error of at most 0.000062.
Values sent between devices are 32-bit elements; how exact they have to be, the bound alone decides.
No kernel may reach another device: no remote copies, remote signals or barrier semaphores. Data moves between devices by JAX's collectives and lax.ppermute only.
A program may use at most 64 MiB of HBM per device.

v0:
```python
import functools

import jax
import jax.numpy as jnp
from jax import lax
from jax.experimental import pallas as pl
from jax.experimental.pallas import tpu as pltpu
from jax.sharding import PartitionSpec as P


VX, VY, VZ, WX, WY, WZ, XX, YY, ZZ, YZ, XZ, XY, PP = range(13)
PH, PK, PM, PL, PS, PB, PA, PF = range(8)
EDGE = 8


class W:
    __slots__ = ("m", "h")

    def __init__(self, m, h):
        self.m, self.h = m, h

    def __add__(self, o):
        return W(self.m + o.m, self.h + o.h)

    def __sub__(self, o):
        return W(self.m - o.m, self.h - o.h)

    def __mul__(self, o):
        if isinstance(o, W):
            return W(self.m * o.m, self.h * o.h)
        return W(self.m * o, self.h * o)

    __rmul__ = __mul__

    def __neg__(self):
        return W(-self.m, -self.h)


def roll(x, shift, axis):
    shift %= x.shape[axis]
    return pltpu.roll(x, shift, axis) if shift else x


class Tile:
    def __init__(self, planes, columns, halo):
        self.shape = (planes, columns)
        self.planes, self.columns, self.halo = planes, columns, halo
        self.lane = lax.broadcasted_iota(jnp.int32, self.shape, 1)
        sub = lax.broadcasted_iota(jnp.int32, self.shape, 0)
        self.first, self.last = self.lane == 0, self.lane == columns - 1
        self.bottom, self.top = sub == 0, sub == planes - 1
        self.zero = jnp.zeros(self.shape, jnp.float32)

    def dy(self, w):
        a, b = roll(w.m, -1, 1), roll(w.h, -1, 1)
        c, d = roll(w.m, 1, 1), roll(w.h, 1, 1)
        return W(
            jnp.where(self.last, b, a) - jnp.where(self.first, d, c),
            jnp.where(self.last, a, b) - jnp.where(self.first, c, d),
        )

    def dz1(self, a):
        return jnp.where(self.top, 0.0, roll(a, -1, 0)) - jnp.where(self.bottom, 0.0, roll(a, 1, 0))

    def dz(self, w):
        return W(self.dz1(w.m), self.dz1(w.h))

    def pack(self, tiles):
        width = 2 * self.halo
        group = self.lane // width
        out = []
        per = self.columns // width
        for base in range(0, len(tiles), per):
            total = self.zero
            for j, tile in enumerate(tiles[base : base + per]):
                total = jnp.where(group == j, roll(tile, self.halo + width * j, 1), total)
            out.append(total)
        return out

    def unpack(self, tiles, index):
        width = 2 * self.halo
        per = self.columns // width
        return roll(tiles[index // per], -(self.halo + width * (index % per)), 1)


def dx(get, name, r, low=True, high=True):
    if low and high:
        return get(name, r + 1) - get(name, r - 1)
    return get(name, r + 1) if high else -get(name, r - 1)


def read(ref, *at):
    planes = ref.shape[-2] // 2
    return W(ref[(*at, pl.ds(0, planes))], ref[(*at, pl.ds(planes, planes))])


def write(ref, value, *at):
    planes = ref.shape[-2] // 2
    ref[(*at, pl.ds(0, planes))] = value.m
    ref[(*at, pl.ds(planes, planes))] = value.h


def memo(fn):
    return functools.lru_cache(maxsize=None)(fn)


def momentum(tile, s, r, low=True, high=True):
    forces = [
        dx(s, XX, r, low, high) + tile.dy(s(XY, r)) + tile.dz(s(XZ, r)),
        dx(s, XY, r, low, high) + tile.dy(s(YY, r)) + tile.dz(s(YZ, r)),
        dx(s, XZ, r, low, high) + tile.dy(s(YZ, r)) + tile.dz(s(ZZ, r)),
    ]
    slopes = [dx(s, PP, r, low, high), tile.dy(s(PP, r)), tile.dz(s(PP, r))]
    return forces, slopes


def forward_edge(tile, s, v, p, r, low, high):
    forces, slopes = momentum(tile, s, r, low, high)
    h, k, m = p(PH, r), p(PK, r), p(PM, r)
    out = []
    for i in range(3):
        g = -(slopes[i] + m * v(WX + i, r))
        out.append(v(VX + i, r) + h * (3.0 * forces[i] - g))
        if i == 0:
            drive = v(WX, r) + h * (k * g - forces[0])
    return [s(XX, r), s(XY, r), s(XZ, r), s(PP, r)] + out + [drive]


def adjoint_stress(p, a, r):
    trace = a(XX, r) + a(YY, r) + a(ZZ, r)
    b, pi = p(PB, r), a(PP, r)
    cross = p(PA, r) * b
    common = p(PL, r) * trace - cross * pi
    s = p(PS, r)
    s2 = 2.0 * s
    return {
        XX: common + s2 * a(XX, r),
        YY: common + s2 * a(YY, r),
        ZZ: common + s2 * a(ZZ, r),
        YZ: s * a(YZ, r),
        XZ: s * a(XZ, r),
        XY: s * a(XY, r),
        PP: cross * trace - b * pi,
    }


def adjoint_edge(tile, q, a, p, r, low, high):
    forces, slopes = momentum(tile, q, r, low, high)
    h, k = p(PH, r), p(PK, r)
    out = []
    for i in range(3):
        lv, lw = a(VX + i, r) - forces[i], a(WX + i, r) - slopes[i]
        out.append(h * (3.0 * lv - lw))
        if i == 0:
            drive = h * (k * lw - lv)
    return [q(XX, r), q(XY, r), q(XZ, r), q(PP, r)] + out + [drive]


def send(tile, even, first_rows, last_rows, a_ref, b_ref):
    ups = [w.m for w in first_rows] + tile.pack([w.h for w in first_rows])
    downs = [w.m for w in last_rows] + tile.pack([w.h for w in last_rows])
    for n, (up, down) in enumerate(zip(ups, downs)):
        a_ref[n] = jnp.where(even, down, up)
        b_ref[n] = jnp.where(even, up, down)


def receive(tile, even, a_ref, b_ref, count):
    total = a_ref.shape[0]
    first = [jnp.where(even, b_ref[n], a_ref[n]) for n in range(total)]
    last = [jnp.where(even, a_ref[n], b_ref[n]) for n in range(total)]
    sides = []
    for got in (first, last):
        sides.append([W(got[n], tile.unpack(got[count:], n)) for n in range(count)])
    return sides


def start_kernel(halo, mx_axis, my_axis, fields_ref, cot_ref, par_ref, mask_ref, index_ref, table_ref, p_ref, a_ref, b_ref):
    even = lax.rem(lax.axis_index(my_axis), 2) == 0
    rows = p_ref.shape[1]
    planes, columns = p_ref.shape[2], p_ref.shape[3]
    lane = lax.broadcasted_iota(jnp.int32, (planes, columns), 1)
    group = lane // halo
    per = columns // halo

    def at(r):
        return pl.ds(r, planes, stride=rows)

    for r in range(rows):
        density, fluid, mobility, lame, shear, modulus, coupling = [par_ref[n][0, at(r), :] for n in range(7)]
        lookup = jnp.zeros((planes, columns), jnp.float32)
        index = index_ref[0, at(r), :]
        for n in range(table_ref.shape[1]):
            lookup = jnp.where(index == n, table_ref[0, n], lookup)
        p_ref[PH, r] = 0.25 / (3.0 * density - fluid)
        p_ref[PK, r] = density / fluid
        p_ref[PM, r] = 2.0 * mobility
        p_ref[PL, r] = 0.25 * lame
        p_ref[PS, r] = 0.25 * shear
        p_ref[PB, r] = 0.25 * modulus
        p_ref[PA, r] = coupling
        p_ref[PF, r] = 1.0 - mask_ref[0, at(r), :].astype(jnp.float32) * lookup
    sources = []
    for ref in (fields_ref, cot_ref):
        for f in range(ref.shape[0]):
            for r in range(rows):
                sources.append(lambda ref=ref, f=f, r=r: ref[f, at(r), :])
    for f in range(p_ref.shape[0]):
        for r in range(rows):
            sources.append(lambda f=f, r=r: p_ref[f, r])
    for n in range(a_ref.shape[0]):
        left = jnp.zeros((planes, columns), jnp.float32)
        right = left
        for g in range(per):
            if n * per + g < len(sources):
                x = sources[n * per + g]()
                left = jnp.where(group == g, roll(x, halo * g, 1), left)
                right = jnp.where(group == g, roll(x, halo * g + halo, 1), right)
        a_ref[n] = jnp.where(even, right, left)
        b_ref[n] = jnp.where(even, left, right)


def inject_kernel(halo, rec_ref, cot_ref, src_ref, amp_ref, rec_out, src_out):
    for cells_ref, amounts_ref, out in ((rec_ref, cot_ref, rec_out), (src_ref, amp_ref, src_out)):
        steps, rows, planes2, columns = out.shape
        planes = planes2 // 2
        count = amounts_ref.shape[1]
        row, col = cells_ref[0:1, :], cells_ref[1:2, :]
        row_at = lax.broadcasted_iota(jnp.int32, (rows * planes, count), 0)
        here = row_at == row
        lhs = jnp.concatenate([jnp.where(here, amounts_ref[t : t + 1, :], 0.0) for t in range(steps)], axis=0)
        lane = lax.broadcasted_iota(jnp.int32, (columns, count), 0)
        side = jnp.where(lane < halo, lane + columns, jnp.where(lane >= columns - halo, lane - columns, -columns))
        for half, where in enumerate((lane, side)):
            rhs = (where == col).astype(jnp.float32)
            got = lax.dot_general(
                lhs, rhs, (((1,), (1,)), ((), ())), precision=lax.Precision.HIGHEST, preferred_element_type=jnp.float32
            )
            for t in range(steps):
                for r in range(rows):
                    base = (t * rows + r) * planes
                    out[t, r, pl.ds(half * planes, planes)] = got[base : base + planes]


def spread_kernel(halo, gx_axis, gy_axis, fields_ref, cot_ref, pm_ref, ay_ref, by_ref, rec_ref,
                  f_out, a_out, p_out, a_msg, b_msg):
    even_x = lax.rem(lax.axis_index(gx_axis), 2) == 0
    even_y = lax.rem(lax.axis_index(gy_axis), 2) == 0
    rows, planes, columns = pm_ref.shape[1:]
    tile = Tile(planes, columns, halo)
    per = columns // halo
    packs = ay_ref.shape[0]
    right = [jnp.where(even_y, ay_ref[n], by_ref[n]) for n in range(packs)]
    left = [jnp.where(even_y, by_ref[n], ay_ref[n]) for n in range(packs)]
    on_right, on_left = tile.lane < halo, tile.lane >= columns - halo

    def side(n):
        g = n % per
        a = roll(right[n // per], -halo * g, 1)
        b = roll(left[n // per], columns - halo - halo * g, 1)
        return jnp.where(on_right, a, jnp.where(on_left, b, 0.0))

    def at(r):
        return pl.ds(r, planes, stride=rows)

    count = fields_ref.shape[0]
    for f in range(p_out.shape[0]):
        for r in range(rows):
            write(p_out, W(pm_ref[f, r], side((2 * count + f) * rows + r)), f, r)
    for f in range(count):
        for r in range(rows):
            write(f_out, W(fields_ref[f, at(r), :], side(f * rows + r)), f, r)
            value = W(cot_ref[f, at(r), :], side((count + f) * rows + r))
            if f == PP:
                value = value + read(rec_ref, rec_ref.shape[0] - 1, r)
            write(a_out, value * read(p_out, PF, r), f, r)
    messages(tile, even_x, f_out, a_out, p_out, a_msg, b_msg, True)


def messages(tile, even, f_ref, a_ref, p_ref, a_msg, b_msg, with_params):
    rows = f_ref.shape[1]
    s = lambda f, r: read(f_ref, f, r)
    a = lambda f, r: read(a_ref, f, r)
    p = lambda f, r: read(p_ref, f, r)
    qs = memo(lambda r: adjoint_stress(p, a, r))
    q = lambda f, r: qs(r)[f]
    sides = []
    for r, low, high in ((0, False, True), (rows - 1, True, False)):
        got = forward_edge(tile, s, s, p, r, low, high) + adjoint_edge(tile, q, a, p, r, low, high)
        if with_params:
            got += [p(PH, r), p(PK, r)]
        sides.append(got)
    send(tile, even, *sides, a_msg, b_msg)


def step_kernel(gx_axis, halo, j, steps, *refs):
    refs = list(refs)
    take = lambda n: [refs.pop(0) for _ in range(n)]
    f_ref, a_ref, p_ref, am_ref, bm_ref = take(5)
    first, final = j == 0, j == steps - 1
    store = 2 * j < steps - 1 or False
    keep_f, keep_a = j < steps - 1 - j, j < steps - 1 - j
    hk_ref = None if first else take(1)[0]
    src_ref = rec_ref = None
    if not final:
        src_ref, rec_ref = take(2)
    old_f_ref = old_a_ref = acc_ref = None
    if not keep_f:
        old_f_ref, old_a_ref = take(2)
        if j - 1 >= steps - j:
            acc_ref = take(1)[0]
    rho_ref = None
    if final:
        grad_out, par_out = take(2)
        f_out = a_out = None
    else:
        f_out, a_out, a_msg, b_msg = take(4)
    hk_out = take(1)[0] if first else None
    save_f = save_a = acc_out = None
    if keep_f:
        save_f, save_a = take(2)
    elif not final:
        acc_out = take(1)[0]
    assert not refs

    even = lax.rem(lax.axis_index(gx_axis), 2) == 0
    rows, planes, columns = f_ref.shape[1], f_ref.shape[2] // 2, f_ref.shape[3]
    tile = Tile(planes, columns, halo)
    sides = receive(tile, even, am_ref, bm_ref, 2 * EDGE + (2 if first else 0))
    p = lambda f, r: read(p_ref, f, r)
    old = lambda f, r: read(f_ref, f, r)
    lam = lambda f, r: read(a_ref, f, r)
    hk = []
    for n in range(2):
        if first:
            pair = sides[n][2 * EDGE : 2 * EDGE + 2]
            for m in range(2):
                write(hk_out, pair[m], n, m)
        else:
            pair = [read(hk_ref, n, m) for m in range(2)]
        hk.append(pair)
    slot = {XX: 0, XY: 1, XZ: 2, PP: 3}

    def end(r):
        return 0 if r < 0 else 1

    def s(f, r):
        return old(f, r) if 0 <= r < rows else sides[end(r)][slot[f]]

    @memo
    def velocity(r):
        if 0 <= r < rows:
            forces, slopes = momentum(tile, s, r)
            h, k, m = p(PH, r), p(PK, r), p(PM, r)
            out, pushes = {}, []
            for i in range(3):
                w = old(WX + i, r)
                g = -(slopes[i] + m * w)
                pushes.append(g)
                out[VX + i] = old(VX + i, r) + h * (3.0 * forces[i] - g)
                out[WX + i] = w + h * (k * g - forces[i])
            return out, forces, pushes
        n = end(r)
        got = sides[n][4:8]
        edge = 0 if n == 0 else rows - 1
        h, k = hk[n]
        t = h if n == 0 else -h
        xx, pp = t * old(XX, edge), t * old(PP, edge)
        return {
            VX: got[0] + (3.0 * xx + pp),
            VY: got[1] + 3.0 * (t * old(XY, edge)),
            VZ: got[2] + 3.0 * (t * old(XZ, edge)),
            WX: got[3] - (k * pp + xx),
        }, None, None

    v = lambda f, r: velocity(r)[0][f]

    def strain(r):
        e = [dx(v, VX, r), tile.dy(v(VY, r)), tile.dz(v(VZ, r))]
        g = [
            tile.dz(v(VY, r)) + tile.dy(v(VZ, r)),
            tile.dz(v(VX, r)) + dx(v, VZ, r),
            tile.dy(v(VX, r)) + dx(v, VY, r),
        ]
        dw = dx(v, WX, r) + tile.dy(v(WY, r)) + tile.dz(v(WZ, r))
        return e, g, dw

    qs = memo(lambda r: adjoint_stress(p, lam, r))

    def q(f, r):
        return qs(r)[f] if 0 <= r < rows else sides[end(r)][EDGE + slot[f]]

    @memo
    def cots(r):
        if 0 <= r < rows:
            forces, slopes = momentum(tile, q, r)
            h, k = p(PH, r), p(PK, r)
            cf, cg, vel = [], [], {}
            for i in range(3):
                lv, lw = lam(VX + i, r) - forces[i], lam(WX + i, r) - slopes[i]
                cf.append(h * (3.0 * lv - lw))
                cg.append(h * (k * lw - lv))
                vel[VX + i] = lv
                vel[WX + i] = lw - p(PM, r) * cg[i]
            return cf, cg, vel
        n = end(r)
        got = sides[n][EDGE + 4 : EDGE + 8]
        edge = 0 if n == 0 else rows - 1
        h, k = hk[n]
        t = -h if n == 0 else h
        xx, pp = t * q(XX, edge), t * q(PP, edge)
        return [
            got[0] + (3.0 * xx - pp),
            got[1] + 3.0 * (t * q(XY, edge)),
            got[2] + 3.0 * (t * q(XZ, edge)),
        ], [got[3] + (k * pp - xx)], None

    cF = lambda i, r: cots(r)[0][i]
    cG = lambda i, r: cots(r)[1][i]

    def adjoint_row(r):
        out = dict(cots(r)[2])
        out[XX] = lam(XX, r) - dx(cF, 0, r)
        out[YY] = lam(YY, r) - tile.dy(cF(1, r))
        out[ZZ] = lam(ZZ, r) - tile.dz(cF(2, r))
        out[YZ] = lam(YZ, r) - (tile.dz(cF(1, r)) + tile.dy(cF(2, r)))
        out[XZ] = lam(XZ, r) - (tile.dz(cF(0, r)) + dx(cF, 2, r))
        out[XY] = lam(XY, r) - (tile.dy(cF(0, r)) + dx(cF, 1, r))
        out[PP] = lam(PP, r) + (dx(cG, 0, r) + tile.dy(cG(1, r)) + tile.dz(cG(2, r)))
        return out

    stress_names = (XX, YY, ZZ, YZ, XZ, XY, PP)
    for r in range(rows):
        e, g, dw = strain(r)
        dv = e[0] + e[1] + e[2]
        new, forces, pushes = velocity(r)
        here_f = [x.m for x in forces + pushes] + [old(WX + i, r).m for i in range(3)]
        here_f += [x.m for x in e + g] + [dw.m]
        if not final:
            new = dict(new)
            sh, b = p(PS, r), p(PB, r)
            ab = p(PA, r) * b
            common = p(PL, r) * dv + ab * dw
            for i in range(3):
                new[XX + i] = old(XX + i, r) + (common + 2.0 * (sh * e[i]))
                new[YZ + i] = old(YZ + i, r) + sh * g[i]
            new[PP] = old(PP, r) - (ab * dv + b * dw) + read(src_ref, j, r)
            factor = p(PF, r)
            for f, value in new.items():
                write(f_out, value * factor, f, r)
        back = adjoint_row(r)
        cf, cg = cots(r)[0], cots(r)[1]
        here_a = [x.m for x in cf + cg] + [lam(f, r).m for f in stress_names]
        if final:
            for f, value in back.items():
                grad_out[f, pl.ds(r, planes, stride=rows), :] = value.m
        else:
            back[PP] = back[PP] + read(rec_ref, steps - 2 - j, r)
            for f, value in back.items():
                write(a_out, value * p(PF, r), f, r)
        if keep_f:
            for n, x in enumerate(here_f):
                save_f[n, r] = x
            for n, x in enumerate(here_a):
                save_a[n, r] = x
            continue
        acc = [0.0] * 9 if acc_ref is None else [acc_ref[n, r] for n in range(9)]
        pairs = [(here_f, [old_a_ref[n, r] for n in range(13)])]
        if 2 * j != steps - 1:
            pairs.append(([old_f_ref[n, r] for n in range(16)], here_a))
        for ff, aa in pairs:
            fo, pu, wo, ee, gg, w_ = ff[0:3], ff[3:6], ff[6:9], ff[9:12], ff[12:15], ff[15]
            af, ag, sg, pi = aa[0:3], aa[3:6], aa[6:12], aa[12]
            tr, dd = sg[0] + sg[1] + sg[2], ee[0] + ee[1] + ee[2]
            dot = lambda x, y: x[0] * y[0] + x[1] * y[1] + x[2] * y[2]
            adds = [
                dot(af, fo), dot(ag, pu), dot(af, pu), dot(ag, wo),
                tr * dd, tr * w_, 2.0 * dot(sg[0:3], ee) + dot(sg[3:6], gg), pi * dd, pi * w_,
            ]
            acc = [x + y for x, y in zip(acc, adds)]
        if not final:
            for n, x in enumerate(acc):
                acc_out[n, r] = x
            continue
        a1, a2, a3, a4, b1, b2, b3, b4, b5 = acc
        h4, k, b, al = 4.0 * p_ref[PH, r, pl.ds(0, planes)], p_ref[PK, r, pl.ds(0, planes)], p_ref[PB, r, pl.ds(0, planes)], p_ref[PA, r, pl.ds(0, planes)]
        grads = [
            h4 * (a3 - 3.0 * a1),
            h4 * (a1 + a2 - k * (3.0 * a2 + a3)),
            -2.0 * a4,
            0.25 * b1,
            0.25 * b3,
            0.25 * (al * (b2 - b4) - b5),
            b * (b2 - b4),
        ]
        for n, x in enumerate(grads):
            par_out[n, pl.ds(r, planes, stride=rows), :] = x
    if not final:
        messages(tile, even, f_out, a_out, p_ref, a_msg, b_msg, False)


def pairs(count, odd):
    out = []
    for i in range(odd, count - 1, 2):
        out += [(i, i + 1), (i + 1, i)]
    return out


def exchange(axis, a, b):
    count = lax.axis_size(axis)
    return lax.ppermute(a, axis, pairs(count, 0)), lax.ppermute(b, axis, pairs(count, 1))


def call(kernel, outs, *args, smem=()):
    specs = [
        pl.BlockSpec(memory_space=pltpu.SMEM if n in smem else pltpu.VMEM) for n in range(len(args))
    ]
    return pl.pallas_call(
        kernel,
        out_shape=[jax.ShapeDtypeStruct(s, jnp.float32) for s in outs],
        in_specs=specs,
        out_specs=[pl.BlockSpec(memory_space=pltpu.VMEM)] * len(outs),
        compiler_params=pltpu.CompilerParams(vmem_limit_bytes=48 << 20),
    )(*args)


def local(cells, planes, rows, columns):
    total_x, total_y = rows * lax.axis_size("gx"), columns * lax.axis_size("gy")
    depth, rest = cells // (total_x * total_y), cells % (total_x * total_y)
    x = rest // total_y - lax.axis_index("gx") * rows
    y = rest % total_y - lax.axis_index("gy") * columns
    inside = (x >= 0) & (x < rows)
    return jnp.stack([jnp.where(inside, x * planes + depth, -1), y])


def per_device(
    fields, density, fluid_density, mobility, lame_lambda, shear_modulus, biot_modulus, biot_coef,
    region_mask, profile_index, profile_table, source_cells, source_amp, receiver_cells, field_cot, receiver_cot,
):
    planes, rows, columns = region_mask.shape
    steps = source_amp.shape[0]
    count = fields.shape[0]
    halo = 2 * steps
    assert planes == 8 and columns == 128 and columns % (2 * halo) == 0 and rows > 1
    flat = lambda x: x.reshape(-1, planes * rows, columns)
    fields, field_cot = flat(fields), flat(field_cot)
    raw = [flat(x) for x in (density, fluid_density, mobility, lame_lambda, shear_modulus, biot_modulus, biot_coef)]
    packs = -(-(2 * count + 8) * rows * halo // columns)
    own, wide = (rows, planes, columns), (rows, 2 * planes, columns)

    def start(fields_ref, cot_ref, *refs):
        start_kernel(halo, "gx", "gy", fields_ref, cot_ref, refs[:7], *refs[7:])

    p_own, ay, by = call(
        start, [(8, *own)] + [(packs, planes, columns)] * 2,
        fields, field_cot, *raw, flat(region_mask), flat(profile_index), profile_table[None], smem=(11,),
    )
    ay, by = exchange("gy", ay, by)
    rec, src = call(
        functools.partial(inject_kernel, halo), [(steps, *wide)] * 2,
        local(receiver_cells, planes, rows, columns), receiver_cot,
        local(source_cells, planes, rows, columns), source_amp,
    )
    tiles = lambda n: n + -(-n * 2 * halo // columns)
    f, a, p, am, bm = call(
        functools.partial(spread_kernel, halo, "gx", "gy"),
        [(count, *wide)] * 2 + [(8, *wide)] + [(tiles(2 * EDGE + 2), planes, columns)] * 2,
        fields, field_cot, p_own, ay, by, rec,
    )
    saved, hk, acc = [], None, None
    for j in range(steps):
        am, bm = exchange("gx", am, bm)
        args, outs = [f, a, p, am, bm], []
        final, keep = j == steps - 1, j < steps - 1 - j
        if j:
            args.append(hk)
        if not final:
            args += [src, rec]
            outs += [(count, *wide)] * 2 + [(tiles(2 * EDGE), planes, columns)] * 2
        else:
            outs += [(count, planes * rows, columns), (7, planes * rows, columns)]
        if j == 0:
            outs.append((2, 2, 2 * planes, columns))
        if keep:
            outs += [(16, *own), (13, *own)]
        else:
            args += saved[steps - 1 - j]
            if acc is not None:
                args.append(acc)
            if not final:
                outs.append((9, *own))
        got = list(call(functools.partial(step_kernel, "gx", halo, j, steps), outs, *args))
        if final:
            return got[0].reshape(count, planes, rows, columns), got[1].reshape(7, planes, rows, columns)
        f, a, am, bm = got[:4]
        got = got[4:]
        if j == 0:
            hk = got.pop(0)
        if keep:
            saved.append(got)
        else:
            saved.append(None)
            acc = got[0]


def solution(mesh):
    plane, field = P(None, "gx", "gy"), P(None, None, "gx", "gy")
    in_specs = (field,) + (plane,) * 9 + (P(),) * 4 + (field, P())
    return jax.shard_map(per_device, mesh=mesh, in_specs=in_specs, out_specs=(field, field), check_vma=False)
```

profile of v0, /device:TPU:20, one launch (start us, length us, event | category | flops | bytes accessed | tf_op | source)
XLA Modules:
  0.0 56.1 jit_solution(1934844192330980850)
XLA Ops:
  0.6 0.0 copy-start.15
  0.6 0.6 %copy-done.15 = f32[8]{0:T(128)S(1)} copy-done((f32[8]{0:T(128)S(1)}, f32[8]{0:T(128)}, u32[]{:S(2)}) %copy-start.15) | copy-done | bytes 56
  1.3 0.0 copy-start
  1.3 1.0 %copy-done = f32[13,8,8,128]{3,2,1,0:T(8,128)S(1)} copy-done((f32[13,8,8,128]{3,2,1,0:T(8,128)S(1)}, f32[13,8,8,128]{3,2,1,0:T(8,128)}, u32[]{:S(2)}) %copy-start) | copy-done | bytes 426008
  2.3 0.0 copy-start.2
  2.3 1.0 %copy-done.2 = f32[13,8,8,128]{3,2,1,0:T(8,128)S(1)} copy-done((f32[13,8,8,128]{3,2,1,0:T(8,128)S(1)}, f32[13,8,8,128]{3,2,1,0:T(8,128)}, u32[]{:S(2)}) %copy-start.2) | copy-done | bytes 426008
  3.3 0.0 copy-start.4
  3.3 0.8 %copy-done.4 = f32[8,8,128]{2,1,0:T(8,128)S(1)} copy-done((f32[8,8,128]{2,1,0:T(8,128)S(1)}, f32[8,8,128]{2,1,0:T(8,128)}, u32[]{:S(2)}) %copy-start.4) | copy-done | bytes 32792
  4.1 0.0 copy-start.5
  4.1 0.8 %copy-done.5 = f32[8,8,128]{2,1,0:T(8,128)S(1)} copy-done((f32[8,8,128]{2,1,0:T(8,128)S(1)}, f32[8,8,128]{2,1,0:T(8,128)}, u32[]{:S(2)}) %copy-start.5) | copy-done | bytes 32792
  4.8 0.0 copy-start.6
  4.8 0.8 %copy-done.6 = f32[8,8,128]{2,1,0:T(8,128)S(1)} copy-done((f32[8,8,128]{2,1,0:T(8,128)S(1)}, f32[8,8,128]{2,1,0:T(8,128)}, u32[]{:S(2)}) %copy-start.6) | copy-done | bytes 32792
  5.6 0.0 copy-start.7
  5.6 0.8 %copy-done.7 = f32[8,8,128]{2,1,0:T(8,128)S(1)} copy-done((f32[8,8,128]{2,1,0:T(8,128)S(1)}, f32[8,8,128]{2,1,0:T(8,128)}, u32[]{:S(2)}) %copy-start.7) | copy-done | bytes 32792
  6.3 0.0 copy-start.8
  6.3 0.8 %copy-done.8 = f32[8,8,128]{2,1,0:T(8,128)S(1)} copy-done((f32[8,8,128]{2,1,0:T(8,128)S(1)}, f32[8,8,128]{2,1,0:T(8,128)}, u32[]{:S(2)}) %copy-start.8) | copy-done | bytes 32792
  7.1 0.0 copy-start.9
  7.1 0.8 %copy-done.9 = f32[8,8,128]{2,1,0:T(8,128)S(1)} copy-done((f32[8,8,128]{2,1,0:T(8,128)S(1)}, f32[8,8,128]{2,1,0:T(8,128)}, u32[]{:S(2)}) %copy-start.9) | copy-done | bytes 32792
  7.9 0.0 copy-start.10
  7.9 0.8 %copy-done.10 = f32[8,8,128]{2,1,0:T(8,128)S(1)} copy-done((f32[8,8,128]{2,1,0:T(8,128)S(1)}, f32[8,8,128]{2,1,0:T(8,128)}, u32[]{:S(2)}) %copy-start.10) | copy-done | bytes 32792
  8.6 0.0 copy-start.11
  8.6 0.8 %copy-done.11 = s32[8,8,128]{2,1,0:T(8,128)S(1)} copy-done((s32[8,8,128]{2,1,0:T(8,128)S(1)}, s32[8,8,128]{2,1,0:T(8,128)}, u32[]{:S(2)}) %copy-start.11) | copy-done | bytes 32792
  9.4 0.0 copy-start.12
  9.4 0.8 %copy-done.12 = s32[8,8,128]{2,1,0:T(8,128)S(1)} copy-done((s32[8,8,128]{2,1,0:T(8,128)S(1)}, s32[8,8,128]{2,1,0:T(8,128)}, u32[]{:S(2)}) %copy-start.12) | copy-done | bytes 32792
  10.1 0.0 copy-start.1
  10.1 0.0 copy-start.3
  10.1 1.1 %shard_map.167 = (f32[8,8,8,128]{3,2,1,0:T(8,128)S(1)}, f32[17,8,128]{2,1,0:T(8,128)S(1)}, f32[17,8,128]{2,1,0:T(8,128)S(1)}) custom-call(f32[13,64,128]{2,1,0:T(8,128)S(1)} %bitcast.20, f32[13,64,128]{2,1,0:T(8,128)S(1)} %bitcast.22, f32[1,64,128]{2,1,0:T(8,128)S(1)} %bitcast.24, f32[1,64,128]{2,1,0:T(8,128)S(1)} %bitcast.25, f32[1,64,128]{2,1,0:T(8,128)S(1)} %bitcast.26, ...), custom_call_target="tpu_custom_call" | custom-call | tf_op jit(solution)/shard_map/pallas_call | solution.py:517
  11.3 0.1 collective-permute-start
  11.4 2.5 %collective-permute-start.1 = (f32[17,8,128]{2,1,0:T(8,128)S(1)}, f32[17,8,128]{2,1,0:T(8,128)S(1)}, u32[]{:S(2)}, u32[]{:S(2)}) collective-permute-start(f32[17,8,128]{2,1,0:T(8,128)S(1)} %get-tuple-element.34), channel_id=1, source_target_pairs={{1,2},{2,1},{5,6},{6,5},{9,10},{10,9},{13,14},{14,13},{17,18},{18,... | collective-permute-start | bytes 208904 | tf_op jit(solution)/shard_map/ppermute | solution.py:510
  13.9 0.0 copy-start.17
  13.9 0.6 %copy-done.17 = s32[64]{0:T(128)S(1)} copy-done((s32[64]{0:T(128)S(1)}, s32[64]{0:T(128)}, u32[]{:S(2)}) %copy-start.17) | copy-done | bytes 280
  14.6 0.0 copy-start.16
  14.6 0.7 %copy-done.16 = s32[512]{0:T(512)S(1)} copy-done((s32[512]{0:T(512)S(1)}, s32[512]{0:T(512)}, u32[]{:S(2)}) %copy-start.16) | copy-done | bytes 2072
  15.3 0.0 copy-start.13
  15.3 0.0 copy-start.14
  15.3 0.6 %copy-done.13 = f32[4,512]{1,0:T(4,128)S(1)} copy-done((f32[4,512]{1,0:T(4,128)S(1)}, f32[4,512]{1,0:T(4,128)}, u32[]{:S(2)}) %copy-start.13) | copy-done | bytes 8216
  16.0 0.0 copy-done.14
  16.0 1.2 %shard_map.168 = (f32[4,8,16,128]{3,2,1,0:T(8,128)S(1)}, f32[4,8,16,128]{3,2,1,0:T(8,128)S(1)}) custom-call(s32[2,512]{1,0:T(2,128)S(1)} %pad_add_fusion.rec_ref, f32[4,512]{1,0:T(4,128)S(1)} %copy-done.13, s32[2,64]{1,0:T(2,128)S(1)} %pad_add_fusion.1.src_ref, f32[4,64]{1,0:T(4,128)S(1)} %copy-done.14), custom_call_target="tpu_custom_call" | custom-call | tf_op jit(solution)/shard_map/pallas_call | solution.py:517
  17.2 0.0 collective-permute-done.ay_ref
  17.2 0.0 collective-permute-done.1.by_ref
  17.2 0.0 copy-done.1
  17.2 0.0 copy-done.3
  17.2 0.8 %shard_map.169 = (f32[13,8,16,128]{3,2,1,0:T(8,128)S(1)}, f32[13,8,16,128]{3,2,1,0:T(8,128)S(1)}, f32[8,8,16,128]{3,2,1,0:T(8,128)S(1)}, f32[21,8,128]{2,1,0:T(8,128)S(1)}, f32[21,8,128]{2,1,0:T(8,128)S(1)}) custom-call(f32[13,64,128]{2,1,0:T(8,128)S(1)} %bitcast.21, f32[13,64,128]{2,1,0:T(8,128)S(1)} %bitcast.23, ...), custom_call_target="tpu_custom_call" | custom-call | tf_op jit(solution)/shard_map/pallas_call | solution.py:517
  18.0 1.6 %collective-permute-start.2 = (f32[21,8,128]{2,1,0:T(8,128)S(1)}, f32[21,8,128]{2,1,0:T(8,128)S(1)}, u32[]{:S(2)}, u32[]{:S(2)}) collective-permute-start(f32[21,8,128]{2,1,0:T(8,128)S(1)} %get-tuple-element.39), channel_id=1, source_target_pairs={{0,4},{4,0},{8,12},{12,8},{16,20},{20,16},{24,28},{28,24},{1,5},{5... | collective-permute-start | bytes 258056 | tf_op jit(solution)/shard_map/ppermute | solution.py:510
  19.6 2.3 %collective-permute-start.3 = (f32[21,8,128]{2,1,0:T(8,128)S(1)}, f32[21,8,128]{2,1,0:T(8,128)S(1)}, u32[]{:S(2)}, u32[]{:S(2)}) collective-permute-start(f32[21,8,128]{2,1,0:T(8,128)S(1)} %get-tuple-element.40), channel_id=1, source_target_pairs={{4,8},{8,4},{12,16},{16,12},{20,24},{24,20},{5,9},{9,5},{13,17},{1... | collective-permute-start | bytes 258056 | tf_op jit(solution)/shard_map/ppermute | solution.py:510
  21.9 0.7 %collective-permute-done.2.refs_3_ = f32[21,8,128]{2,1,0:T(8,128)S(1)} collective-permute-done((f32[21,8,128]{2,1,0:T(8,128)S(1)}, f32[21,8,128]{2,1,0:T(8,128)S(1)}, u32[]{:S(2)}, u32[]{:S(2)}) %collective-permute-start.2) | collective-permute-done | bytes 86048 | tf_op jit(solution)/shard_map/ppermute | solution.py:510
  22.6 4.3 %collective-permute-done.3.refs_4_ = f32[21,8,128]{2,1,0:T(8,128)S(1)} collective-permute-done((f32[21,8,128]{2,1,0:T(8,128)S(1)}, f32[21,8,128]{2,1,0:T(8,128)S(1)}, u32[]{:S(2)}, u32[]{:S(2)}) %collective-permute-start.3) | collective-permute-done | bytes 86048 | tf_op jit(solution)/shard_map/ppermute | solution.py:510
  26.9 1.1 %shard_map.170 = (f32[13,8,16,128]{3,2,1,0:T(8,128)S(1)}, f32[13,8,16,128]{3,2,1,0:T(8,128)S(1)}, f32[18,8,128]{2,1,0:T(8,128)S(1)}, f32[18,8,128]{2,1,0:T(8,128...) custom-call(f32[13,8,16,128]{3,2,1,0:T(8,128)S(1)} %get-tuple-element.36.refs_0_,, ...), custom_call_target="tpu_custom_call" | custom-call | tf_op jit(solution)/shard_map/pallas_call | solution.py:517
  28.0 0.6 %collective-permute-start.4 = (f32[18,8,128]{2,1,0:T(8,128)S(1)}, f32[18,8,128]{2,1,0:T(8,128)S(1)}, u32[]{:S(2)}, u32[]{:S(2)}) collective-permute-start(f32[18,8,128]{2,1,0:T(8,128)S(1)} %get-tuple-element.44), channel_id=1, source_target_pairs={{0,4},{4,0},{8,12},{12,8},{16,20},{20,16},{24,28},{28,24},{1,5},{5... | collective-permute-start | bytes 221192 | tf_op jit(solution)/shard_map/ppermute | solution.py:510
  28.6 3.3 %collective-permute-start.5 = (f32[18,8,128]{2,1,0:T(8,128)S(1)}, f32[18,8,128]{2,1,0:T(8,128)S(1)}, u32[]{:S(2)}, u32[]{:S(2)}) collective-permute-start(f32[18,8,128]{2,1,0:T(8,128)S(1)} %get-tuple-element.45), channel_id=1, source_target_pairs={{4,8},{8,4},{12,16},{16,12},{20,24},{24,20},{5,9},{9,5},{13,17},{1... | collective-permute-start | bytes 221192 | tf_op jit(solution)/shard_map/ppermute | solution.py:510
  31.9 0.7 %collective-permute-done.4.refs_3_ = f32[18,8,128]{2,1,0:T(8,128)S(1)} collective-permute-done((f32[18,8,128]{2,1,0:T(8,128)S(1)}, f32[18,8,128]{2,1,0:T(8,128)S(1)}, u32[]{:S(2)}, u32[]{:S(2)}) %collective-permute-start.4) | collective-permute-done | bytes 73760 | tf_op jit(solution)/shard_map/ppermute | solution.py:510
  32.6 3.2 %collective-permute-done.5.refs_4_ = f32[18,8,128]{2,1,0:T(8,128)S(1)} collective-permute-done((f32[18,8,128]{2,1,0:T(8,128)S(1)}, f32[18,8,128]{2,1,0:T(8,128)S(1)}, u32[]{:S(2)}, u32[]{:S(2)}) %collective-permute-start.5) | collective-permute-done | bytes 73760 | tf_op jit(solution)/shard_map/ppermute | solution.py:510
  35.8 1.1 %shard_map.171 = (f32[13,8,16,128]{3,2,1,0:T(8,128)S(1)}, f32[13,8,16,128]{3,2,1,0:T(8,128)S(1)}, f32[18,8,128]{2,1,0:T(8,128)S(1)}, f32[18,8,128]{2,1,0:T(8,128...) custom-call(f32[13,8,16,128]{3,2,1,0:T(8,128)S(1)} %get-tuple-element.42.refs_0_, ...), custom_call_target="tpu_custom_call" | custom-call | tf_op jit(solution)/shard_map/pallas_call | solution.py:517
  36.9 1.6 %collective-permute-start.6 = (f32[18,8,128]{2,1,0:T(8,128)S(1)}, f32[18,8,128]{2,1,0:T(8,128)S(1)}, u32[]{:S(2)}, u32[]{:S(2)}) collective-permute-start(f32[18,8,128]{2,1,0:T(8,128)S(1)} %get-tuple-element.49), channel_id=1, source_target_pairs={{0,4},{4,0},{8,12},{12,8},{16,20},{20,16},{24,28},{28,24},{1,5},{5... | collective-permute-start | bytes 221192 | tf_op jit(solution)/shard_map/ppermute | solution.py:510
  38.4 2.3 %collective-permute-start.7 = (f32[18,8,128]{2,1,0:T(8,128)S(1)}, f32[18,8,128]{2,1,0:T(8,128)S(1)}, u32[]{:S(2)}, u32[]{:S(2)}) collective-permute-start(f32[18,8,128]{2,1,0:T(8,128)S(1)} %get-tuple-element.50), channel_id=1, source_target_pairs={{4,8},{8,4},{12,16},{16,12},{20,24},{24,20},{5,9},{9,5},{13,17},{1... | collective-permute-start | bytes 221192 | tf_op jit(solution)/shard_map/ppermute | solution.py:510
  40.8 0.5 collective-permute-done.6.refs_3_
  41.3 4.3 %collective-permute-done.7.refs_4_ = f32[18,8,128]{2,1,0:T(8,128)S(1)} collective-permute-done((f32[18,8,128]{2,1,0:T(8,128)S(1)}, f32[18,8,128]{2,1,0:T(8,128)S(1)}, u32[]{:S(2)}, u32[]{:S(2)}) %collective-permute-start.7) | collective-permute-done | bytes 73760 | tf_op jit(solution)/shard_map/ppermute | solution.py:510
  45.6 1.2 %shard_map.172 = (f32[13,8,16,128]{3,2,1,0:T(8,128)S(1)}, f32[13,8,16,128]{3,2,1,0:T(8,128)S(1)}, f32[18,8,128]{2,1,0:T(8,128)S(1)}, f32[18,8,128]{2,1,0:T(8,128)S(1)}, f32[9,8,8,128]{3,2,1,0:T(8,128)S(1)}) custom-call(f32[13,8,16,128]{3,2,1,0:T(8,128)S(1)} %get-tuple-element.47.refs_0_, f32[13,8,16,128]{3,2,1,0:T(8,128)S(1)} %get-tuple-element.48.refs_1_, ...), custom_call_target="tpu_custom_call" | custom-call | tf_op jit(solution)/shard_map/pallas_call | solution.py:517
  46.7 0.6 %collective-permute-start.8 = (f32[18,8,128]{2,1,0:T(8,128)S(1)}, f32[18,8,128]{2,1,0:T(8,128)S(1)}, u32[]{:S(2)}, u32[]{:S(2)}) collective-permute-start(f32[18,8,128]{2,1,0:T(8,128)S(1)} %get-tuple-element.55), channel_id=1, source_target_pairs={{0,4},{4,0},{8,12},{12,8},{16,20},{20,16},{24,28},{28,24},{1,5},{5... | collective-permute-start | bytes 221192 | tf_op jit(solution)/shard_map/ppermute | solution.py:510
  47.3 3.3 %collective-permute-start.9 = (f32[18,8,128]{2,1,0:T(8,128)S(1)}, f32[18,8,128]{2,1,0:T(8,128)S(1)}, u32[]{:S(2)}, u32[]{:S(2)}) collective-permute-start(f32[18,8,128]{2,1,0:T(8,128)S(1)} %get-tuple-element.56), channel_id=1, source_target_pairs={{4,8},{8,4},{12,16},{16,12},{20,24},{24,20},{5,9},{9,5},{13,17},{1... | collective-permute-start | bytes 221192 | tf_op jit(solution)/shard_map/ppermute | solution.py:510
  50.6 0.5 collective-permute-done.8.refs_3_
  51.1 3.3 %collective-permute-done.9.refs_4_ = f32[18,8,128]{2,1,0:T(8,128)S(1)} collective-permute-done((f32[18,8,128]{2,1,0:T(8,128)S(1)}, f32[18,8,128]{2,1,0:T(8,128)S(1)}, u32[]{:S(2)}, u32[]{:S(2)}) %collective-permute-start.9) | collective-permute-done | bytes 73760 | tf_op jit(solution)/shard_map/ppermute | solution.py:510
  54.5 1.6 %shard_map.173 = (f32[13,64,128]{2,1,0:T(8,128)}, f32[7,64,128]{2,1,0:T(8,128)}) custom-call(f32[13,8,16,128]{3,2,1,0:T(8,128)S(1)} %get-tuple-element.53.refs_0_, f32[13,8,16,128]{3,2,1,0:T(8,128)S(1)} %get-tuple-element.54.refs_1_, f32[8,8,16,128]{3,2,1,0:T(8,128)S(1)} %get-tuple-element.38.refs_2_, f32[18,8,128]{2,1,0:T(8,128)S(1)} %collective-permute-done.8.refs_3_, ...), custom_call_target="tpu_custom_call" | custom-call | tf_op jit(solution)/shard_map/pallas_call | solution.py:517
  (5 shorter events, 0.1 us)
Async XLA Ops:
  0.6 0.7 %copy-start.15 = (f32[8]{0:T(128)S(1)}, f32[8]{0:T(128)}, u32[]{:S(2)}) copy-start(f32[8]{0:T(128)} %param.26) | copy-start | bytes 100
  1.3 1.0 %copy-start = (f32[13,8,8,128]{3,2,1,0:T(8,128)S(1)}, f32[13,8,8,128]{3,2,1,0:T(8,128)}, u32[]{:S(2)}) copy-start(f32[13,8,8,128]{3,2,1,0:T(8,128)} %param.16) | copy-start | bytes 1277956
  2.3 1.0 %copy-start.2 = (f32[13,8,8,128]{3,2,1,0:T(8,128)S(1)}, f32[13,8,8,128]{3,2,1,0:T(8,128)}, u32[]{:S(2)}) copy-start(f32[13,8,8,128]{3,2,1,0:T(8,128)} %param.30) | copy-start | bytes 1277956
  3.3 0.8 %copy-start.4 = (f32[8,8,128]{2,1,0:T(8,128)S(1)}, f32[8,8,128]{2,1,0:T(8,128)}, u32[]{:S(2)}) copy-start(f32[8,8,128]{2,1,0:T(8,128)} %param.17) | copy-start | bytes 98308
  4.1 0.8 %copy-start.5 = (f32[8,8,128]{2,1,0:T(8,128)S(1)}, f32[8,8,128]{2,1,0:T(8,128)}, u32[]{:S(2)}) copy-start(f32[8,8,128]{2,1,0:T(8,128)} %param.18) | copy-start | bytes 98308
  4.8 0.8 %copy-start.6 = (f32[8,8,128]{2,1,0:T(8,128)S(1)}, f32[8,8,128]{2,1,0:T(8,128)}, u32[]{:S(2)}) copy-start(f32[8,8,128]{2,1,0:T(8,128)} %param.19) | copy-start | bytes 98308
  5.6 0.8 %copy-start.7 = (f32[8,8,128]{2,1,0:T(8,128)S(1)}, f32[8,8,128]{2,1,0:T(8,128)}, u32[]{:S(2)}) copy-start(f32[8,8,128]{2,1,0:T(8,128)} %param.20) | copy-start | bytes 98308
  6.3 0.8 %copy-start.8 = (f32[8,8,128]{2,1,0:T(8,128)S(1)}, f32[8,8,128]{2,1,0:T(8,128)}, u32[]{:S(2)}) copy-start(f32[8,8,128]{2,1,0:T(8,128)} %param.21) | copy-start | bytes 98308
  7.1 0.8 %copy-start.9 = (f32[8,8,128]{2,1,0:T(8,128)S(1)}, f32[8,8,128]{2,1,0:T(8,128)}, u32[]{:S(2)}) copy-start(f32[8,8,128]{2,1,0:T(8,128)} %param.22) | copy-start | bytes 98308
  7.9 0.8 %copy-start.10 = (f32[8,8,128]{2,1,0:T(8,128)S(1)}, f32[8,8,128]{2,1,0:T(8,128)}, u32[]{:S(2)}) copy-start(f32[8,8,128]{2,1,0:T(8,128)} %param.23) | copy-start | bytes 98308
  8.6 0.8 %copy-start.11 = (s32[8,8,128]{2,1,0:T(8,128)S(1)}, s32[8,8,128]{2,1,0:T(8,128)}, u32[]{:S(2)}) copy-start(s32[8,8,128]{2,1,0:T(8,128)} %param.24) | copy-start | bytes 98308
  9.4 0.8 %copy-start.12 = (s32[8,8,128]{2,1,0:T(8,128)S(1)}, s32[8,8,128]{2,1,0:T(8,128)}, u32[]{:S(2)}) copy-start(s32[8,8,128]{2,1,0:T(8,128)} %param.25) | copy-start | bytes 98308
  10.1 7.1 %copy-start.1 = (f32[13,8,8,128]{3,2,1,0:T(8,128)S(1)}, f32[13,8,8,128]{3,2,1,0:T(8,128)}, u32[]{:S(2)}) copy-start(f32[13,8,8,128]{3,2,1,0:T(8,128)} %param.16) | copy-start | bytes 1277956
  10.1 7.1 %copy-start.3 = (f32[13,8,8,128]{3,2,1,0:T(8,128)S(1)}, f32[13,8,8,128]{3,2,1,0:T(8,128)}, u32[]{:S(2)}) copy-start(f32[13,8,8,128]{3,2,1,0:T(8,128)} %param.30) | copy-start | bytes 1277956
  11.3 5.9 %collective-permute-start = (f32[17,8,128]{2,1,0:T(8,128)S(1)}, f32[17,8,128]{2,1,0:T(8,128)S(1)}, u32[]{:S(2)}, u32[]{:S(2)}) collective-permute-start(f32[17,8,128]{2,1,0:T(8,128)S(1)} %get-tuple-element.33), channel_id=1, source_target_pairs={{0,1},{1,0},{2,3},{3,2},{4,5},{5,4},{6,7},{7,6},{8,9},{9,8},{10,11... | collective-permute-start | bytes 208904 | tf_op jit(solution)/shard_map/ppermute | solution.py:510
  11.4 5.8 %collective-permute-start.1 = (f32[17,8,128]{2,1,0:T(8,128)S(1)}, f32[17,8,128]{2,1,0:T(8,128)S(1)}, u32[]{:S(2)}, u32[]{:S(2)}) collective-permute-start(f32[17,8,128]{2,1,0:T(8,128)S(1)} %get-tuple-element.34), channel_id=1, source_target_pairs={{1,2},{2,1},{5,6},{6,5},{9,10},{10,9},{13,14},{14,13},{17,18},{18,... | collective-permute-start | bytes 208904 | tf_op jit(solution)/shard_map/ppermute | solution.py:510
  13.9 0.7 %copy-start.17 = (s32[64]{0:T(128)S(1)}, s32[64]{0:T(128)}, u32[]{:S(2)}) copy-start(s32[64]{0:T(128)} %param.27) | copy-start | bytes 772
  14.6 0.7 %copy-start.16 = (s32[512]{0:T(512)S(1)}, s32[512]{0:T(512)}, u32[]{:S(2)}) copy-start(s32[512]{0:T(512)} %param.29) | copy-start | bytes 6148
  15.3 0.7 %copy-start.13 = (f32[4,512]{1,0:T(4,128)S(1)}, f32[4,512]{1,0:T(4,128)}, u32[]{:S(2)}) copy-start(f32[4,512]{1,0:T(4,128)} %cot_ref.1) | copy-start | bytes 24580
  15.3 0.7 %copy-start.14 = (f32[4,64]{1,0:T(4,128)S(1)}, f32[4,64]{1,0:T(4,128)}, u32[]{:S(2)}) copy-start(f32[4,64]{1,0:T(4,128)} %amp_ref.1) | copy-start | bytes 3076
  18.0 4.6 %collective-permute-start.2 = (f32[21,8,128]{2,1,0:T(8,128)S(1)}, f32[21,8,128]{2,1,0:T(8,128)S(1)}, u32[]{:S(2)}, u32[]{:S(2)}) collective-permute-start(f32[21,8,128]{2,1,0:T(8,128)S(1)} %get-tuple-element.39), channel_id=1, source_target_pairs={{0,4},{4,0},{8,12},{12,8},{16,20},{20,16},{24,28},{28,24},{1,5},{5... | collective-permute-start | bytes 258056 | tf_op jit(solution)/shard_map/ppermute | solution.py:510
  19.6 7.3 %collective-permute-start.3 = (f32[21,8,128]{2,1,0:T(8,128)S(1)}, f32[21,8,128]{2,1,0:T(8,128)S(1)}, u32[]{:S(2)}, u32[]{:S(2)}) collective-permute-start(f32[21,8,128]{2,1,0:T(8,128)S(1)} %get-tuple-element.40), channel_id=1, source_target_pairs={{4,8},{8,4},{12,16},{16,12},{20,24},{24,20},{5,9},{9,5},{13,17},{1... | collective-permute-start | bytes 258056 | tf_op jit(solution)/shard_map/ppermute | solution.py:510
  28.0 4.6 %collective-permute-start.4 = (f32[18,8,128]{2,1,0:T(8,128)S(1)}, f32[18,8,128]{2,1,0:T(8,128)S(1)}, u32[]{:S(2)}, u32[]{:S(2)}) collective-permute-start(f32[18,8,128]{2,1,0:T(8,128)S(1)} %get-tuple-element.44), channel_id=1, source_target_pairs={{0,4},{4,0},{8,12},{12,8},{16,20},{20,16},{24,28},{28,24},{1,5},{5... | collective-permute-start | bytes 221192 | tf_op jit(solution)/shard_map/ppermute | solution.py:510
  28.6 7.2 %collective-permute-start.5 = (f32[18,8,128]{2,1,0:T(8,128)S(1)}, f32[18,8,128]{2,1,0:T(8,128)S(1)}, u32[]{:S(2)}, u32[]{:S(2)}) collective-permute-start(f32[18,8,128]{2,1,0:T(8,128)S(1)} %get-tuple-element.45), channel_id=1, source_target_pairs={{4,8},{8,4},{12,16},{16,12},{20,24},{24,20},{5,9},{9,5},{13,17},{1... | collective-permute-start | bytes 221192 | tf_op jit(solution)/shard_map/ppermute | solution.py:510
  36.9 4.4 %collective-permute-start.6 = (f32[18,8,128]{2,1,0:T(8,128)S(1)}, f32[18,8,128]{2,1,0:T(8,128)S(1)}, u32[]{:S(2)}, u32[]{:S(2)}) collective-permute-start(f32[18,8,128]{2,1,0:T(8,128)S(1)} %get-tuple-element.49), channel_id=1, source_target_pairs={{0,4},{4,0},{8,12},{12,8},{16,20},{20,16},{24,28},{28,24},{1,5},{5... | collective-permute-start | bytes 221192 | tf_op jit(solution)/shard_map/ppermute | solution.py:510
  38.4 7.1 %collective-permute-start.7 = (f32[18,8,128]{2,1,0:T(8,128)S(1)}, f32[18,8,128]{2,1,0:T(8,128)S(1)}, u32[]{:S(2)}, u32[]{:S(2)}) collective-permute-start(f32[18,8,128]{2,1,0:T(8,128)S(1)} %get-tuple-element.50), channel_id=1, source_target_pairs={{4,8},{8,4},{12,16},{16,12},{20,24},{24,20},{5,9},{9,5},{13,17},{1... | collective-permute-start | bytes 221192 | tf_op jit(solution)/shard_map/ppermute | solution.py:510
  46.7 4.4 %collective-permute-start.8 = (f32[18,8,128]{2,1,0:T(8,128)S(1)}, f32[18,8,128]{2,1,0:T(8,128)S(1)}, u32[]{:S(2)}, u32[]{:S(2)}) collective-permute-start(f32[18,8,128]{2,1,0:T(8,128)S(1)} %get-tuple-element.55), channel_id=1, source_target_pairs={{0,4},{4,0},{8,12},{12,8},{16,20},{20,16},{24,28},{28,24},{1,5},{5... | collective-permute-start | bytes 221192 | tf_op jit(solution)/shard_map/ppermute | solution.py:510
  47.3 7.1 %collective-permute-start.9 = (f32[18,8,128]{2,1,0:T(8,128)S(1)}, f32[18,8,128]{2,1,0:T(8,128)S(1)}, u32[]{:S(2)}, u32[]{:S(2)}) collective-permute-start(f32[18,8,128]{2,1,0:T(8,128)S(1)} %get-tuple-element.56), channel_id=1, source_target_pairs={{4,8},{8,4},{12,16},{16,12},{20,24},{24,20},{5,9},{9,5},{13,17},{1... | collective-permute-start | bytes 221192 | tf_op jit(solution)/shard_map/ppermute | solution.py:510
where the time goes:
time: 57.1 us; the launch traced here: 56.1 us
  starting transfers between devices  18.1 us (32%)
  waiting for transfers between devices  17.5 us (31%)
  local copies, waits for them, and re-layouts  11.5 us (20%)
  Pallas kernels  8.19 us (14%)
  between operations  0.83 us (1%)
    ppermute x5, waiting for transfers between devices, exchange(): lax.ppermute(b, axis, pairs(count, 1))  15 us
    ppermute x5, starting transfers between devices, exchange(): lax.ppermute(b, axis, pairs(count, 1))  13.7 us
    unnamed x36, local copies, waits for them, and re-layouts  11.5 us
    pallas_call x7, Pallas kernels, call(): pl.pallas_call(kernel, out_shape=[jax.ShapeDtypeStruct(s, jnp.float32) fo...  8.19 us
    ppermute x5, starting transfers between devices, exchange(): lax.ppermute(a, axis, pairs(count, 0))  4.38 us
    ppermute x5, waiting for transfers between devices, exchange(): lax.ppermute(a, axis, pairs(count, 0))  2.47 us
  transfers between devices with their start and end apart: 10, of which 8 were waited for; matrix products, arithmetic and copies ran while one was open for 0% of the time, Pallas kernels for 2%

commit v1 on v0

--- a/solution.py
+++ b/solution.py
@@ -174,7 +174,19 @@
     return sides
 
 
-def start_kernel(halo, mx_axis, my_axis, fields_ref, cot_ref, par_ref, mask_ref, index_ref, table_ref, p_ref, a_ref, b_ref):
+def start_kernel(halo, my_axis, inputs, outs, scratch):
+    par_hbm, (mask_hbm, index_hbm, table_hbm), rest_hbm = inputs[:7], inputs[7:10], inputs[10:]
+    p_ref, a_ref, b_ref, *rest = outs
+    par_ref, mask_ref, index_ref, table_ref, sems = scratch
+    fields_ref, cot_ref = rest[:2]
+    copies = [pltpu.make_async_copy(src, par_ref.at[n], sems.at[n]) for n, src in enumerate(par_hbm)]
+    for src, dst in zip((table_hbm, mask_hbm, index_hbm, *rest_hbm), (table_ref, mask_ref, index_ref, *rest)):
+        copies.append(pltpu.make_async_copy(src, dst, sems.at[len(copies)]))
+    for copy in copies:
+        copy.start()
+    for copy in copies[:10]:
+        copy.wait()
+
     even = lax.rem(lax.axis_index(my_axis), 2) == 0
     rows = p_ref.shape[1]
     planes, columns = p_ref.shape[2], p_ref.shape[3]
@@ -186,7 +198,7 @@
         return pl.ds(r, planes, stride=rows)
 
     for r in range(rows):
-        density, fluid, mobility, lame, shear, modulus, coupling = [par_ref[n][0, at(r), :] for n in range(7)]
+        density, fluid, mobility, lame, shear, modulus, coupling = [par_ref[n, 0, at(r), :] for n in range(7)]
         lookup = jnp.zeros((planes, columns), jnp.float32)
         index = index_ref[0, at(r), :]
         for n in range(table_ref.shape[1]):
@@ -200,14 +212,19 @@
         p_ref[PA, r] = coupling
         p_ref[PF, r] = 1.0 - mask_ref[0, at(r), :].astype(jnp.float32) * lookup
     sources = []
+    for f in range(p_ref.shape[0]):
+        for r in range(rows):
+            sources.append(lambda f=f, r=r: p_ref[f, r])
     for ref in (fields_ref, cot_ref):
         for f in range(ref.shape[0]):
             for r in range(rows):
                 sources.append(lambda ref=ref, f=f, r=r: ref[f, at(r), :])
-    for f in range(p_ref.shape[0]):
-        for r in range(rows):
-            sources.append(lambda f=f, r=r: p_ref[f, r])
+    waited = False
     for n in range(a_ref.shape[0]):
+        if (n + 1) * per > p_ref.shape[0] * rows and not waited:
+            for copy in copies[10:]:
+                copy.wait()
+            waited = True
         left = jnp.zeros((planes, columns), jnp.float32)
         right = left
         for g in range(per):
@@ -219,12 +236,18 @@
         b_ref[n] = jnp.where(even, left, right)
 
 
-def inject_kernel(halo, rec_ref, cot_ref, src_ref, amp_ref, rec_out, src_out):
+def inject_kernel(halo, gx_axis, gy_axis, rec_ref, cot_ref, src_ref, amp_ref, rec_out, src_out):
     for cells_ref, amounts_ref, out in ((rec_ref, cot_ref, rec_out), (src_ref, amp_ref, src_out)):
         steps, rows, planes2, columns = out.shape
         planes = planes2 // 2
         count = amounts_ref.shape[1]
-        row, col = cells_ref[0:1, :], cells_ref[1:2, :]
+        total_x, total_y = rows * lax.axis_size(gx_axis), columns * lax.axis_size(gy_axis)
+        cells = cells_ref[...]
+        line = lax.div(cells, jnp.full_like(cells, total_y))
+        depth = lax.div(line, jnp.full_like(cells, total_x))
+        col = cells - line * total_y - lax.axis_index(gy_axis) * columns
+        x = line - depth * total_x - lax.axis_index(gx_axis) * rows
+        row = jnp.where((x >= 0) & (x < rows), x * planes + depth, -1)
         row_at = lax.broadcasted_iota(jnp.int32, (rows * planes, count), 0)
         here = row_at == row
         lhs = jnp.concatenate([jnp.where(here, amounts_ref[t : t + 1, :], 0.0) for t in range(steps)], axis=0)
@@ -262,14 +285,14 @@
     def at(r):
         return pl.ds(r, planes, stride=rows)
 
-    count = fields_ref.shape[0]
+    count, base = fields_ref.shape[0], p_out.shape[0]
     for f in range(p_out.shape[0]):
         for r in range(rows):
-            write(p_out, W(pm_ref[f, r], side((2 * count + f) * rows + r)), f, r)
+            write(p_out, W(pm_ref[f, r], side(f * rows + r)), f, r)
     for f in range(count):
         for r in range(rows):
-            write(f_out, W(fields_ref[f, at(r), :], side(f * rows + r)), f, r)
-            value = W(cot_ref[f, at(r), :], side((count + f) * rows + r))
+            write(f_out, W(fields_ref[f, at(r), :], side((base + f) * rows + r)), f, r)
+            value = W(cot_ref[f, at(r), :], side((base + count + f) * rows + r))
             if f == PP:
                 value = value + read(rec_ref, rec_ref.shape[0] - 1, r)
             write(a_out, value * read(p_out, PF, r), f, r)
@@ -297,7 +320,6 @@
     take = lambda n: [refs.pop(0) for _ in range(n)]
     f_ref, a_ref, p_ref, am_ref, bm_ref = take(5)
     first, final = j == 0, j == steps - 1
-    store = 2 * j < steps - 1 or False
     keep_f, keep_a = j < steps - 1 - j, j < steps - 1 - j
     hk_ref = None if first else take(1)[0]
     src_ref = rec_ref = None
@@ -308,7 +330,6 @@
         old_f_ref, old_a_ref = take(2)
         if j - 1 >= steps - j:
             acc_ref = take(1)[0]
-    rho_ref = None
     if final:
         grad_out, par_out = take(2)
         f_out = a_out = None
@@ -510,26 +531,15 @@
     return lax.ppermute(a, axis, pairs(count, 0)), lax.ppermute(b, axis, pairs(count, 1))
 
 
-def call(kernel, outs, *args, smem=()):
-    specs = [
-        pl.BlockSpec(memory_space=pltpu.SMEM if n in smem else pltpu.VMEM) for n in range(len(args))
-    ]
+def call(kernel, outs, *args):
+    shapes = [o if isinstance(o, jax.ShapeDtypeStruct) else jax.ShapeDtypeStruct(o, jnp.float32) for o in outs]
     return pl.pallas_call(
         kernel,
-        out_shape=[jax.ShapeDtypeStruct(s, jnp.float32) for s in outs],
-        in_specs=specs,
+        out_shape=shapes,
+        in_specs=[pl.BlockSpec(memory_space=pltpu.VMEM)] * len(args),
         out_specs=[pl.BlockSpec(memory_space=pltpu.VMEM)] * len(outs),
         compiler_params=pltpu.CompilerParams(vmem_limit_bytes=48 << 20),
     )(*args)
-
-
-def local(cells, planes, rows, columns):
-    total_x, total_y = rows * lax.axis_size("gx"), columns * lax.axis_size("gy")
-    depth, rest = cells // (total_x * total_y), cells % (total_x * total_y)
-    x = rest // total_y - lax.axis_index("gx") * rows
-    y = rest % total_y - lax.axis_index("gy") * columns
-    inside = (x >= 0) & (x < rows)
-    return jnp.stack([jnp.where(inside, x * planes + depth, -1), y])
 
 
 def per_device(
@@ -540,26 +550,39 @@
     steps = source_amp.shape[0]
     count = fields.shape[0]
     halo = 2 * steps
-    assert planes == 8 and columns == 128 and columns % (2 * halo) == 0 and rows > 1
+    assert steps % 2 == 0 and planes == 8 and columns == 128 and columns % (2 * halo) == 0 and rows > 1
     flat = lambda x: x.reshape(-1, planes * rows, columns)
     fields, field_cot = flat(fields), flat(field_cot)
     raw = [flat(x) for x in (density, fluid_density, mobility, lame_lambda, shear_modulus, biot_modulus, biot_coef)]
     packs = -(-(2 * count + 8) * rows * halo // columns)
     own, wide = (rows, planes, columns), (rows, 2 * planes, columns)
 
-    def start(fields_ref, cot_ref, *refs):
-        start_kernel(halo, "gx", "gy", fields_ref, cot_ref, refs[:7], *refs[7:])
-
-    p_own, ay, by = call(
-        start, [(8, *own)] + [(packs, planes, columns)] * 2,
-        fields, field_cot, *raw, flat(region_mask), flat(profile_index), profile_table[None], smem=(11,),
-    )
+    table = profile_table[None]
+    small = [receiver_cells[None], receiver_cot, source_cells[None], source_amp]
+    inputs = [*raw, table, flat(region_mask), flat(profile_index), fields, field_cot, *small]
+    whole = [fields, field_cot, *small]
+    plane = (planes * rows, columns)
+
+    def start(*refs):
+        refs = list(refs)
+        hbm = refs[:7] + refs[8:10] + refs[7:8] + refs[10:16]
+        start_kernel(halo, "gy", hbm, refs[16:25], refs[25:])
+
+    p_own, ay, by, fields, field_cot, *small = pl.pallas_call(
+        start,
+        out_shape=[jax.ShapeDtypeStruct(s, jnp.float32) for s in [(8, *own)] + [(packs, planes, columns)] * 2]
+        + [jax.ShapeDtypeStruct(x.shape, x.dtype) for x in whole],
+        in_specs=[pl.BlockSpec(memory_space=pltpu.HBM)] * 16,
+        out_specs=[pl.BlockSpec(memory_space=pltpu.VMEM)] * 9,
+        scratch_shapes=[
+            pltpu.VMEM((7, 1, *plane), jnp.float32), pltpu.VMEM((1, *plane), jnp.int32),
+            pltpu.VMEM((1, *plane), jnp.int32), pltpu.SMEM(table.shape, jnp.float32),
+            pltpu.SemaphoreType.DMA((16,)),
+        ],
+        compiler_params=pltpu.CompilerParams(vmem_limit_bytes=48 << 20),
+    )(*[pltpu.with_memory_space_constraint(x, pltpu.HBM) for x in inputs])
     ay, by = exchange("gy", ay, by)
-    rec, src = call(
-        functools.partial(inject_kernel, halo), [(steps, *wide)] * 2,
-        local(receiver_cells, planes, rows, columns), receiver_cot,
-        local(source_cells, planes, rows, columns), source_amp,
-    )
+    rec, src = call(functools.partial(inject_kernel, halo, "gx", "gy"), [(steps, *wide)] * 2, *small)
     tiles = lambda n: n + -(-n * 2 * halo // columns)
     f, a, p, am, bm = call(
         functools.partial(spread_kernel, halo, "gx", "gy"),

time: 57.1 us -> 48.2 us (0.84)
  the two profiles are of different devices: /device:TPU:20 before, /device:TPU:14 now
where the time goes in v1:
time: 48.2 us; the launch traced here: 48 us
  starting transfers between devices  22.8 us (47%)
  waiting for transfers between devices  15.4 us (32%)
  Pallas kernels  9.01 us (19%)
  between operations  0.76 us (2%)
    ppermute x5, starting transfers between devices, exchange(): lax.ppermute(b, axis, pairs(count, 1))  17.7 us
    ppermute x5, waiting for transfers between devices, exchange(): lax.ppermute(b, axis, pairs(count, 1))  15.4 us
    pallas_call x6, Pallas kernels, call(): pl.pallas_call(kernel, out_shape=shapes, in_specs=[pl.BlockSpec(memory_sp...  7.06 us
    ppermute x5, starting transfers between devices, exchange(): lax.ppermute(a, axis, pairs(count, 0))  5.12 us
    pallas_call x1, Pallas kernels, per_device(): pl.pallas_call(start, out_shape=[jax.ShapeDtypeStruct(s, jnp.float32) for...  1.95 us
  transfers between devices with their start and end apart: 10, of which 5 were waited for; matrix products, arithmetic and copies ran while one was open for 0% of the time, Pallas kernels for 3%

profile of v1, /device:TPU:14, one launch (start us, length us, event | category | flops | bytes accessed | tf_op | source)
XLA Modules:
  0.0 48.0 jit_solution(1941436566618499003)
XLA Ops:
  0.6 1.9 %shard_map.167 = (f32[8,8,8,128]{3,2,1,0:T(8,128)S(1)}, f32[17,8,128]{2,1,0:T(8,128)S(1)}, f32[17,8,128]{2,1,0:T(8,128)S(1)}, f32[13,64,128]{2,1,0:T(8,128)S(1)}...) custom-call(f32[1,64,128]{2,1,0:T(8,128)} %bitcast.18, ...), custom_call_target="tpu_custom_call" | custom-call | tf_op jit(solution)/shard_map/pallas_call | solution.py:571
  2.6 0.1 collective-permute-start
  2.7 2.5 %collective-permute-start.1 = (f32[17,8,128]{2,1,0:T(8,128)S(1)}, f32[17,8,128]{2,1,0:T(8,128)S(1)}, u32[]{:S(2)}, u32[]{:S(2)}) collective-permute-start(f32[17,8,128]{2,1,0:T(8,128)S(1)} %get-tuple-element.42), channel_id=1, source_target_pairs={{1,2},{2,1},{5,6},{6,5},{9,10},{10,9},{13,14},{14,13},{17,18},{18,... | collective-permute-start | bytes 208904 | tf_op jit(solution)/shard_map/ppermute | solution.py:531
  5.2 1.2 %shard_map.168 = (f32[4,8,16,128]{3,2,1,0:T(8,128)S(1)}, f32[4,8,16,128]{3,2,1,0:T(8,128)S(1)}) custom-call(s32[1,512]{1,0:T(1,128)S(1)} %get-tuple-element.43.rec_ref, f32[4,512]{1,0:T(4,128)S(1)} %get-tuple-element.44.cot_ref, s32[1,64]{1,0:T(1,128)S(1)} %get-tuple-element.45.src_ref, f32[4,64]{1,0:T(4,128)S(1)} %get-tuple-element.46.amp_ref), custom_call_target="tpu_custom_call" | custom-call | tf_op jit(solution)/shard_map/pallas_call | solution.py:536
  6.4 0.0 collective-permute-done.ay_ref
  6.4 1.9 %collective-permute-done.1.by_ref = f32[17,8,128]{2,1,0:T(8,128)S(1)} collective-permute-done((f32[17,8,128]{2,1,0:T(8,128)S(1)}, f32[17,8,128]{2,1,0:T(8,128)S(1)}, u32[]{:S(2)}, u32[]{:S(2)}) %collective-permute-start.1) | collective-permute-done | bytes 69664 | tf_op jit(solution)/shard_map/ppermute | solution.py:531
  8.3 0.8 %shard_map.169 = (f32[13,8,16,128]{3,2,1,0:T(8,128)S(1)}, f32[13,8,16,128]{3,2,1,0:T(8,128)S(1)}, f32[8,8,16,128]{3,2,1,0:T(8,128)S(1)}, f32[21,8,128]{2,1,0:T(8,128)S(1)}, f32[21,8,128]{2,1,0:T(8,128)S(1)}) custom-call(f32[13,64,128]{2,1,0:T(8,128)S(1)} %get-tuple-element.38.fields_ref, f32[13,64,128]{2,1,0:T(8,128)S(1)} %get-tuple-element.39.cot_ref, ...), custom_call_target="tpu_custom_call" | custom-call | tf_op jit(solution)/shard_map/pallas_call | solution.py:536
  9.1 0.6 %collective-permute-start.2 = (f32[21,8,128]{2,1,0:T(8,128)S(1)}, f32[21,8,128]{2,1,0:T(8,128)S(1)}, u32[]{:S(2)}, u32[]{:S(2)}) collective-permute-start(f32[21,8,128]{2,1,0:T(8,128)S(1)} %get-tuple-element.51), channel_id=1, source_target_pairs={{0,4},{4,0},{8,12},{12,8},{16,20},{20,16},{24,28},{28,24},{1,5},{5... | collective-permute-start | bytes 258056 | tf_op jit(solution)/shard_map/ppermute | solution.py:531
  9.7 4.4 %collective-permute-start.3 = (f32[21,8,128]{2,1,0:T(8,128)S(1)}, f32[21,8,128]{2,1,0:T(8,128)S(1)}, u32[]{:S(2)}, u32[]{:S(2)}) collective-permute-start(f32[21,8,128]{2,1,0:T(8,128)S(1)} %get-tuple-element.52), channel_id=1, source_target_pairs={{4,8},{8,4},{12,16},{16,12},{20,24},{24,20},{5,9},{9,5},{13,17},{1... | collective-permute-start | bytes 258056 | tf_op jit(solution)/shard_map/ppermute | solution.py:531
  14.1 0.0 collective-permute-done.2.refs_3_
  14.1 2.9 %collective-permute-done.3.refs_4_ = f32[21,8,128]{2,1,0:T(8,128)S(1)} collective-permute-done((f32[21,8,128]{2,1,0:T(8,128)S(1)}, f32[21,8,128]{2,1,0:T(8,128)S(1)}, u32[]{:S(2)}, u32[]{:S(2)}) %collective-permute-start.3) | collective-permute-done | bytes 86048 | tf_op jit(solution)/shard_map/ppermute | solution.py:531
  17.1 1.1 %shard_map.170 = (f32[13,8,16,128]{3,2,1,0:T(8,128)S(1)}, f32[13,8,16,128]{3,2,1,0:T(8,128)S(1)}, f32[18,8,128]{2,1,0:T(8,128)S(1)}, f32[18,8,128]{2,1,0:T(8,128...) custom-call(f32[13,8,16,128]{3,2,1,0:T(8,128)S(1)} %get-tuple-element.48.refs_0_,, ...), custom_call_target="tpu_custom_call" | custom-call | tf_op jit(solution)/shard_map/pallas_call | solution.py:536
  18.2 1.5 %collective-permute-start.4 = (f32[18,8,128]{2,1,0:T(8,128)S(1)}, f32[18,8,128]{2,1,0:T(8,128)S(1)}, u32[]{:S(2)}, u32[]{:S(2)}) collective-permute-start(f32[18,8,128]{2,1,0:T(8,128)S(1)} %get-tuple-element.56), channel_id=1, source_target_pairs={{0,4},{4,0},{8,12},{12,8},{16,20},{20,16},{24,28},{28,24},{1,5},{5... | collective-permute-start | bytes 221192 | tf_op jit(solution)/shard_map/ppermute | solution.py:531
  19.8 3.5 %collective-permute-start.5 = (f32[18,8,128]{2,1,0:T(8,128)S(1)}, f32[18,8,128]{2,1,0:T(8,128)S(1)}, u32[]{:S(2)}, u32[]{:S(2)}) collective-permute-start(f32[18,8,128]{2,1,0:T(8,128)S(1)} %get-tuple-element.57), channel_id=1, source_target_pairs={{4,8},{8,4},{12,16},{16,12},{20,24},{24,20},{5,9},{9,5},{13,17},{1... | collective-permute-start | bytes 221192 | tf_op jit(solution)/shard_map/ppermute | solution.py:531
  23.2 0.0 collective-permute-done.4.refs_3_
  23.2 3.7 %collective-permute-done.5.refs_4_ = f32[18,8,128]{2,1,0:T(8,128)S(1)} collective-permute-done((f32[18,8,128]{2,1,0:T(8,128)S(1)}, f32[18,8,128]{2,1,0:T(8,128)S(1)}, u32[]{:S(2)}, u32[]{:S(2)}) %collective-permute-start.5) | collective-permute-done | bytes 73760 | tf_op jit(solution)/shard_map/ppermute | solution.py:531
  26.9 1.1 %shard_map.171 = (f32[13,8,16,128]{3,2,1,0:T(8,128)S(1)}, f32[13,8,16,128]{3,2,1,0:T(8,128)S(1)}, f32[18,8,128]{2,1,0:T(8,128)S(1)}, f32[18,8,128]{2,1,0:T(8,128...) custom-call(f32[13,8,16,128]{3,2,1,0:T(8,128)S(1)} %get-tuple-element.54.refs_0_, ...), custom_call_target="tpu_custom_call" | custom-call | tf_op jit(solution)/shard_map/pallas_call | solution.py:536
  28.0 0.6 %collective-permute-start.6 = (f32[18,8,128]{2,1,0:T(8,128)S(1)}, f32[18,8,128]{2,1,0:T(8,128)S(1)}, u32[]{:S(2)}, u32[]{:S(2)}) collective-permute-start(f32[18,8,128]{2,1,0:T(8,128)S(1)} %get-tuple-element.61), channel_id=1, source_target_pairs={{0,4},{4,0},{8,12},{12,8},{16,20},{20,16},{24,28},{28,24},{1,5},{5... | collective-permute-start | bytes 221192 | tf_op jit(solution)/shard_map/ppermute | solution.py:531
  28.6 4.4 %collective-permute-start.7 = (f32[18,8,128]{2,1,0:T(8,128)S(1)}, f32[18,8,128]{2,1,0:T(8,128)S(1)}, u32[]{:S(2)}, u32[]{:S(2)}) collective-permute-start(f32[18,8,128]{2,1,0:T(8,128)S(1)} %get-tuple-element.62), channel_id=1, source_target_pairs={{4,8},{8,4},{12,16},{16,12},{20,24},{24,20},{5,9},{9,5},{13,17},{1... | collective-permute-start | bytes 221192 | tf_op jit(solution)/shard_map/ppermute | solution.py:531
  33.0 0.0 collective-permute-done.6.refs_3_
  33.0 2.7 %collective-permute-done.7.refs_4_ = f32[18,8,128]{2,1,0:T(8,128)S(1)} collective-permute-done((f32[18,8,128]{2,1,0:T(8,128)S(1)}, f32[18,8,128]{2,1,0:T(8,128)S(1)}, u32[]{:S(2)}, u32[]{:S(2)}) %collective-permute-start.7) | collective-permute-done | bytes 73760 | tf_op jit(solution)/shard_map/ppermute | solution.py:531
  35.8 1.2 %shard_map.172 = (f32[13,8,16,128]{3,2,1,0:T(8,128)S(1)}, f32[13,8,16,128]{3,2,1,0:T(8,128)S(1)}, f32[18,8,128]{2,1,0:T(8,128)S(1)}, f32[18,8,128]{2,1,0:T(8,128)S(1)}, f32[9,8,8,128]{3,2,1,0:T(8,128)S(1)}) custom-call(f32[13,8,16,128]{3,2,1,0:T(8,128)S(1)} %get-tuple-element.59.refs_0_, f32[13,8,16,128]{3,2,1,0:T(8,128)S(1)} %get-tuple-element.60.refs_1_, ...), custom_call_target="tpu_custom_call" | custom-call | tf_op jit(solution)/shard_map/pallas_call | solution.py:536
  36.9 2.3 %collective-permute-start.8 = (f32[18,8,128]{2,1,0:T(8,128)S(1)}, f32[18,8,128]{2,1,0:T(8,128)S(1)}, u32[]{:S(2)}, u32[]{:S(2)}) collective-permute-start(f32[18,8,128]{2,1,0:T(8,128)S(1)} %get-tuple-element.67), channel_id=1, source_target_pairs={{0,4},{4,0},{8,12},{12,8},{16,20},{20,16},{24,28},{28,24},{1,5},{5... | collective-permute-start | bytes 221192 | tf_op jit(solution)/shard_map/ppermute | solution.py:531
  39.2 2.9 %collective-permute-start.9 = (f32[18,8,128]{2,1,0:T(8,128)S(1)}, f32[18,8,128]{2,1,0:T(8,128)S(1)}, u32[]{:S(2)}, u32[]{:S(2)}) collective-permute-start(f32[18,8,128]{2,1,0:T(8,128)S(1)} %get-tuple-element.68), channel_id=1, source_target_pairs={{4,8},{8,4},{12,16},{16,12},{20,24},{24,20},{5,9},{9,5},{13,17},{1... | collective-permute-start | bytes 221192 | tf_op jit(solution)/shard_map/ppermute | solution.py:531
  42.1 0.0 collective-permute-done.8.refs_3_
  42.2 4.2 %collective-permute-done.9.refs_4_ = f32[18,8,128]{2,1,0:T(8,128)S(1)} collective-permute-done((f32[18,8,128]{2,1,0:T(8,128)S(1)}, f32[18,8,128]{2,1,0:T(8,128)S(1)}, u32[]{:S(2)}, u32[]{:S(2)}) %collective-permute-start.9) | collective-permute-done | bytes 73760 | tf_op jit(solution)/shard_map/ppermute | solution.py:531
  46.3 1.6 %shard_map.173 = (f32[13,64,128]{2,1,0:T(8,128)}, f32[7,64,128]{2,1,0:T(8,128)}) custom-call(f32[13,8,16,128]{3,2,1,0:T(8,128)S(1)} %get-tuple-element.65.refs_0_, f32[13,8,16,128]{3,2,1,0:T(8,128)S(1)} %get-tuple-element.66.refs_1_, f32[8,8,16,128]{3,2,1,0:T(8,128)S(1)} %get-tuple-element.50.refs_2_, f32[18,8,128]{2,1,0:T(8,128)S(1)} %collective-permute-done.8.refs_3_, ...), custom_call_target="tpu_custom_call" | custom-call | tf_op jit(solution)/shard_map/pallas_call | solution.py:536
Async XLA Ops:
  2.6 3.8 %collective-permute-start = (f32[17,8,128]{2,1,0:T(8,128)S(1)}, f32[17,8,128]{2,1,0:T(8,128)S(1)}, u32[]{:S(2)}, u32[]{:S(2)}) collective-permute-start(f32[17,8,128]{2,1,0:T(8,128)S(1)} %get-tuple-element.41), channel_id=1, source_target_pairs={{0,1},{1,0},{2,3},{3,2},{4,5},{5,4},{6,7},{7,6},{8,9},{9,8},{10,11... | collective-permute-start | bytes 208904 | tf_op jit(solution)/shard_map/ppermute | solution.py:531
  2.7 5.6 %collective-permute-start.1 = (f32[17,8,128]{2,1,0:T(8,128)S(1)}, f32[17,8,128]{2,1,0:T(8,128)S(1)}, u32[]{:S(2)}, u32[]{:S(2)}) collective-permute-start(f32[17,8,128]{2,1,0:T(8,128)S(1)} %get-tuple-element.42), channel_id=1, source_target_pairs={{1,2},{2,1},{5,6},{6,5},{9,10},{10,9},{13,14},{14,13},{17,18},{18,... | collective-permute-start | bytes 208904 | tf_op jit(solution)/shard_map/ppermute | solution.py:531
  9.1 5.0 %collective-permute-start.2 = (f32[21,8,128]{2,1,0:T(8,128)S(1)}, f32[21,8,128]{2,1,0:T(8,128)S(1)}, u32[]{:S(2)}, u32[]{:S(2)}) collective-permute-start(f32[21,8,128]{2,1,0:T(8,128)S(1)} %get-tuple-element.51), channel_id=1, source_target_pairs={{0,4},{4,0},{8,12},{12,8},{16,20},{20,16},{24,28},{28,24},{1,5},{5... | collective-permute-start | bytes 258056 | tf_op jit(solution)/shard_map/ppermute | solution.py:531
  9.7 7.4 %collective-permute-start.3 = (f32[21,8,128]{2,1,0:T(8,128)S(1)}, f32[21,8,128]{2,1,0:T(8,128)S(1)}, u32[]{:S(2)}, u32[]{:S(2)}) collective-permute-start(f32[21,8,128]{2,1,0:T(8,128)S(1)} %get-tuple-element.52), channel_id=1, source_target_pairs={{4,8},{8,4},{12,16},{16,12},{20,24},{24,20},{5,9},{9,5},{13,17},{1... | collective-permute-start | bytes 258056 | tf_op jit(solution)/shard_map/ppermute | solution.py:531
  18.2 5.0 %collective-permute-start.4 = (f32[18,8,128]{2,1,0:T(8,128)S(1)}, f32[18,8,128]{2,1,0:T(8,128)S(1)}, u32[]{:S(2)}, u32[]{:S(2)}) collective-permute-start(f32[18,8,128]{2,1,0:T(8,128)S(1)} %get-tuple-element.56), channel_id=1, source_target_pairs={{0,4},{4,0},{8,12},{12,8},{16,20},{20,16},{24,28},{28,24},{1,5},{5... | collective-permute-start | bytes 221192 | tf_op jit(solution)/shard_map/ppermute | solution.py:531
  19.8 7.1 %collective-permute-start.5 = (f32[18,8,128]{2,1,0:T(8,128)S(1)}, f32[18,8,128]{2,1,0:T(8,128)S(1)}, u32[]{:S(2)}, u32[]{:S(2)}) collective-permute-start(f32[18,8,128]{2,1,0:T(8,128)S(1)} %get-tuple-element.57), channel_id=1, source_target_pairs={{4,8},{8,4},{12,16},{16,12},{20,24},{24,20},{5,9},{9,5},{13,17},{1... | collective-permute-start | bytes 221192 | tf_op jit(solution)/shard_map/ppermute | solution.py:531
  28.0 5.0 %collective-permute-start.6 = (f32[18,8,128]{2,1,0:T(8,128)S(1)}, f32[18,8,128]{2,1,0:T(8,128)S(1)}, u32[]{:S(2)}, u32[]{:S(2)}) collective-permute-start(f32[18,8,128]{2,1,0:T(8,128)S(1)} %get-tuple-element.61), channel_id=1, source_target_pairs={{0,4},{4,0},{8,12},{12,8},{16,20},{20,16},{24,28},{28,24},{1,5},{5... | collective-permute-start | bytes 221192 | tf_op jit(solution)/shard_map/ppermute | solution.py:531
  28.6 7.1 %collective-permute-start.7 = (f32[18,8,128]{2,1,0:T(8,128)S(1)}, f32[18,8,128]{2,1,0:T(8,128)S(1)}, u32[]{:S(2)}, u32[]{:S(2)}) collective-permute-start(f32[18,8,128]{2,1,0:T(8,128)S(1)} %get-tuple-element.62), channel_id=1, source_target_pairs={{4,8},{8,4},{12,16},{16,12},{20,24},{24,20},{5,9},{9,5},{13,17},{1... | collective-permute-start | bytes 221192 | tf_op jit(solution)/shard_map/ppermute | solution.py:531
  36.9 5.2 %collective-permute-start.8 = (f32[18,8,128]{2,1,0:T(8,128)S(1)}, f32[18,8,128]{2,1,0:T(8,128)S(1)}, u32[]{:S(2)}, u32[]{:S(2)}) collective-permute-start(f32[18,8,128]{2,1,0:T(8,128)S(1)} %get-tuple-element.67), channel_id=1, source_target_pairs={{0,4},{4,0},{8,12},{12,8},{16,20},{20,16},{24,28},{28,24},{1,5},{5... | collective-permute-start | bytes 221192 | tf_op jit(solution)/shard_map/ppermute | solution.py:531
  39.2 7.1 %collective-permute-start.9 = (f32[18,8,128]{2,1,0:T(8,128)S(1)}, f32[18,8,128]{2,1,0:T(8,128)S(1)}, u32[]{:S(2)}, u32[]{:S(2)}) collective-permute-start(f32[18,8,128]{2,1,0:T(8,128)S(1)} %get-tuple-element.68), channel_id=1, source_target_pairs={{4,8},{8,4},{12,16},{16,12},{20,24},{24,20},{5,9},{9,5},{13,17},{1... | collective-permute-start | bytes 221192 | tf_op jit(solution)/shard_map/ppermute | solution.py:531

commit v2 on v1

--- a/solution.py
+++ b/solution.py
@@ -164,10 +164,13 @@
         b_ref[n] = jnp.where(even, up, down)
 
 
-def receive(tile, even, a_ref, b_ref, count):
+def receive(tile, axis, a_ref, b_ref, count):
     total = a_ref.shape[0]
-    first = [jnp.where(even, b_ref[n], a_ref[n]) for n in range(total)]
-    last = [jnp.where(even, a_ref[n], b_ref[n]) for n in range(total)]
+    at = lax.axis_index(axis)
+    even = lax.rem(at, 2) == 0
+    before, after = at > 0, at < lax.axis_size(axis) - 1
+    first = [jnp.where(before, jnp.where(even, b_ref[n], a_ref[n]), 0.0) for n in range(total)]
+    last = [jnp.where(after, jnp.where(even, a_ref[n], b_ref[n]), 0.0) for n in range(total)]
     sides = []
     for got in (first, last):
         sides.append([W(got[n], tile.unpack(got[count:], n)) for n in range(count)])
@@ -274,7 +277,9 @@
     packs = ay_ref.shape[0]
     right = [jnp.where(even_y, ay_ref[n], by_ref[n]) for n in range(packs)]
     left = [jnp.where(even_y, by_ref[n], ay_ref[n]) for n in range(packs)]
-    on_right, on_left = tile.lane < halo, tile.lane >= columns - halo
+    at_y = lax.axis_index(gy_axis)
+    on_right = (tile.lane < halo) & (at_y < lax.axis_size(gy_axis) - 1)
+    on_left = (tile.lane >= columns - halo) & (at_y > 0)
 
     def side(n):
         g = n % per
@@ -346,7 +351,7 @@
     even = lax.rem(lax.axis_index(gx_axis), 2) == 0
     rows, planes, columns = f_ref.shape[1], f_ref.shape[2] // 2, f_ref.shape[3]
     tile = Tile(planes, columns, halo)
-    sides = receive(tile, even, am_ref, bm_ref, 2 * EDGE + (2 if first else 0))
+    sides = receive(tile, gx_axis, am_ref, bm_ref, 2 * EDGE + (2 if first else 0))
     p = lambda f, r: read(p_ref, f, r)
     old = lambda f, r: read(f_ref, f, r)
     lam = lambda f, r: read(a_ref, f, r)
@@ -519,16 +524,26 @@
         messages(tile, even, f_out, a_out, p_ref, a_msg, b_msg, False)
 
 
-def pairs(count, odd):
-    out = []
+def swaps(axis, odd):
+    nx, ny = lax.axis_size("gx"), lax.axis_size("gy")
+    count, other = (nx, ny) if axis == "gx" else (ny, nx)
+    place = (lambda i, k: i * ny + k) if axis == "gx" else (lambda i, k: k * ny + i)
+    out, met = [], set()
     for i in range(odd, count - 1, 2):
-        out += [(i, i + 1), (i + 1, i)]
-    return out
+        met |= {i, i + 1}
+        for k in range(other):
+            out += [(place(i, k), place(i + 1, k)), (place(i + 1, k), place(i, k))]
+    for i in set(range(count)) - met:
+        for k in range(0, other - 1, 2):
+            out += [(place(i, k), place(i, k + 1)), (place(i, k + 1), place(i, k))]
+    return sorted(out)
 
 
 def exchange(axis, a, b):
-    count = lax.axis_size(axis)
-    return lax.ppermute(a, axis, pairs(count, 0)), lax.ppermute(b, axis, pairs(count, 1))
+    mesh = ("gx", "gy")
+    b = lax.ppermute(b, mesh, swaps(axis, 1))
+    a = lax.ppermute(a, mesh, swaps(axis, 0))
+    return a, b
 
 
 def call(kernel, outs, *args):

time: 48.2 us -> 39.1 us (0.81)
  the two profiles are of different devices: /device:TPU:14 before, /device:TPU:16 now
where the time goes in v2:
time: 39.1 us; the launch traced here: 38.9 us
  waiting for transfers between devices  19.7 us (50%)
  starting transfers between devices  9.53 us (24%)
  Pallas kernels  9.01 us (23%)
  between operations  0.69 us (2%)
    ppermute x5, waiting for transfers between devices, exchange(): a = lax.ppermute(a, mesh, swaps(axis, 0))  10.9 us
    ppermute x5, waiting for transfers between devices, exchange(): b = lax.ppermute(b, mesh, swaps(axis, 1))  8.86 us
    pallas_call x6, Pallas kernels, call(): pl.pallas_call(kernel, out_shape=shapes, in_specs=[pl.BlockSpec(memory_sp...  7.06 us
    ppermute x5, starting transfers between devices, exchange(): a = lax.ppermute(a, mesh, swaps(axis, 0))  4.91 us
    ppermute x5, starting transfers between devices, exchange(): b = lax.ppermute(b, mesh, swaps(axis, 1))  4.63 us
    pallas_call x1, Pallas kernels, per_device(): pl.pallas_call(start, out_shape=[jax.ShapeDtypeStruct(s, jnp.float32) for...  1.95 us
  transfers between devices with their start and end apart: 10, of which 9 were waited for; matrix products, arithmetic and copies ran while one was open for 0% of the time, Pallas kernels for 3%

profile of v2, /device:TPU:16, one launch (start us, length us, event | category | flops | bytes accessed | tf_op | source)
XLA Modules:
  0.0 38.9 jit_solution(15367044522011864950)
XLA Ops:
  0.6 1.9 %shard_map.167 = (f32[8,8,8,128]{3,2,1,0:T(8,128)S(1)}, f32[17,8,128]{2,1,0:T(8,128)S(1)}, f32[17,8,128]{2,1,0:T(8,128)S(1)}, f32[13,64,128]{2,1,0:T(8,128)S(1)}...) custom-call(f32[1,64,128]{2,1,0:T(8,128)} %bitcast.18, ...), custom_call_target="tpu_custom_call" | custom-call | tf_op jit(solution)/shard_map/pallas_call | solution.py:586
  2.6 0.1 collective-permute-start
  2.7 1.6 %collective-permute-start.1 = (f32[17,8,128]{2,1,0:T(8,128)S(1)}, f32[17,8,128]{2,1,0:T(8,128)S(1)}, u32[]{:S(2)}, u32[]{:S(2)}) collective-permute-start(f32[17,8,128]{2,1,0:T(8,128)S(1)} %get-tuple-element.42), channel_id=1, source_target_pairs={{0,4},{1,2},{2,1},{3,7},{4,0},{5,6},{6,5},{7,3},{8,12},{9,10},{10,... | collective-permute-start | bytes 208904 | tf_op jit(solution)/shard_map/ppermute | solution.py:544
  4.2 1.2 %shard_map.168 = (f32[4,8,16,128]{3,2,1,0:T(8,128)S(1)}, f32[4,8,16,128]{3,2,1,0:T(8,128)S(1)}) custom-call(s32[1,512]{1,0:T(1,128)S(1)} %get-tuple-element.43.rec_ref, f32[4,512]{1,0:T(4,128)S(1)} %get-tuple-element.44.cot_ref, s32[1,64]{1,0:T(1,128)S(1)} %get-tuple-element.45.src_ref, f32[4,64]{1,0:T(4,128)S(1)} %get-tuple-element.46.amp_ref), custom_call_target="tpu_custom_call" | custom-call | tf_op jit(solution)/shard_map/pallas_call | solution.py:551
  5.4 0.0 collective-permute-done.ay_ref
  5.4 1.6 %collective-permute-done.1.by_ref = f32[17,8,128]{2,1,0:T(8,128)S(1)} collective-permute-done((f32[17,8,128]{2,1,0:T(8,128)S(1)}, f32[17,8,128]{2,1,0:T(8,128)S(1)}, u32[]{:S(2)}, u32[]{:S(2)}) %collective-permute-start.1) | collective-permute-done | bytes 69664 | tf_op jit(solution)/shard_map/ppermute | solution.py:544
  7.0 0.8 %shard_map.169 = (f32[13,8,16,128]{3,2,1,0:T(8,128)S(1)}, f32[13,8,16,128]{3,2,1,0:T(8,128)S(1)}, f32[8,8,16,128]{3,2,1,0:T(8,128)S(1)}, f32[21,8,128]{2,1,0:T(8,128)S(1)}, f32[21,8,128]{2,1,0:T(8,128)S(1)}) custom-call(f32[13,64,128]{2,1,0:T(8,128)S(1)} %get-tuple-element.38.fields_ref, f32[13,64,128]{2,1,0:T(8,128)S(1)} %get-tuple-element.39.cot_ref, ...), custom_call_target="tpu_custom_call" | custom-call | tf_op jit(solution)/shard_map/pallas_call | solution.py:551
  7.9 1.6 %collective-permute-start.2 = (f32[21,8,128]{2,1,0:T(8,128)S(1)}, f32[21,8,128]{2,1,0:T(8,128)S(1)}, u32[]{:S(2)}, u32[]{:S(2)}) collective-permute-start(f32[21,8,128]{2,1,0:T(8,128)S(1)} %get-tuple-element.51), channel_id=1, source_target_pairs={{0,4},{1,5},{2,6},{3,7},{4,0},{5,1},{6,2},{7,3},{8,12},{9,13},{10,... | collective-permute-start | bytes 258056 | tf_op jit(solution)/shard_map/ppermute | solution.py:545
  9.4 0.4 %collective-permute-start.3 = (f32[21,8,128]{2,1,0:T(8,128)S(1)}, f32[21,8,128]{2,1,0:T(8,128)S(1)}, u32[]{:S(2)}, u32[]{:S(2)}) collective-permute-start(f32[21,8,128]{2,1,0:T(8,128)S(1)} %get-tuple-element.52), channel_id=1, source_target_pairs={{0,1},{1,0},{2,3},{3,2},{4,8},{5,9},{6,10},{7,11},{8,4},{9,5},{10,... | collective-permute-start | bytes 258056 | tf_op jit(solution)/shard_map/ppermute | solution.py:544
  9.8 3.5 %collective-permute-done.2.refs_3_ = f32[21,8,128]{2,1,0:T(8,128)S(1)} collective-permute-done((f32[21,8,128]{2,1,0:T(8,128)S(1)}, f32[21,8,128]{2,1,0:T(8,128)S(1)}, u32[]{:S(2)}, u32[]{:S(2)}) %collective-permute-start.2) | collective-permute-done | bytes 86048 | tf_op jit(solution)/shard_map/ppermute | solution.py:545
  13.4 1.4 %collective-permute-done.3.refs_4_ = f32[21,8,128]{2,1,0:T(8,128)S(1)} collective-permute-done((f32[21,8,128]{2,1,0:T(8,128)S(1)}, f32[21,8,128]{2,1,0:T(8,128)S(1)}, u32[]{:S(2)}, u32[]{:S(2)}) %collective-permute-start.3) | collective-permute-done | bytes 86048 | tf_op jit(solution)/shard_map/ppermute | solution.py:544
  14.8 1.1 %shard_map.170 = (f32[13,8,16,128]{3,2,1,0:T(8,128)S(1)}, f32[13,8,16,128]{3,2,1,0:T(8,128)S(1)}, f32[18,8,128]{2,1,0:T(8,128)S(1)}, f32[18,8,128]{2,1,0:T(8,128...) custom-call(f32[13,8,16,128]{3,2,1,0:T(8,128)S(1)} %get-tuple-element.48.refs_0_,, ...), custom_call_target="tpu_custom_call" | custom-call | tf_op jit(solution)/shard_map/pallas_call | solution.py:551
  15.9 1.1 %collective-permute-start.4 = (f32[18,8,128]{2,1,0:T(8,128)S(1)}, f32[18,8,128]{2,1,0:T(8,128)S(1)}, u32[]{:S(2)}, u32[]{:S(2)}) collective-permute-start(f32[18,8,128]{2,1,0:T(8,128)S(1)} %get-tuple-element.56), channel_id=1, source_target_pairs={{0,4},{1,5},{2,6},{3,7},{4,0},{5,1},{6,2},{7,3},{8,12},{9,13},{10,... | collective-permute-start | bytes 221192 | tf_op jit(solution)/shard_map/ppermute | solution.py:545
  17.0 0.9 %collective-permute-start.5 = (f32[18,8,128]{2,1,0:T(8,128)S(1)}, f32[18,8,128]{2,1,0:T(8,128)S(1)}, u32[]{:S(2)}, u32[]{:S(2)}) collective-permute-start(f32[18,8,128]{2,1,0:T(8,128)S(1)} %get-tuple-element.57), channel_id=1, source_target_pairs={{0,1},{1,0},{2,3},{3,2},{4,8},{5,9},{6,10},{7,11},{8,4},{9,5},{10,... | collective-permute-start | bytes 221192 | tf_op jit(solution)/shard_map/ppermute | solution.py:544
  17.9 2.4 %collective-permute-done.4.refs_3_ = f32[18,8,128]{2,1,0:T(8,128)S(1)} collective-permute-done((f32[18,8,128]{2,1,0:T(8,128)S(1)}, f32[18,8,128]{2,1,0:T(8,128)S(1)}, u32[]{:S(2)}, u32[]{:S(2)}) %collective-permute-start.4) | collective-permute-done | bytes 73760 | tf_op jit(solution)/shard_map/ppermute | solution.py:545
  20.4 1.9 %collective-permute-done.5.refs_4_ = f32[18,8,128]{2,1,0:T(8,128)S(1)} collective-permute-done((f32[18,8,128]{2,1,0:T(8,128)S(1)}, f32[18,8,128]{2,1,0:T(8,128)S(1)}, u32[]{:S(2)}, u32[]{:S(2)}) %collective-permute-start.5) | collective-permute-done | bytes 73760 | tf_op jit(solution)/shard_map/ppermute | solution.py:544
  22.3 1.1 %shard_map.171 = (f32[13,8,16,128]{3,2,1,0:T(8,128)S(1)}, f32[13,8,16,128]{3,2,1,0:T(8,128)S(1)}, f32[18,8,128]{2,1,0:T(8,128)S(1)}, f32[18,8,128]{2,1,0:T(8,128...) custom-call(f32[13,8,16,128]{3,2,1,0:T(8,128)S(1)} %get-tuple-element.54.refs_0_, ...), custom_call_target="tpu_custom_call" | custom-call | tf_op jit(solution)/shard_map/pallas_call | solution.py:551
  23.4 1.1 %collective-permute-start.6 = (f32[18,8,128]{2,1,0:T(8,128)S(1)}, f32[18,8,128]{2,1,0:T(8,128)S(1)}, u32[]{:S(2)}, u32[]{:S(2)}) collective-permute-start(f32[18,8,128]{2,1,0:T(8,128)S(1)} %get-tuple-element.61), channel_id=1, source_target_pairs={{0,4},{1,5},{2,6},{3,7},{4,0},{5,1},{6,2},{7,3},{8,12},{9,13},{10,... | collective-permute-start | bytes 221192 | tf_op jit(solution)/shard_map/ppermute | solution.py:545
  24.5 0.9 %collective-permute-start.7 = (f32[18,8,128]{2,1,0:T(8,128)S(1)}, f32[18,8,128]{2,1,0:T(8,128)S(1)}, u32[]{:S(2)}, u32[]{:S(2)}) collective-permute-start(f32[18,8,128]{2,1,0:T(8,128)S(1)} %get-tuple-element.62), channel_id=1, source_target_pairs={{0,1},{1,0},{2,3},{3,2},{4,8},{5,9},{6,10},{7,11},{8,4},{9,5},{10,... | collective-permute-start | bytes 221192 | tf_op jit(solution)/shard_map/ppermute | solution.py:544
  25.4 2.4 %collective-permute-done.6.refs_3_ = f32[18,8,128]{2,1,0:T(8,128)S(1)} collective-permute-done((f32[18,8,128]{2,1,0:T(8,128)S(1)}, f32[18,8,128]{2,1,0:T(8,128)S(1)}, u32[]{:S(2)}, u32[]{:S(2)}) %collective-permute-start.6) | collective-permute-done | bytes 73760 | tf_op jit(solution)/shard_map/ppermute | solution.py:545
  27.8 1.9 %collective-permute-done.7.refs_4_ = f32[18,8,128]{2,1,0:T(8,128)S(1)} collective-permute-done((f32[18,8,128]{2,1,0:T(8,128)S(1)}, f32[18,8,128]{2,1,0:T(8,128)S(1)}, u32[]{:S(2)}, u32[]{:S(2)}) %collective-permute-start.7) | collective-permute-done | bytes 73760 | tf_op jit(solution)/shard_map/ppermute | solution.py:544
  29.8 1.2 %shard_map.172 = (f32[13,8,16,128]{3,2,1,0:T(8,128)S(1)}, f32[13,8,16,128]{3,2,1,0:T(8,128)S(1)}, f32[18,8,128]{2,1,0:T(8,128)S(1)}, f32[18,8,128]{2,1,0:T(8,128)S(1)}, f32[9,8,8,128]{3,2,1,0:T(8,128)S(1)}) custom-call(f32[13,8,16,128]{3,2,1,0:T(8,128)S(1)} %get-tuple-element.59.refs_0_, f32[13,8,16,128]{3,2,1,0:T(8,128)S(1)} %get-tuple-element.60.refs_1_, ...), custom_call_target="tpu_custom_call" | custom-call | tf_op jit(solution)/shard_map/pallas_call | solution.py:551
  30.9 1.1 %collective-permute-start.8 = (f32[18,8,128]{2,1,0:T(8,128)S(1)}, f32[18,8,128]{2,1,0:T(8,128)S(1)}, u32[]{:S(2)}, u32[]{:S(2)}) collective-permute-start(f32[18,8,128]{2,1,0:T(8,128)S(1)} %get-tuple-element.67), channel_id=1, source_target_pairs={{0,4},{1,5},{2,6},{3,7},{4,0},{5,1},{6,2},{7,3},{8,12},{9,13},{10,... | collective-permute-start | bytes 221192 | tf_op jit(solution)/shard_map/ppermute | solution.py:545
  32.0 0.9 %collective-permute-start.9 = (f32[18,8,128]{2,1,0:T(8,128)S(1)}, f32[18,8,128]{2,1,0:T(8,128)S(1)}, u32[]{:S(2)}, u32[]{:S(2)}) collective-permute-start(f32[18,8,128]{2,1,0:T(8,128)S(1)} %get-tuple-element.68), channel_id=1, source_target_pairs={{0,1},{1,0},{2,3},{3,2},{4,8},{5,9},{6,10},{7,11},{8,4},{9,5},{10,... | collective-permute-start | bytes 221192 | tf_op jit(solution)/shard_map/ppermute | solution.py:544
  32.9 2.4 %collective-permute-done.8.refs_3_ = f32[18,8,128]{2,1,0:T(8,128)S(1)} collective-permute-done((f32[18,8,128]{2,1,0:T(8,128)S(1)}, f32[18,8,128]{2,1,0:T(8,128)S(1)}, u32[]{:S(2)}, u32[]{:S(2)}) %collective-permute-start.8) | collective-permute-done | bytes 73760 | tf_op jit(solution)/shard_map/ppermute | solution.py:545
  35.3 2.0 %collective-permute-done.9.refs_4_ = f32[18,8,128]{2,1,0:T(8,128)S(1)} collective-permute-done((f32[18,8,128]{2,1,0:T(8,128)S(1)}, f32[18,8,128]{2,1,0:T(8,128)S(1)}, u32[]{:S(2)}, u32[]{:S(2)}) %collective-permute-start.9) | collective-permute-done | bytes 73760 | tf_op jit(solution)/shard_map/ppermute | solution.py:544
  37.3 1.7 %shard_map.173 = (f32[13,64,128]{2,1,0:T(8,128)}, f32[7,64,128]{2,1,0:T(8,128)}) custom-call(f32[13,8,16,128]{3,2,1,0:T(8,128)S(1)} %get-tuple-element.65.refs_0_, f32[13,8,16,128]{3,2,1,0:T(8,128)S(1)} %get-tuple-element.66.refs_1_, f32[8,8,16,128]{3,2,1,0:T(8,128)S(1)} %get-tuple-element.50.refs_2_, f32[18,8,128]{2,1,0:T(8,128)S(1)} %collective-permute-done.8.refs_3_, ...), custom_call_target="tpu_custom_call" | custom-call | tf_op jit(solution)/shard_map/pallas_call | solution.py:551
Async XLA Ops:
  2.6 2.8 %collective-permute-start = (f32[17,8,128]{2,1,0:T(8,128)S(1)}, f32[17,8,128]{2,1,0:T(8,128)S(1)}, u32[]{:S(2)}, u32[]{:S(2)}) collective-permute-start(f32[17,8,128]{2,1,0:T(8,128)S(1)} %get-tuple-element.41), channel_id=1, source_target_pairs={{0,1},{1,0},{2,3},{3,2},{4,5},{5,4},{6,7},{7,6},{8,9},{9,8},{10,11... | collective-permute-start | bytes 208904 | tf_op jit(solution)/shard_map/ppermute | solution.py:545
  2.7 4.4 %collective-permute-start.1 = (f32[17,8,128]{2,1,0:T(8,128)S(1)}, f32[17,8,128]{2,1,0:T(8,128)S(1)}, u32[]{:S(2)}, u32[]{:S(2)}) collective-permute-start(f32[17,8,128]{2,1,0:T(8,128)S(1)} %get-tuple-element.42), channel_id=1, source_target_pairs={{0,4},{1,2},{2,1},{3,7},{4,0},{5,6},{6,5},{7,3},{8,12},{9,10},{10,... | collective-permute-start | bytes 208904 | tf_op jit(solution)/shard_map/ppermute | solution.py:544
  7.9 5.5 %collective-permute-start.2 = (f32[21,8,128]{2,1,0:T(8,128)S(1)}, f32[21,8,128]{2,1,0:T(8,128)S(1)}, u32[]{:S(2)}, u32[]{:S(2)}) collective-permute-start(f32[21,8,128]{2,1,0:T(8,128)S(1)} %get-tuple-element.51), channel_id=1, source_target_pairs={{0,4},{1,5},{2,6},{3,7},{4,0},{5,1},{6,2},{7,3},{8,12},{9,13},{10,... | collective-permute-start | bytes 258056 | tf_op jit(solution)/shard_map/ppermute | solution.py:545
  9.4 5.4 %collective-permute-start.3 = (f32[21,8,128]{2,1,0:T(8,128)S(1)}, f32[21,8,128]{2,1,0:T(8,128)S(1)}, u32[]{:S(2)}, u32[]{:S(2)}) collective-permute-start(f32[21,8,128]{2,1,0:T(8,128)S(1)} %get-tuple-element.52), channel_id=1, source_target_pairs={{0,1},{1,0},{2,3},{3,2},{4,8},{5,9},{6,10},{7,11},{8,4},{9,5},{10,... | collective-permute-start | bytes 258056 | tf_op jit(solution)/shard_map/ppermute | solution.py:544
  15.9 4.4 %collective-permute-start.4 = (f32[18,8,128]{2,1,0:T(8,128)S(1)}, f32[18,8,128]{2,1,0:T(8,128)S(1)}, u32[]{:S(2)}, u32[]{:S(2)}) collective-permute-start(f32[18,8,128]{2,1,0:T(8,128)S(1)} %get-tuple-element.56), channel_id=1, source_target_pairs={{0,4},{1,5},{2,6},{3,7},{4,0},{5,1},{6,2},{7,3},{8,12},{9,13},{10,... | collective-permute-start | bytes 221192 | tf_op jit(solution)/shard_map/ppermute | solution.py:545
  17.0 5.3 %collective-permute-start.5 = (f32[18,8,128]{2,1,0:T(8,128)S(1)}, f32[18,8,128]{2,1,0:T(8,128)S(1)}, u32[]{:S(2)}, u32[]{:S(2)}) collective-permute-start(f32[18,8,128]{2,1,0:T(8,128)S(1)} %get-tuple-element.57), channel_id=1, source_target_pairs={{0,1},{1,0},{2,3},{3,2},{4,8},{5,9},{6,10},{7,11},{8,4},{9,5},{10,... | collective-permute-start | bytes 221192 | tf_op jit(solution)/shard_map/ppermute | solution.py:544
  23.4 4.4 %collective-permute-start.6 = (f32[18,8,128]{2,1,0:T(8,128)S(1)}, f32[18,8,128]{2,1,0:T(8,128)S(1)}, u32[]{:S(2)}, u32[]{:S(2)}) collective-permute-start(f32[18,8,128]{2,1,0:T(8,128)S(1)} %get-tuple-element.61), channel_id=1, source_target_pairs={{0,4},{1,5},{2,6},{3,7},{4,0},{5,1},{6,2},{7,3},{8,12},{9,13},{10,... | collective-permute-start | bytes 221192 | tf_op jit(solution)/shard_map/ppermute | solution.py:545
  24.5 5.3 %collective-permute-start.7 = (f32[18,8,128]{2,1,0:T(8,128)S(1)}, f32[18,8,128]{2,1,0:T(8,128)S(1)}, u32[]{:S(2)}, u32[]{:S(2)}) collective-permute-start(f32[18,8,128]{2,1,0:T(8,128)S(1)} %get-tuple-element.62), channel_id=1, source_target_pairs={{0,1},{1,0},{2,3},{3,2},{4,8},{5,9},{6,10},{7,11},{8,4},{9,5},{10,... | collective-permute-start | bytes 221192 | tf_op jit(solution)/shard_map/ppermute | solution.py:544
  30.9 4.4 %collective-permute-start.8 = (f32[18,8,128]{2,1,0:T(8,128)S(1)}, f32[18,8,128]{2,1,0:T(8,128)S(1)}, u32[]{:S(2)}, u32[]{:S(2)}) collective-permute-start(f32[18,8,128]{2,1,0:T(8,128)S(1)} %get-tuple-element.67), channel_id=1, source_target_pairs={{0,4},{1,5},{2,6},{3,7},{4,0},{5,1},{6,2},{7,3},{8,12},{9,13},{10,... | collective-permute-start | bytes 221192 | tf_op jit(solution)/shard_map/ppermute | solution.py:545
  32.0 5.3 %collective-permute-start.9 = (f32[18,8,128]{2,1,0:T(8,128)S(1)}, f32[18,8,128]{2,1,0:T(8,128)S(1)}, u32[]{:S(2)}, u32[]{:S(2)}) collective-permute-start(f32[18,8,128]{2,1,0:T(8,128)S(1)} %get-tuple-element.68), channel_id=1, source_target_pairs={{0,1},{1,0},{2,3},{3,2},{4,8},{5,9},{6,10},{7,11},{8,4},{9,5},{10,... | collective-permute-start | bytes 221192 | tf_op jit(solution)/shard_map/ppermute | solution.py:544

commit v3 on v2

--- a/solution.py
+++ b/solution.py
@@ -267,110 +267,141 @@
                     out[t, r, pl.ds(half * planes, planes)] = got[base : base + planes]
 
 
-def spread_kernel(halo, gx_axis, gy_axis, fields_ref, cot_ref, pm_ref, ay_ref, by_ref, rec_ref,
-                  f_out, a_out, p_out, a_msg, b_msg):
-    even_x = lax.rem(lax.axis_index(gx_axis), 2) == 0
-    even_y = lax.rem(lax.axis_index(gy_axis), 2) == 0
+def spreader(halo, gy_axis, ay_ref, by_ref, rows, tile):
+    at_y = lax.axis_index(gy_axis)
+    even_y = lax.rem(at_y, 2) == 0
+    columns = tile.columns
+    per = columns // halo
+    on_right = (tile.lane < halo) & (at_y < lax.axis_size(gy_axis) - 1)
+    on_left = (tile.lane >= columns - halo) & (at_y > 0)
+
+    @memo
+    def packs(n):
+        a, b = ay_ref[n], by_ref[n]
+        return jnp.where(even_y, a, b), jnp.where(even_y, b, a)
+
+    def side(f, r):
+        n = f * rows + r
+        g = n % per
+        right, left = packs(n // per)
+        a, b = roll(right, -halo * g, 1), roll(left, -halo * (g + 1), 1)
+        return jnp.where(on_right, a, jnp.where(on_left, b, 0.0))
+
+    return side
+
+
+def spread_forward(halo, gx_axis, gy_axis, fields_ref, pm_ref, ay_ref, by_ref, rec_ref, f_out, p_out, a_msg, b_msg):
+    even = lax.rem(lax.axis_index(gx_axis), 2) == 0
     rows, planes, columns = pm_ref.shape[1:]
     tile = Tile(planes, columns, halo)
-    per = columns // halo
-    packs = ay_ref.shape[0]
-    right = [jnp.where(even_y, ay_ref[n], by_ref[n]) for n in range(packs)]
-    left = [jnp.where(even_y, by_ref[n], ay_ref[n]) for n in range(packs)]
-    at_y = lax.axis_index(gy_axis)
-    on_right = (tile.lane < halo) & (at_y < lax.axis_size(gy_axis) - 1)
-    on_left = (tile.lane >= columns - halo) & (at_y > 0)
-
-    def side(n):
-        g = n % per
-        a = roll(right[n // per], -halo * g, 1)
-        b = roll(left[n // per], columns - halo - halo * g, 1)
-        return jnp.where(on_right, a, jnp.where(on_left, b, 0.0))
-
-    def at(r):
-        return pl.ds(r, planes, stride=rows)
-
-    count, base = fields_ref.shape[0], p_out.shape[0]
-    for f in range(p_out.shape[0]):
+    side = spreader(halo, gy_axis, ay_ref, by_ref, rows, tile)
+    base = p_out.shape[0]
+    for f in range(base):
         for r in range(rows):
-            write(p_out, W(pm_ref[f, r], side(f * rows + r)), f, r)
+            write(p_out, W(pm_ref[f, r], side(f, r)), f, r)
+    for f in range(fields_ref.shape[0]):
+        for r in range(rows):
+            write(f_out, W(fields_ref[f, pl.ds(r, planes, stride=rows), :], side(base + f, r)), f, r)
+    forward_messages(tile, even, f_out, p_out, a_msg, b_msg, True)
+
+
+def spread_adjoint(halo, gx_axis, gy_axis, cot_ref, p_ref, ay_ref, by_ref, rec_ref, a_out, a_msg, b_msg):
+    even = lax.rem(lax.axis_index(gx_axis), 2) == 0
+    rows, planes, columns = p_ref.shape[1], p_ref.shape[2] // 2, p_ref.shape[3]
+    tile = Tile(planes, columns, halo)
+    side = spreader(halo, gy_axis, ay_ref, by_ref, rows, tile)
+    count = cot_ref.shape[0]
     for f in range(count):
         for r in range(rows):
-            write(f_out, W(fields_ref[f, at(r), :], side((base + f) * rows + r)), f, r)
-            value = W(cot_ref[f, at(r), :], side((base + count + f) * rows + r))
+            value = W(cot_ref[f, pl.ds(r, planes, stride=rows), :], side(p_ref.shape[0] + count + f, r))
             if f == PP:
                 value = value + read(rec_ref, rec_ref.shape[0] - 1, r)
-            write(a_out, value * read(p_out, PF, r), f, r)
-    messages(tile, even_x, f_out, a_out, p_out, a_msg, b_msg, True)
-
-
-def messages(tile, even, f_ref, a_ref, p_ref, a_msg, b_msg, with_params):
+            write(a_out, value * read(p_ref, PF, r), f, r)
+    adjoint_messages(tile, even, a_out, p_ref, a_msg, b_msg)
+
+
+def forward_messages(tile, even, f_ref, p_ref, a_msg, b_msg, with_params):
     rows = f_ref.shape[1]
     s = lambda f, r: read(f_ref, f, r)
+    p = lambda f, r: read(p_ref, f, r)
+    sides = []
+    for r, low, high in ((0, False, True), (rows - 1, True, False)):
+        got = forward_edge(tile, s, s, p, r, low, high)
+        sides.append(got + [p(PH, r), p(PK, r)] if with_params else got)
+    send(tile, even, *sides, a_msg, b_msg)
+
+
+def adjoint_messages(tile, even, a_ref, p_ref, a_msg, b_msg):
+    rows = a_ref.shape[1]
     a = lambda f, r: read(a_ref, f, r)
     p = lambda f, r: read(p_ref, f, r)
     qs = memo(lambda r: adjoint_stress(p, a, r))
     q = lambda f, r: qs(r)[f]
-    sides = []
-    for r, low, high in ((0, False, True), (rows - 1, True, False)):
-        got = forward_edge(tile, s, s, p, r, low, high) + adjoint_edge(tile, q, a, p, r, low, high)
-        if with_params:
-            got += [p(PH, r), p(PK, r)]
-        sides.append(got)
-    send(tile, even, *sides, a_msg, b_msg)
-
-
-def step_kernel(gx_axis, halo, j, steps, *refs):
+    send(tile, even, *[
+        adjoint_edge(tile, q, a, p, r, low, high) for r, low, high in ((0, False, True), (rows - 1, True, False))
+    ], a_msg, b_msg)
+
+
+SLOT = {XX: 0, XY: 1, XZ: 2, PP: 3}
+
+
+def end(r):
+    return 0 if r < 0 else 1
+
+
+def sums(ff, aa):
+    fo, pu, wo, ee, gg, w_ = ff[0:3], ff[3:6], ff[6:9], ff[9:12], ff[12:15], ff[15]
+    af, ag, sg, pi = aa[0:3], aa[3:6], aa[6:12], aa[12]
+    tr, dd = sg[0] + sg[1] + sg[2], ee[0] + ee[1] + ee[2]
+    dot = lambda x, y: x[0] * y[0] + x[1] * y[1] + x[2] * y[2]
+    return [
+        dot(af, fo), dot(ag, pu), dot(af, pu), dot(ag, wo),
+        tr * dd, tr * w_, 2.0 * dot(sg[0:3], ee) + dot(sg[3:6], gg), pi * dd, pi * w_,
+    ]
+
+
+def sums_kernel(*refs):
+    out, pairs = refs[-1], refs[:-1]
+    for r in range(out.shape[1]):
+        acc = [0.0] * 9
+        for n in range(0, len(pairs), 2):
+            adds = sums([pairs[n][m, r] for m in range(16)], [pairs[n + 1][m, r] for m in range(13)])
+            acc = [x + y for x, y in zip(acc, adds)]
+        for n, x in enumerate(acc):
+            out[n, r] = x
+
+
+def forward_kernel(gx_axis, halo, j, steps, *refs):
     refs = list(refs)
     take = lambda n: [refs.pop(0) for _ in range(n)]
-    f_ref, a_ref, p_ref, am_ref, bm_ref = take(5)
+    f_ref, p_ref, am_ref, bm_ref = take(4)
     first, final = j == 0, j == steps - 1
-    keep_f, keep_a = j < steps - 1 - j, j < steps - 1 - j
-    hk_ref = None if first else take(1)[0]
-    src_ref = rec_ref = None
-    if not final:
-        src_ref, rec_ref = take(2)
-    old_f_ref = old_a_ref = acc_ref = None
-    if not keep_f:
-        old_f_ref, old_a_ref = take(2)
-        if j - 1 >= steps - j:
-            acc_ref = take(1)[0]
+    if not first:
+        (hk_ref,) = take(1)
     if final:
-        grad_out, par_out = take(2)
-        f_out = a_out = None
+        old_ref, acc_ref, acc_out = take(3)
     else:
-        f_out, a_out, a_msg, b_msg = take(4)
-    hk_out = take(1)[0] if first else None
-    save_f = save_a = acc_out = None
-    if keep_f:
-        save_f, save_a = take(2)
-    elif not final:
-        acc_out = take(1)[0]
+        src_ref, f_out, a_msg, b_msg, save = take(5)
+    if first:
+        (hk_out,) = take(1)
     assert not refs
-
-    even = lax.rem(lax.axis_index(gx_axis), 2) == 0
     rows, planes, columns = f_ref.shape[1], f_ref.shape[2] // 2, f_ref.shape[3]
     tile = Tile(planes, columns, halo)
-    sides = receive(tile, gx_axis, am_ref, bm_ref, 2 * EDGE + (2 if first else 0))
+    sides = receive(tile, gx_axis, am_ref, bm_ref, EDGE + (2 if first else 0))
     p = lambda f, r: read(p_ref, f, r)
     old = lambda f, r: read(f_ref, f, r)
-    lam = lambda f, r: read(a_ref, f, r)
     hk = []
     for n in range(2):
         if first:
-            pair = sides[n][2 * EDGE : 2 * EDGE + 2]
+            pair = sides[n][EDGE : EDGE + 2]
             for m in range(2):
                 write(hk_out, pair[m], n, m)
         else:
             pair = [read(hk_ref, n, m) for m in range(2)]
         hk.append(pair)
-    slot = {XX: 0, XY: 1, XZ: 2, PP: 3}
-
-    def end(r):
-        return 0 if r < 0 else 1
 
     def s(f, r):
-        return old(f, r) if 0 <= r < rows else sides[end(r)][slot[f]]
+        return old(f, r) if 0 <= r < rows else sides[end(r)][SLOT[f]]
 
     @memo
     def velocity(r):
@@ -399,8 +430,7 @@
         }, None, None
 
     v = lambda f, r: velocity(r)[0][f]
-
-    def strain(r):
+    for r in range(rows):
         e = [dx(v, VX, r), tile.dy(v(VY, r)), tile.dz(v(VZ, r))]
         g = [
             tile.dz(v(VY, r)) + tile.dy(v(VZ, r)),
@@ -408,12 +438,52 @@
             tile.dy(v(VX, r)) + dx(v, VY, r),
         ]
         dw = dx(v, WX, r) + tile.dy(v(WY, r)) + tile.dz(v(WZ, r))
-        return e, g, dw
-
+        new, forces, pushes = velocity(r)
+        here = [x.m for x in forces + pushes] + [old(WX + i, r).m for i in range(3)]
+        here += [x.m for x in e + g] + [dw.m]
+        if final:
+            adds = sums(here, [old_ref[n, r] for n in range(13)])
+            for n, x in enumerate(adds):
+                acc_out[n, r] = acc_ref[n, r] + x
+            continue
+        for n, x in enumerate(here):
+            save[n, r] = x
+        new = dict(new)
+        dv = e[0] + e[1] + e[2]
+        sh, b = p(PS, r), p(PB, r)
+        ab = p(PA, r) * b
+        common = p(PL, r) * dv + ab * dw
+        for i in range(3):
+            new[XX + i] = old(XX + i, r) + (common + 2.0 * (sh * e[i]))
+            new[YZ + i] = old(YZ + i, r) + sh * g[i]
+        new[PP] = old(PP, r) - (ab * dv + b * dw) + read(src_ref, j, r)
+        factor = p(PF, r)
+        for f, value in new.items():
+            write(f_out, value * factor, f, r)
+    if not final:
+        even = lax.rem(lax.axis_index(gx_axis), 2) == 0
+        forward_messages(tile, even, f_out, p_ref, a_msg, b_msg, False)
+
+
+def adjoint_kernel(gx_axis, halo, j, steps, *refs):
+    refs = list(refs)
+    take = lambda n: [refs.pop(0) for _ in range(n)]
+    a_ref, p_ref, am_ref, bm_ref, hk_ref = take(5)
+    final = j == steps - 1
+    if final:
+        old_ref, acc_ref, grad_out, par_out = take(4)
+    else:
+        rec_ref, a_out, a_msg, b_msg, save = take(5)
+    assert not refs
+    rows, planes, columns = a_ref.shape[1], a_ref.shape[2] // 2, a_ref.shape[3]
+    tile = Tile(planes, columns, halo)
+    sides = receive(tile, gx_axis, am_ref, bm_ref, EDGE)
+    p = lambda f, r: read(p_ref, f, r)
+    lam = lambda f, r: read(a_ref, f, r)
     qs = memo(lambda r: adjoint_stress(p, lam, r))
 
     def q(f, r):
-        return qs(r)[f] if 0 <= r < rows else sides[end(r)][EDGE + slot[f]]
+        return qs(r)[f] if 0 <= r < rows else sides[end(r)][SLOT[f]]
 
     @memo
     def cots(r):
@@ -429,9 +499,9 @@
                 vel[WX + i] = lw - p(PM, r) * cg[i]
             return cf, cg, vel
         n = end(r)
-        got = sides[n][EDGE + 4 : EDGE + 8]
+        got = sides[n][4:8]
         edge = 0 if n == 0 else rows - 1
-        h, k = hk[n]
+        h, k = [read(hk_ref, n, m) for m in range(2)]
         t = -h if n == 0 else h
         xx, pp = t * q(XX, edge), t * q(PP, edge)
         return [
@@ -442,9 +512,9 @@
 
     cF = lambda i, r: cots(r)[0][i]
     cG = lambda i, r: cots(r)[1][i]
-
-    def adjoint_row(r):
-        out = dict(cots(r)[2])
+    for r in range(rows):
+        cf, cg, vel = cots(r)
+        out = dict(vel)
         out[XX] = lam(XX, r) - dx(cF, 0, r)
         out[YY] = lam(YY, r) - tile.dy(cF(1, r))
         out[ZZ] = lam(ZZ, r) - tile.dz(cF(2, r))
@@ -452,63 +522,20 @@
         out[XZ] = lam(XZ, r) - (tile.dz(cF(0, r)) + dx(cF, 2, r))
         out[XY] = lam(XY, r) - (tile.dy(cF(0, r)) + dx(cF, 1, r))
         out[PP] = lam(PP, r) + (dx(cG, 0, r) + tile.dy(cG(1, r)) + tile.dz(cG(2, r)))
-        return out
-
-    stress_names = (XX, YY, ZZ, YZ, XZ, XY, PP)
-    for r in range(rows):
-        e, g, dw = strain(r)
-        dv = e[0] + e[1] + e[2]
-        new, forces, pushes = velocity(r)
-        here_f = [x.m for x in forces + pushes] + [old(WX + i, r).m for i in range(3)]
-        here_f += [x.m for x in e + g] + [dw.m]
+        here = [x.m for x in cf + cg] + [lam(f, r).m for f in (XX, YY, ZZ, YZ, XZ, XY, PP)]
         if not final:
-            new = dict(new)
-            sh, b = p(PS, r), p(PB, r)
-            ab = p(PA, r) * b
-            common = p(PL, r) * dv + ab * dw
-            for i in range(3):
-                new[XX + i] = old(XX + i, r) + (common + 2.0 * (sh * e[i]))
-                new[YZ + i] = old(YZ + i, r) + sh * g[i]
-            new[PP] = old(PP, r) - (ab * dv + b * dw) + read(src_ref, j, r)
-            factor = p(PF, r)
-            for f, value in new.items():
-                write(f_out, value * factor, f, r)
-        back = adjoint_row(r)
-        cf, cg = cots(r)[0], cots(r)[1]
-        here_a = [x.m for x in cf + cg] + [lam(f, r).m for f in stress_names]
-        if final:
-            for f, value in back.items():
-                grad_out[f, pl.ds(r, planes, stride=rows), :] = value.m
-        else:
-            back[PP] = back[PP] + read(rec_ref, steps - 2 - j, r)
-            for f, value in back.items():
+            for n, x in enumerate(here):
+                save[n, r] = x
+            out[PP] = out[PP] + read(rec_ref, steps - 2 - j, r)
+            for f, value in out.items():
                 write(a_out, value * p(PF, r), f, r)
-        if keep_f:
-            for n, x in enumerate(here_f):
-                save_f[n, r] = x
-            for n, x in enumerate(here_a):
-                save_a[n, r] = x
             continue
-        acc = [0.0] * 9 if acc_ref is None else [acc_ref[n, r] for n in range(9)]
-        pairs = [(here_f, [old_a_ref[n, r] for n in range(13)])]
-        if 2 * j != steps - 1:
-            pairs.append(([old_f_ref[n, r] for n in range(16)], here_a))
-        for ff, aa in pairs:
-            fo, pu, wo, ee, gg, w_ = ff[0:3], ff[3:6], ff[6:9], ff[9:12], ff[12:15], ff[15]
-            af, ag, sg, pi = aa[0:3], aa[3:6], aa[6:12], aa[12]
-            tr, dd = sg[0] + sg[1] + sg[2], ee[0] + ee[1] + ee[2]
-            dot = lambda x, y: x[0] * y[0] + x[1] * y[1] + x[2] * y[2]
-            adds = [
-                dot(af, fo), dot(ag, pu), dot(af, pu), dot(ag, wo),
-                tr * dd, tr * w_, 2.0 * dot(sg[0:3], ee) + dot(sg[3:6], gg), pi * dd, pi * w_,
-            ]
-            acc = [x + y for x, y in zip(acc, adds)]
-        if not final:
-            for n, x in enumerate(acc):
-                acc_out[n, r] = x
-            continue
-        a1, a2, a3, a4, b1, b2, b3, b4, b5 = acc
-        h4, k, b, al = 4.0 * p_ref[PH, r, pl.ds(0, planes)], p_ref[PK, r, pl.ds(0, planes)], p_ref[PB, r, pl.ds(0, planes)], p_ref[PA, r, pl.ds(0, planes)]
+        for f, value in out.items():
+            grad_out[f, pl.ds(r, planes, stride=rows), :] = value.m
+        adds = sums([old_ref[n, r] for n in range(16)], here)
+        a1, a2, a3, a4, b1, b2, b3, b4, b5 = [acc_ref[n, r] + x for n, x in enumerate(adds)]
+        h, k, b, al = [p_ref[n, r, pl.ds(0, planes)] for n in (PH, PK, PB, PA)]
+        h4 = 4.0 * h
         grads = [
             h4 * (a3 - 3.0 * a1),
             h4 * (a1 + a2 - k * (3.0 * a2 + a3)),
@@ -521,7 +548,8 @@
         for n, x in enumerate(grads):
             par_out[n, pl.ds(r, planes, stride=rows), :] = x
     if not final:
-        messages(tile, even, f_out, a_out, p_ref, a_msg, b_msg, False)
+        even = lax.rem(lax.axis_index(gx_axis), 2) == 0
+        adjoint_messages(tile, even, a_out, p_ref, a_msg, b_msg)
 
 
 def swaps(axis, odd):
@@ -565,7 +593,7 @@
     steps = source_amp.shape[0]
     count = fields.shape[0]
     halo = 2 * steps
-    assert steps % 2 == 0 and planes == 8 and columns == 128 and columns % (2 * halo) == 0 and rows > 1
+    assert steps > 2 and planes == 8 and columns == 128 and columns % (2 * halo) == 0 and rows > 1
     flat = lambda x: x.reshape(-1, planes * rows, columns)
     fields, field_cot = flat(fields), flat(field_cot)
     raw = [flat(x) for x in (density, fluid_density, mobility, lame_lambda, shear_modulus, biot_modulus, biot_coef)]
@@ -598,46 +626,42 @@
     )(*[pltpu.with_memory_space_constraint(x, pltpu.HBM) for x in inputs])
     ay, by = exchange("gy", ay, by)
     rec, src = call(functools.partial(inject_kernel, halo, "gx", "gy"), [(steps, *wide)] * 2, *small)
-    tiles = lambda n: n + -(-n * 2 * halo // columns)
-    f, a, p, am, bm = call(
-        functools.partial(spread_kernel, halo, "gx", "gy"),
-        [(count, *wide)] * 2 + [(8, *wide)] + [(tiles(2 * EDGE + 2), planes, columns)] * 2,
-        fields, field_cot, p_own, ay, by, rec,
+    tiles = lambda n: (n + -(-n * 2 * halo // columns), planes, columns)
+    names = (halo, "gx", "gy")
+    f, p, am, bm = call(
+        functools.partial(spread_forward, *names),
+        [(count, *wide), (8, *wide)] + [tiles(EDGE + 2)] * 2, fields, p_own, ay, by,
+        rec,
     )
-    saved, hk, acc = [], None, None
-    for j in range(steps):
-        am, bm = exchange("gx", am, bm)
-        args, outs = [f, a, p, am, bm], []
-        final, keep = j == steps - 1, j < steps - 1 - j
-        if j:
-            args.append(hk)
-        if not final:
-            args += [src, rec]
-            outs += [(count, *wide)] * 2 + [(tiles(2 * EDGE), planes, columns)] * 2
-        else:
-            outs += [(count, planes * rows, columns), (7, planes * rows, columns)]
-        if j == 0:
-            outs.append((2, 2, 2 * planes, columns))
-        if keep:
-            outs += [(16, *own), (13, *own)]
-        else:
-            args += saved[steps - 1 - j]
-            if acc is not None:
-                args.append(acc)
-            if not final:
-                outs.append((9, *own))
-        got = list(call(functools.partial(step_kernel, "gx", halo, j, steps), outs, *args))
-        if final:
-            return got[0].reshape(count, planes, rows, columns), got[1].reshape(7, planes, rows, columns)
-        f, a, am, bm = got[:4]
-        got = got[4:]
-        if j == 0:
-            hk = got.pop(0)
-        if keep:
-            saved.append(got)
-        else:
-            saved.append(None)
-            acc = got[0]
+    forward = exchange("gx", am, bm)
+    a, am, bm = call(
+        functools.partial(spread_adjoint, *names), [(count, *wide)] + [tiles(EDGE)] * 2, field_cot, p, ay, by, rec,
+    )
+    adjoint = exchange("gx", am, bm)
+    saved_f, saved_a, hk = [], [], None
+    for j in range(steps - 1):
+        args = [f, p, *forward] + ([src] if j == 0 else [hk, src])
+        outs = [(count, *wide)] + [tiles(EDGE)] * 2 + [(16, *own)] + ([(2, 2, 2 * planes, columns)] if j == 0 else [])
+        f, am, bm, save, *rest = call(functools.partial(forward_kernel, "gx", halo, j, steps), outs, *args)
+        forward = exchange("gx", am, bm)
+        saved_f.append(save)
+        hk = rest[0] if j == 0 else hk
+        outs = [(count, *wide)] + [tiles(EDGE)] * 2 + [(13, *own)]
+        a, am, bm, save = call(
+            functools.partial(adjoint_kernel, "gx", halo, j, steps), outs, a, p, *adjoint, hk, rec
+        )
+        adjoint = exchange("gx", am, bm)
+        saved_a.append(save)
+    middle = [x for t in range(1, steps - 1) for x in (saved_f[t], saved_a[steps - 1 - t])]
+    (acc,) = call(sums_kernel, [(9, *own)], *middle)
+    (acc,) = call(
+        functools.partial(forward_kernel, "gx", halo, steps - 1, steps), [(9, *own)], f, p, *forward, hk, saved_a[0], acc
+    )
+    grad, par = call(
+        functools.partial(adjoint_kernel, "gx", halo, steps - 1, steps),
+        [(count, *plane), (7, *plane)], a, p, *adjoint, hk, saved_f[0], acc,
+    )
+    return grad.reshape(count, planes, rows, columns), par.reshape(7, planes, rows, columns)
 
 
 def solution(mesh):

time: 39.1 us -> 38.9 us (level)
  waiting for transfers between devices: 19.7 us -> 8.64 us
  starting transfers between devices: 9.53 us -> 19.4 us
  Pallas kernels: 9.01 us -> 10 us
    ppermute x5 -> x9, waiting for transfers between devices: 10.9 us -> 1.14 us  [exchange(): a = lax.ppermute(a, mesh, swaps(axis, 0))]
    ppermute x5 -> x9, starting transfers between devices: 4.91 us -> 9.95 us  [exchange(): a = lax.ppermute(a, mesh, swaps(axis, 0))]
    ppermute x5 -> x9, starting transfers between devices: 4.63 us -> 9.46 us  [exchange(): b = lax.ppermute(b, mesh, swaps(axis, 1))]
    ppermute x5 -> x9, waiting for transfers between devices: 8.86 us -> 7.5 us  [exchange(): b = lax.ppermute(b, mesh, swaps(axis, 1))]
    pallas_call x6 -> x12, Pallas kernels: 7.06 us -> 8.05 us  [call(): pl.pallas_call(kernel, out_shape=shapes, in_specs=[pl.BlockSpec(memory_sp...]
  transfers between devices with their start and end apart: 10 -> 18, of which waited for: 9 -> 8; matrix products, arithmetic and copies ran while one was open for 0% -> 0% of each run, Pallas kernels for 3% -> 16%
where the time goes in v3:
time: 38.9 us; the launch traced here: 38.8 us
  starting transfers between devices  19.4 us (50%)
  Pallas kernels  10 us (26%)
  waiting for transfers between devices  8.64 us (22%)
  between operations  0.72 us (2%)
    ppermute x9, starting transfers between devices, exchange(): a = lax.ppermute(a, mesh, swaps(axis, 0))  9.95 us
    ppermute x9, starting transfers between devices, exchange(): b = lax.ppermute(b, mesh, swaps(axis, 1))  9.46 us
    pallas_call x12, Pallas kernels, call(): pl.pallas_call(kernel, out_shape=shapes, in_specs=[pl.BlockSpec(memory_sp...  8.05 us
    ppermute x9, waiting for transfers between devices, exchange(): b = lax.ppermute(b, mesh, swaps(axis, 1))  7.5 us
    pallas_call x1, Pallas kernels, per_device(): pl.pallas_call(start, out_shape=[jax.ShapeDtypeStruct(s, jnp.float32) for...  1.95 us
    ppermute x9, waiting for transfers between devices, exchange(): a = lax.ppermute(a, mesh, swaps(axis, 0))  1.14 us
  transfers between devices with their start and end apart: 18, of which 8 were waited for; matrix products, arithmetic and copies ran while one was open for 0% of the time, Pallas kernels for 16%

profile of v3, /device:TPU:16, one launch (start us, length us, event | category | flops | bytes accessed | tf_op | source)
XLA Modules:
  0.0 38.8 jit_solution(4237525903574328615)
XLA Ops:
  0.6 1.9 %shard_map.167 = (f32[8,8,8,128]{3,2,1,0:T(8,128)S(1)}, f32[17,8,128]{2,1,0:T(8,128)S(1)}, f32[17,8,128]{2,1,0:T(8,128)S(1)}, f32[13,64,128]{2,1,0:T(8,128)S(1)}...) custom-call(f32[1,64,128]{2,1,0:T(8,128)} %bitcast.18, ...), custom_call_target="tpu_custom_call" | custom-call | tf_op jit(solution)/shard_map/pallas_call | solution.py:614
  2.6 0.1 collective-permute-start
  2.7 1.6 %collective-permute-start.1 = (f32[17,8,128]{2,1,0:T(8,128)S(1)}, f32[17,8,128]{2,1,0:T(8,128)S(1)}, u32[]{:S(2)}, u32[]{:S(2)}) collective-permute-start(f32[17,8,128]{2,1,0:T(8,128)S(1)} %get-tuple-element.51), channel_id=1, source_target_pairs={{0,4},{1,2},{2,1},{3,7},{4,0},{5,6},{6,5},{7,3},{8,12},{9,10},{10,... | collective-permute-start | bytes 208904 | tf_op jit(solution)/shard_map/ppermute | solution.py:572
  4.2 1.2 %shard_map.168 = (f32[4,8,16,128]{3,2,1,0:T(8,128)S(1)}, f32[4,8,16,128]{3,2,1,0:T(8,128)S(1)}) custom-call(s32[1,512]{1,0:T(1,128)S(1)} %get-tuple-element.52.rec_ref, f32[4,512]{1,0:T(4,128)S(1)} %get-tuple-element.53.cot_ref, s32[1,64]{1,0:T(1,128)S(1)} %get-tuple-element.54.src_ref, f32[4,64]{1,0:T(4,128)S(1)} %get-tuple-element.55.amp_ref), custom_call_target="tpu_custom_call" | custom-call | tf_op jit(solution)/shard_map/pallas_call | solution.py:579
  5.4 0.0 collective-permute-done.ay_ref
  5.4 1.6 %collective-permute-done.1.by_ref = f32[17,8,128]{2,1,0:T(8,128)S(1)} collective-permute-done((f32[17,8,128]{2,1,0:T(8,128)S(1)}, f32[17,8,128]{2,1,0:T(8,128)S(1)}, u32[]{:S(2)}, u32[]{:S(2)}) %collective-permute-start.1) | collective-permute-done | bytes 69664 | tf_op jit(solution)/shard_map/ppermute | solution.py:572
  7.0 0.5 %shard_map.169 = (f32[13,8,16,128]{3,2,1,0:T(8,128)S(1)}, f32[8,8,16,128]{3,2,1,0:T(8,128)S(1)}, f32[12,8,128]{2,1,0:T(8,128)S(1)}, f32[12,8,128]{2,1,0:T(8,128)S(1)}) custom-call(f32[13,64,128]{2,1,0:T(8,128)S(1)} %get-tuple-element.48.fields_ref, f32[8,8,8,128]{3,2,1,0:T(8,128)S(1)} %get-tuple-element.49.pm_ref, ...), custom_call_target="tpu_custom_call" | custom-call | tf_op jit(solution)/shard_map/pallas_call | solution.py:579
  7.6 1.6 %collective-permute-start.4 = (f32[12,8,128]{2,1,0:T(8,128)S(1)}, f32[12,8,128]{2,1,0:T(8,128)S(1)}, u32[]{:S(2)}, u32[]{:S(2)}) collective-permute-start(f32[12,8,128]{2,1,0:T(8,128)S(1)} %get-tuple-element.62), channel_id=1, source_target_pairs={{0,4},{1,5},{2,6},{3,7},{4,0},{5,1},{6,2},{7,3},{8,12},{9,13},{10,... | collective-permute-start | bytes 147464 | tf_op jit(solution)/shard_map/ppermute | solution.py:573
  9.1 0.4 %collective-permute-start.5 = (f32[12,8,128]{2,1,0:T(8,128)S(1)}, f32[12,8,128]{2,1,0:T(8,128)S(1)}, u32[]{:S(2)}, u32[]{:S(2)}) collective-permute-start(f32[12,8,128]{2,1,0:T(8,128)S(1)} %get-tuple-element.63), channel_id=1, source_target_pairs={{0,1},{1,0},{2,3},{3,2},{4,8},{5,9},{6,10},{7,11},{8,4},{9,5},{10,... | collective-permute-start | bytes 147464 | tf_op jit(solution)/shard_map/ppermute | solution.py:572
  9.6 0.4 %shard_map.170 = (f32[13,8,16,128]{3,2,1,0:T(8,128)S(1)}, f32[9,8,128]{2,1,0:T(8,128)S(1)}, f32[9,8,128]{2,1,0:T(8,128)S(1)}) custom-call(f32[13,64,128]{2,1,0:T(8,128)S(1)} %get-tuple-element.47.cot_ref, f32[8,8,16,128]{3,2,1,0:T(8,128)S(1)} %get-tuple-element.57.p_ref.refs_1_, f32[17,8,128]{2,1,0:T(8,128)S(1)} %collective-permute-done.ay_ref, ...), custom_call_target="tpu_custom_call" | custom-call | tf_op jit(solution)/shard_map/pallas_call | solution.py:579
  10.0 2.7 %collective-permute-start.2 = (f32[9,8,128]{2,1,0:T(8,128)S(1)}, f32[9,8,128]{2,1,0:T(8,128)S(1)}, u32[]{:S(2)}, u32[]{:S(2)}) collective-permute-start(f32[9,8,128]{2,1,0:T(8,128)S(1)} %get-tuple-element.59), channel_id=1, source_target_pairs={{0,4},{1,5},{2,6},{3,7},{4,0},{5,1},{6,2},{7,3},{8,12},{9,13},{10,... | collective-permute-start | bytes 110600 | tf_op jit(solution)/shard_map/ppermute | solution.py:573
  12.7 0.0 collective-permute-start.3
  12.7 0.0 collective-permute-done.4.refs_2_
  12.7 1.5 %collective-permute-done.5.refs_3_ = f32[12,8,128]{2,1,0:T(8,128)S(1)} collective-permute-done((f32[12,8,128]{2,1,0:T(8,128)S(1)}, f32[12,8,128]{2,1,0:T(8,128)S(1)}, u32[]{:S(2)}, u32[]{:S(2)}) %collective-permute-start.5) | collective-permute-done | bytes 49184 | tf_op jit(solution)/shard_map/ppermute | solution.py:572
  14.1 0.7 %shard_map.171 = (f32[13,8,16,128]{3,2,1,0:T(8,128)S(1)}, f32[9,8,128]{2,1,0:T(8,128)S(1)}, f32[9,8,128]{2,1,0:T(8,128)S(1)}, f32[16,8,8,128]{3,2,1,0:T(8,128)S(1)}, f32[2,2,16,128]{3,2,1,0:T(8,128)S(1)}) custom-call(f32[13,8,16,128]{3,2,1,0:T(8,128)S(1)} %get-tuple-element.61.refs_0_, f32[8,8,16,128]{3,2,1,0:T(8,128)S(1)} %get-tuple-element.57.p_ref.refs_1_, ...), custom_call_target="tpu_custom_call" | custom-call | tf_op jit(solution)/shard_map/pallas_call | solution.py:579
  14.8 0.6 %collective-permute-start.12 = (f32[9,8,128]{2,1,0:T(8,128)S(1)}, f32[9,8,128]{2,1,0:T(8,128)S(1)}, u32[]{:S(2)}, u32[]{:S(2)}) collective-permute-start(f32[9,8,128]{2,1,0:T(8,128)S(1)} %get-tuple-element.77), channel_id=1, source_target_pairs={{0,4},{1,5},{2,6},{3,7},{4,0},{5,1},{6,2},{7,3},{8,12},{9,13},{10,... | collective-permute-start | bytes 110600 | tf_op jit(solution)/shard_map/ppermute | solution.py:573
  15.4 1.4 %collective-permute-start.13 = (f32[9,8,128]{2,1,0:T(8,128)S(1)}, f32[9,8,128]{2,1,0:T(8,128)S(1)}, u32[]{:S(2)}, u32[]{:S(2)}) collective-permute-start(f32[9,8,128]{2,1,0:T(8,128)S(1)} %get-tuple-element.78), channel_id=1, source_target_pairs={{0,1},{1,0},{2,3},{3,2},{4,8},{5,9},{6,10},{7,11},{8,4},{9,5},{10,... | collective-permute-start | bytes 110600 | tf_op jit(solution)/shard_map/ppermute | solution.py:572
  16.8 0.0 collective-permute-done.2.refs_2_
  16.8 0.9 %collective-permute-done.3.refs_3_ = f32[9,8,128]{2,1,0:T(8,128)S(1)} collective-permute-done((f32[9,8,128]{2,1,0:T(8,128)S(1)}, f32[9,8,128]{2,1,0:T(8,128)S(1)}, u32[]{:S(2)}, u32[]{:S(2)}) %collective-permute-start.3) | collective-permute-done | bytes 36896 | tf_op jit(solution)/shard_map/ppermute | solution.py:572
  17.6 0.6 %shard_map.172 = (f32[13,8,16,128]{3,2,1,0:T(8,128)S(1)}, f32[9,8,128]{2,1,0:T(8,128)S(1)}, f32[9,8,128]{2,1,0:T(8,128)S(1)}, f32[13,8,8,128]{3,2,1,0:T(8,128)S(1)}) custom-call(f32[13,8,16,128]{3,2,1,0:T(8,128)S(1)} %get-tuple-element.58.refs_0_, f32[8,8,16,128]{3,2,1,0:T(8,128)S(1)} %get-tuple-element.57.p_ref.refs_1_, ...), custom_call_target="tpu_custom_call" | custom-call | tf_op jit(solution)/shard_map/pallas_call | solution.py:579
  18.3 0.8 %collective-permute-start.6 = (f32[9,8,128]{2,1,0:T(8,128)S(1)}, f32[9,8,128]{2,1,0:T(8,128)S(1)}, u32[]{:S(2)}, u32[]{:S(2)}) collective-permute-start(f32[9,8,128]{2,1,0:T(8,128)S(1)} %get-tuple-element.67), channel_id=1, source_target_pairs={{0,4},{1,5},{2,6},{3,7},{4,0},{5,1},{6,2},{7,3},{8,12},{9,13},{10,... | collective-permute-start | bytes 110600 | tf_op jit(solution)/shard_map/ppermute | solution.py:573
  19.0 1.1 %collective-permute-start.7 = (f32[9,8,128]{2,1,0:T(8,128)S(1)}, f32[9,8,128]{2,1,0:T(8,128)S(1)}, u32[]{:S(2)}, u32[]{:S(2)}) collective-permute-start(f32[9,8,128]{2,1,0:T(8,128)S(1)} %get-tuple-element.68), channel_id=1, source_target_pairs={{0,1},{1,0},{2,3},{3,2},{4,8},{5,9},{6,10},{7,11},{8,4},{9,5},{10,... | collective-permute-start | bytes 110600 | tf_op jit(solution)/shard_map/ppermute | solution.py:572
  20.1 0.0 collective-permute-done.12.refs_2_
  20.1 0.1 collective-permute-done.13.refs_3_
  20.2 0.7 %shard_map.175 = (f32[13,8,16,128]{3,2,1,0:T(8,128)S(1)}, f32[9,8,128]{2,1,0:T(8,128)S(1)}, f32[9,8,128]{2,1,0:T(8,128)S(1)}, f32[16,8,8,128]{3,2,1,0:T(8,128)S(1)}) custom-call(f32[13,8,16,128]{3,2,1,0:T(8,128)S(1)} %get-tuple-element.76.refs_0_, f32[8,8,16,128]{3,2,1,0:T(8,128)S(1)} %get-tuple-element.57.p_ref.refs_1_, ...), custom_call_target="tpu_custom_call" | custom-call | tf_op jit(solution)/shard_map/pallas_call | solution.py:579
  20.9 1.5 %collective-permute-start.14 = (f32[9,8,128]{2,1,0:T(8,128)S(1)}, f32[9,8,128]{2,1,0:T(8,128)S(1)}, u32[]{:S(2)}, u32[]{:S(2)}) collective-permute-start(f32[9,8,128]{2,1,0:T(8,128)S(1)} %get-tuple-element.80), channel_id=1, source_target_pairs={{0,4},{1,5},{2,6},{3,7},{4,0},{5,1},{6,2},{7,3},{8,12},{9,13},{10,... | collective-permute-start | bytes 110600 | tf_op jit(solution)/shard_map/ppermute | solution.py:573
  22.5 1.5 %collective-permute-start.15 = (f32[9,8,128]{2,1,0:T(8,128)S(1)}, f32[9,8,128]{2,1,0:T(8,128)S(1)}, u32[]{:S(2)}, u32[]{:S(2)}) collective-permute-start(f32[9,8,128]{2,1,0:T(8,128)S(1)} %get-tuple-element.81), channel_id=1, source_target_pairs={{0,1},{1,0},{2,3},{3,2},{4,8},{5,9},{6,10},{7,11},{8,4},{9,5},{10,... | collective-permute-start | bytes 110600 | tf_op jit(solution)/shard_map/ppermute | solution.py:572
  24.0 0.0 collective-permute-done.6.refs_2_
  24.0 0.0 collective-permute-done.7.refs_3_
  24.0 0.6 %shard_map.173 = (f32[13,8,16,128]{3,2,1,0:T(8,128)S(1)}, f32[9,8,128]{2,1,0:T(8,128)S(1)}, f32[9,8,128]{2,1,0:T(8,128)S(1)}, f32[13,8,8,128]{3,2,1,0:T(8,128)S(1)}) custom-call(f32[13,8,16,128]{3,2,1,0:T(8,128)S(1)} %get-tuple-element.66.refs_0_, f32[8,8,16,128]{3,2,1,0:T(8,128)S(1)} %get-tuple-element.57.p_ref.refs_1_, ...), custom_call_target="tpu_custom_call" | custom-call | tf_op jit(solution)/shard_map/pallas_call | solution.py:579
  24.6 1.3 %collective-permute-start.8 = (f32[9,8,128]{2,1,0:T(8,128)S(1)}, f32[9,8,128]{2,1,0:T(8,128)S(1)}, u32[]{:S(2)}, u32[]{:S(2)}) collective-permute-start(f32[9,8,128]{2,1,0:T(8,128)S(1)} %get-tuple-element.70), channel_id=1, source_target_pairs={{0,4},{1,5},{2,6},{3,7},{4,0},{5,1},{6,2},{7,3},{8,12},{9,13},{10,... | collective-permute-start | bytes 110600 | tf_op jit(solution)/shard_map/ppermute | solution.py:573
  25.9 0.8 %collective-permute-start.9 = (f32[9,8,128]{2,1,0:T(8,128)S(1)}, f32[9,8,128]{2,1,0:T(8,128)S(1)}, u32[]{:S(2)}, u32[]{:S(2)}) collective-permute-start(f32[9,8,128]{2,1,0:T(8,128)S(1)} %get-tuple-element.71), channel_id=1, source_target_pairs={{0,1},{1,0},{2,3},{3,2},{4,8},{5,9},{6,10},{7,11},{8,4},{9,5},{10,... | collective-permute-start | bytes 110600 | tf_op jit(solution)/shard_map/ppermute | solution.py:572
  26.7 0.0 collective-permute-done.14.refs_2_
  26.7 0.9 %collective-permute-done.15.refs_3_ = f32[9,8,128]{2,1,0:T(8,128)S(1)} collective-permute-done((f32[9,8,128]{2,1,0:T(8,128)S(1)}, f32[9,8,128]{2,1,0:T(8,128)S(1)}, u32[]{:S(2)}, u32[]{:S(2)}) %collective-permute-start.15) | collective-permute-done | bytes 36896 | tf_op jit(solution)/shard_map/ppermute | solution.py:572
  27.5 0.7 %shard_map.176 = (f32[13,8,16,128]{3,2,1,0:T(8,128)S(1)}, f32[9,8,128]{2,1,0:T(8,128)S(1)}, f32[9,8,128]{2,1,0:T(8,128)S(1)}, f32[16,8,8,128]{3,2,1,0:T(8,128)S(1)}) custom-call(f32[13,8,16,128]{3,2,1,0:T(8,128)S(1)} %get-tuple-element.79.refs_0_, f32[8,8,16,128]{3,2,1,0:T(8,128)S(1)} %get-tuple-element.57.p_ref.refs_1_, ...), custom_call_target="tpu_custom_call" | custom-call | tf_op jit(solution)/shard_map/pallas_call | solution.py:579
  28.2 0.4 %collective-permute-start.16 = (f32[9,8,128]{2,1,0:T(8,128)S(1)}, f32[9,8,128]{2,1,0:T(8,128)S(1)}, u32[]{:S(2)}, u32[]{:S(2)}) collective-permute-start(f32[9,8,128]{2,1,0:T(8,128)S(1)} %get-tuple-element.83), channel_id=1, source_target_pairs={{0,4},{1,5},{2,6},{3,7},{4,0},{5,1},{6,2},{7,3},{8,12},{9,13},{10,... | collective-permute-start | bytes 110600 | tf_op jit(solution)/shard_map/ppermute | solution.py:573
  28.6 1.6 %collective-permute-start.17 = (f32[9,8,128]{2,1,0:T(8,128)S(1)}, f32[9,8,128]{2,1,0:T(8,128)S(1)}, u32[]{:S(2)}, u32[]{:S(2)}) collective-permute-start(f32[9,8,128]{2,1,0:T(8,128)S(1)} %get-tuple-element.84), channel_id=1, source_target_pairs={{0,1},{1,0},{2,3},{3,2},{4,8},{5,9},{6,10},{7,11},{8,4},{9,5},{10,... | collective-permute-start | bytes 110600 | tf_op jit(solution)/shard_map/ppermute | solution.py:572
  30.3 0.0 collective-permute-done.8.refs_2_
  30.3 0.6 %collective-permute-done.9.refs_3_ = f32[9,8,128]{2,1,0:T(8,128)S(1)} collective-permute-done((f32[9,8,128]{2,1,0:T(8,128)S(1)}, f32[9,8,128]{2,1,0:T(8,128)S(1)}, u32[]{:S(2)}, u32[]{:S(2)}) %collective-permute-start.9) | collective-permute-done | bytes 36896 | tf_op jit(solution)/shard_map/ppermute | solution.py:572
  30.9 0.6 %shard_map.174 = (f32[13,8,16,128]{3,2,1,0:T(8,128)S(1)}, f32[9,8,128]{2,1,0:T(8,128)S(1)}, f32[9,8,128]{2,1,0:T(8,128)S(1)}, f32[13,8,8,128]{3,2,1,0:T(8,128)S(1)}) custom-call(f32[13,8,16,128]{3,2,1,0:T(8,128)S(1)} %get-tuple-element.69.refs_0_, f32[8,8,16,128]{3,2,1,0:T(8,128)S(1)} %get-tuple-element.57.p_ref.refs_1_, ...), custom_call_target="tpu_custom_call" | custom-call | tf_op jit(solution)/shard_map/pallas_call | solution.py:579
  31.5 1.1 %collective-permute-start.10 = (f32[9,8,128]{2,1,0:T(8,128)S(1)}, f32[9,8,128]{2,1,0:T(8,128)S(1)}, u32[]{:S(2)}, u32[]{:S(2)}) collective-permute-start(f32[9,8,128]{2,1,0:T(8,128)S(1)} %get-tuple-element.73), channel_id=1, source_target_pairs={{0,4},{1,5},{2,6},{3,7},{4,0},{5,1},{6,2},{7,3},{8,12},{9,13},{10,... | collective-permute-start | bytes 110600 | tf_op jit(solution)/shard_map/ppermute | solution.py:573
  32.6 1.1 %collective-permute-start.11 = (f32[9,8,128]{2,1,0:T(8,128)S(1)}, f32[9,8,128]{2,1,0:T(8,128)S(1)}, u32[]{:S(2)}, u32[]{:S(2)}) collective-permute-start(f32[9,8,128]{2,1,0:T(8,128)S(1)} %get-tuple-element.74), channel_id=1, source_target_pairs={{0,1},{1,0},{2,3},{3,2},{4,8},{5,9},{6,10},{7,11},{8,4},{9,5},{10,... | collective-permute-start | bytes 110600 | tf_op jit(solution)/shard_map/ppermute | solution.py:572
  33.7 0.2 shard_map.177.refs_6_
  33.8 0.0 collective-permute-done.16.refs_2_
  33.9 0.0 collective-permute-done.17.refs_3_
  33.9 0.5 %shard_map.178.refs_6_ = f32[9,8,8,128]{3,2,1,0:T(8,128)S(1)} custom-call(f32[13,8,16,128]{3,2,1,0:T(8,128)S(1)} %get-tuple-element.82.refs_0_, f32[8,8,16,128]{3,2,1,0:T(8,128)S(1)} %get-tuple-element.57.p_ref.refs_1_, f32[9,8,128]{2,1,0:T(8,128)S(1)} %collective-permute-done.16.refs_2_, f32[9,8,128]{2,1,0:T(8,128)S(1)} %collective-permute-done.17.refs_3_, ...), custom_call_target="tpu_custom_call" | custom-call | tf_op jit(solution)/shard_map/pallas_call | solution.py:579
  34.4 1.1 %collective-permute-done.10.refs_2_ = f32[9,8,128]{2,1,0:T(8,128)S(1)} collective-permute-done((f32[9,8,128]{2,1,0:T(8,128)S(1)}, f32[9,8,128]{2,1,0:T(8,128)S(1)}, u32[]{:S(2)}, u32[]{:S(2)}) %collective-permute-start.10) | collective-permute-done | bytes 36896 | tf_op jit(solution)/shard_map/ppermute | solution.py:573
  35.5 2.0 %collective-permute-done.11.refs_3_ = f32[9,8,128]{2,1,0:T(8,128)S(1)} collective-permute-done((f32[9,8,128]{2,1,0:T(8,128)S(1)}, f32[9,8,128]{2,1,0:T(8,128)S(1)}, u32[]{:S(2)}, u32[]{:S(2)}) %collective-permute-start.11) | collective-permute-done | bytes 36896 | tf_op jit(solution)/shard_map/ppermute | solution.py:572
  37.5 1.3 %shard_map.179 = (f32[13,64,128]{2,1,0:T(8,128)}, f32[7,64,128]{2,1,0:T(8,128)}) custom-call(f32[13,8,16,128]{3,2,1,0:T(8,128)S(1)} %get-tuple-element.72.refs_0_, f32[8,8,16,128]{3,2,1,0:T(8,128)S(1)} %get-tuple-element.57.p_ref.refs_1_, f32[9,8,128]{2,1,0:T(8,128)S(1)} %collective-permute-done.10.refs_2_, ...), custom_call_target="tpu_custom_call" | custom-call | tf_op jit(solution)/shard_map/pallas_call | solution.py:579
Async XLA Ops:
  2.6 2.8 %collective-permute-start = (f32[17,8,128]{2,1,0:T(8,128)S(1)}, f32[17,8,128]{2,1,0:T(8,128)S(1)}, u32[]{:S(2)}, u32[]{:S(2)}) collective-permute-start(f32[17,8,128]{2,1,0:T(8,128)S(1)} %get-tuple-element.50), channel_id=1, source_target_pairs={{0,1},{1,0},{2,3},{3,2},{4,5},{5,4},{6,7},{7,6},{8,9},{9,8},{10,11... | collective-permute-start | bytes 208904 | tf_op jit(solution)/shard_map/ppermute | solution.py:573
  2.7 4.4 %collective-permute-start.1 = (f32[17,8,128]{2,1,0:T(8,128)S(1)}, f32[17,8,128]{2,1,0:T(8,128)S(1)}, u32[]{:S(2)}, u32[]{:S(2)}) collective-permute-start(f32[17,8,128]{2,1,0:T(8,128)S(1)} %get-tuple-element.51), channel_id=1, source_target_pairs={{0,4},{1,2},{2,1},{3,7},{4,0},{5,6},{6,5},{7,3},{8,12},{9,10},{10,... | collective-permute-start | bytes 208904 | tf_op jit(solution)/shard_map/ppermute | solution.py:572
  7.6 5.1 %collective-permute-start.4 = (f32[12,8,128]{2,1,0:T(8,128)S(1)}, f32[12,8,128]{2,1,0:T(8,128)S(1)}, u32[]{:S(2)}, u32[]{:S(2)}) collective-permute-start(f32[12,8,128]{2,1,0:T(8,128)S(1)} %get-tuple-element.62), channel_id=1, source_target_pairs={{0,4},{1,5},{2,6},{3,7},{4,0},{5,1},{6,2},{7,3},{8,12},{9,13},{10,... | collective-permute-start | bytes 147464 | tf_op jit(solution)/shard_map/ppermute | solution.py:573
  9.1 5.0 %collective-permute-start.5 = (f32[12,8,128]{2,1,0:T(8,128)S(1)}, f32[12,8,128]{2,1,0:T(8,128)S(1)}, u32[]{:S(2)}, u32[]{:S(2)}) collective-permute-start(f32[12,8,128]{2,1,0:T(8,128)S(1)} %get-tuple-element.63), channel_id=1, source_target_pairs={{0,1},{1,0},{2,3},{3,2},{4,8},{5,9},{6,10},{7,11},{8,4},{9,5},{10,... | collective-permute-start | bytes 147464 | tf_op jit(solution)/shard_map/ppermute | solution.py:572
  10.0 6.8 %collective-permute-start.2 = (f32[9,8,128]{2,1,0:T(8,128)S(1)}, f32[9,8,128]{2,1,0:T(8,128)S(1)}, u32[]{:S(2)}, u32[]{:S(2)}) collective-permute-start(f32[9,8,128]{2,1,0:T(8,128)S(1)} %get-tuple-element.59), channel_id=1, source_target_pairs={{0,4},{1,5},{2,6},{3,7},{4,0},{5,1},{6,2},{7,3},{8,12},{9,13},{10,... | collective-permute-start | bytes 110600 | tf_op jit(solution)/shard_map/ppermute | solution.py:573
  12.7 5.0 %collective-permute-start.3 = (f32[9,8,128]{2,1,0:T(8,128)S(1)}, f32[9,8,128]{2,1,0:T(8,128)S(1)}, u32[]{:S(2)}, u32[]{:S(2)}) collective-permute-start(f32[9,8,128]{2,1,0:T(8,128)S(1)} %get-tuple-element.60), channel_id=1, source_target_pairs={{0,1},{1,0},{2,3},{3,2},{4,8},{5,9},{6,10},{7,11},{8,4},{9,5},{10,... | collective-permute-start | bytes 110600 | tf_op jit(solution)/shard_map/ppermute | solution.py:572
  14.8 5.3 %collective-permute-start.12 = (f32[9,8,128]{2,1,0:T(8,128)S(1)}, f32[9,8,128]{2,1,0:T(8,128)S(1)}, u32[]{:S(2)}, u32[]{:S(2)}) collective-permute-start(f32[9,8,128]{2,1,0:T(8,128)S(1)} %get-tuple-element.77), channel_id=1, source_target_pairs={{0,4},{1,5},{2,6},{3,7},{4,0},{5,1},{6,2},{7,3},{8,12},{9,13},{10,... | collective-permute-start | bytes 110600 | tf_op jit(solution)/shard_map/ppermute | solution.py:573
  15.4 4.9 %collective-permute-start.13 = (f32[9,8,128]{2,1,0:T(8,128)S(1)}, f32[9,8,128]{2,1,0:T(8,128)S(1)}, u32[]{:S(2)}, u32[]{:S(2)}) collective-permute-start(f32[9,8,128]{2,1,0:T(8,128)S(1)} %get-tuple-element.78), channel_id=1, source_target_pairs={{0,1},{1,0},{2,3},{3,2},{4,8},{5,9},{6,10},{7,11},{8,4},{9,5},{10,... | collective-permute-start | bytes 110600 | tf_op jit(solution)/shard_map/ppermute | solution.py:572
  18.3 5.7 %collective-permute-start.6 = (f32[9,8,128]{2,1,0:T(8,128)S(1)}, f32[9,8,128]{2,1,0:T(8,128)S(1)}, u32[]{:S(2)}, u32[]{:S(2)}) collective-permute-start(f32[9,8,128]{2,1,0:T(8,128)S(1)} %get-tuple-element.67), channel_id=1, source_target_pairs={{0,4},{1,5},{2,6},{3,7},{4,0},{5,1},{6,2},{7,3},{8,12},{9,13},{10,... | collective-permute-start | bytes 110600 | tf_op jit(solution)/shard_map/ppermute | solution.py:573
  19.0 5.0 %collective-permute-start.7 = (f32[9,8,128]{2,1,0:T(8,128)S(1)}, f32[9,8,128]{2,1,0:T(8,128)S(1)}, u32[]{:S(2)}, u32[]{:S(2)}) collective-permute-start(f32[9,8,128]{2,1,0:T(8,128)S(1)} %get-tuple-element.68), channel_id=1, source_target_pairs={{0,1},{1,0},{2,3},{3,2},{4,8},{5,9},{6,10},{7,11},{8,4},{9,5},{10,... | collective-permute-start | bytes 110600 | tf_op jit(solution)/shard_map/ppermute | solution.py:572
  20.9 5.7 %collective-permute-start.14 = (f32[9,8,128]{2,1,0:T(8,128)S(1)}, f32[9,8,128]{2,1,0:T(8,128)S(1)}, u32[]{:S(2)}, u32[]{:S(2)}) collective-permute-start(f32[9,8,128]{2,1,0:T(8,128)S(1)} %get-tuple-element.80), channel_id=1, source_target_pairs={{0,4},{1,5},{2,6},{3,7},{4,0},{5,1},{6,2},{7,3},{8,12},{9,13},{10,... | collective-permute-start | bytes 110600 | tf_op jit(solution)/shard_map/ppermute | solution.py:573
  22.5 5.1 %collective-permute-start.15 = (f32[9,8,128]{2,1,0:T(8,128)S(1)}, f32[9,8,128]{2,1,0:T(8,128)S(1)}, u32[]{:S(2)}, u32[]{:S(2)}) collective-permute-start(f32[9,8,128]{2,1,0:T(8,128)S(1)} %get-tuple-element.81), channel_id=1, source_target_pairs={{0,1},{1,0},{2,3},{3,2},{4,8},{5,9},{6,10},{7,11},{8,4},{9,5},{10,... | collective-permute-start | bytes 110600 | tf_op jit(solution)/shard_map/ppermute | solution.py:572
  24.6 5.7 %collective-permute-start.8 = (f32[9,8,128]{2,1,0:T(8,128)S(1)}, f32[9,8,128]{2,1,0:T(8,128)S(1)}, u32[]{:S(2)}, u32[]{:S(2)}) collective-permute-start(f32[9,8,128]{2,1,0:T(8,128)S(1)} %get-tuple-element.70), channel_id=1, source_target_pairs={{0,4},{1,5},{2,6},{3,7},{4,0},{5,1},{6,2},{7,3},{8,12},{9,13},{10,... | collective-permute-start | bytes 110600 | tf_op jit(solution)/shard_map/ppermute | solution.py:573
  25.9 5.0 %collective-permute-start.9 = (f32[9,8,128]{2,1,0:T(8,128)S(1)}, f32[9,8,128]{2,1,0:T(8,128)S(1)}, u32[]{:S(2)}, u32[]{:S(2)}) collective-permute-start(f32[9,8,128]{2,1,0:T(8,128)S(1)} %get-tuple-element.71), channel_id=1, source_target_pairs={{0,1},{1,0},{2,3},{3,2},{4,8},{5,9},{6,10},{7,11},{8,4},{9,5},{10,... | collective-permute-start | bytes 110600 | tf_op jit(solution)/shard_map/ppermute | solution.py:572
  28.2 5.6 %collective-permute-start.16 = (f32[9,8,128]{2,1,0:T(8,128)S(1)}, f32[9,8,128]{2,1,0:T(8,128)S(1)}, u32[]{:S(2)}, u32[]{:S(2)}) collective-permute-start(f32[9,8,128]{2,1,0:T(8,128)S(1)} %get-tuple-element.83), channel_id=1, source_target_pairs={{0,4},{1,5},{2,6},{3,7},{4,0},{5,1},{6,2},{7,3},{8,12},{9,13},{10,... | collective-permute-start | bytes 110600 | tf_op jit(solution)/shard_map/ppermute | solution.py:573
  28.6 5.2 %collective-permute-start.17 = (f32[9,8,128]{2,1,0:T(8,128)S(1)}, f32[9,8,128]{2,1,0:T(8,128)S(1)}, u32[]{:S(2)}, u32[]{:S(2)}) collective-permute-start(f32[9,8,128]{2,1,0:T(8,128)S(1)} %get-tuple-element.84), channel_id=1, source_target_pairs={{0,1},{1,0},{2,3},{3,2},{4,8},{5,9},{6,10},{7,11},{8,4},{9,5},{10,... | collective-permute-start | bytes 110600 | tf_op jit(solution)/shard_map/ppermute | solution.py:572
  31.5 4.0 %collective-permute-start.10 = (f32[9,8,128]{2,1,0:T(8,128)S(1)}, f32[9,8,128]{2,1,0:T(8,128)S(1)}, u32[]{:S(2)}, u32[]{:S(2)}) collective-permute-start(f32[9,8,128]{2,1,0:T(8,128)S(1)} %get-tuple-element.73), channel_id=1, source_target_pairs={{0,4},{1,5},{2,6},{3,7},{4,0},{5,1},{6,2},{7,3},{8,12},{9,13},{10,... | collective-permute-start | bytes 110600 | tf_op jit(solution)/shard_map/ppermute | solution.py:573
  32.6 4.9 %collective-permute-start.11 = (f32[9,8,128]{2,1,0:T(8,128)S(1)}, f32[9,8,128]{2,1,0:T(8,128)S(1)}, u32[]{:S(2)}, u32[]{:S(2)}) collective-permute-start(f32[9,8,128]{2,1,0:T(8,128)S(1)} %get-tuple-element.74), channel_id=1, source_target_pairs={{0,1},{1,0},{2,3},{3,2},{4,8},{5,9},{6,10},{7,11},{8,4},{9,5},{10,... | collective-permute-start | bytes 110600 | tf_op jit(solution)/shard_map/ppermute | solution.py:572

commit v4 on v3

v4 whole, which is shorter than its diff:
```python
import functools

import jax
import jax.numpy as jnp
from jax import lax
from jax.experimental import pallas as pl
from jax.experimental.pallas import tpu as pltpu
from jax.sharding import PartitionSpec as P


VX, VY, VZ, WX, WY, WZ, XX, YY, ZZ, YZ, XZ, XY, PP = range(13)
PH, PK, PM, PL, PS, PB, PA, PF = range(8)
EDGE = 8


class W:
    __slots__ = ("m", "h")

    def __init__(self, m, h):
        self.m, self.h = m, h

    def __add__(self, o):
        return W(self.m + o.m, self.h + o.h)

    def __sub__(self, o):
        return W(self.m - o.m, self.h - o.h)

    def __mul__(self, o):
        if isinstance(o, W):
            return W(self.m * o.m, self.h * o.h)
        return W(self.m * o, self.h * o)

    __rmul__ = __mul__

    def __neg__(self):
        return W(-self.m, -self.h)


def roll(x, shift, axis):
    shift %= x.shape[axis]
    return pltpu.roll(x, shift, axis) if shift else x


class Tile:
    def __init__(self, planes, columns, halo):
        self.shape = (planes, columns)
        self.planes, self.columns, self.halo = planes, columns, halo
        self.lane = lax.broadcasted_iota(jnp.int32, self.shape, 1)
        sub = lax.broadcasted_iota(jnp.int32, self.shape, 0)
        self.first, self.last = self.lane == 0, self.lane == columns - 1
        self.bottom, self.top = sub == 0, sub == planes - 1
        self.zero = jnp.zeros(self.shape, jnp.float32)

    def dy(self, w):
        a, b = roll(w.m, -1, 1), roll(w.h, -1, 1)
        c, d = roll(w.m, 1, 1), roll(w.h, 1, 1)
        return W(
            jnp.where(self.last, b, a) - jnp.where(self.first, d, c),
            jnp.where(self.last, a, b) - jnp.where(self.first, c, d),
        )

    def dz1(self, a):
        return jnp.where(self.top, 0.0, roll(a, -1, 0)) - jnp.where(self.bottom, 0.0, roll(a, 1, 0))

    def dz(self, w):
        return W(self.dz1(w.m), self.dz1(w.h))

    def pack(self, tiles, reach):
        width = 2 * reach
        group = self.lane // width
        out = []
        per = self.columns // width
        for base in range(0, len(tiles), per):
            total = self.zero
            for j, tile in enumerate(tiles[base : base + per]):
                total = jnp.where(group == j, roll(tile, reach + width * j, 1), total)
            out.append(total)
        return out

    def unpack(self, tiles, index, reach):
        width = 2 * reach
        per = self.columns // width
        return roll(tiles[index // per], -(reach + width * (index % per)), 1)


def dx(get, name, r, low=True, high=True):
    if low and high:
        return get(name, r + 1) - get(name, r - 1)
    return get(name, r + 1) if high else -get(name, r - 1)


def read(ref, *at):
    planes = ref.shape[-2] // 2
    return W(ref[(*at, pl.ds(0, planes))], ref[(*at, pl.ds(planes, planes))])


def write(ref, value, *at):
    planes = ref.shape[-2] // 2
    ref[(*at, pl.ds(0, planes))] = value.m
    ref[(*at, pl.ds(planes, planes))] = value.h


def memo(fn):
    return functools.lru_cache(maxsize=None)(fn)


def momentum(tile, s, r, low=True, high=True):
    forces = [
        dx(s, XX, r, low, high) + tile.dy(s(XY, r)) + tile.dz(s(XZ, r)),
        dx(s, XY, r, low, high) + tile.dy(s(YY, r)) + tile.dz(s(YZ, r)),
        dx(s, XZ, r, low, high) + tile.dy(s(YZ, r)) + tile.dz(s(ZZ, r)),
    ]
    slopes = [dx(s, PP, r, low, high), tile.dy(s(PP, r)), tile.dz(s(PP, r))]
    return forces, slopes


def forward_edge(tile, s, v, p, r, low, high):
    forces, slopes = momentum(tile, s, r, low, high)
    h, k, m = p(PH, r), p(PK, r), p(PM, r)
    solid, fluid, pushes = [], [], []
    for i in range(3):
        w = v(WX + i, r)
        g = -(slopes[i] + m * w)
        pushes.append(g)
        solid.append(v(VX + i, r) + h * (3.0 * forces[i] - g))
        fluid.append(w + h * (k * g - forces[i]))
    sent = [s(XX, r), s(XY, r), s(XZ, r), s(PP, r)] + solid + fluid[:1]
    return sent, solid + fluid, forces + pushes


def adjoint_stress(p, a, r):
    trace = a(XX, r) + a(YY, r) + a(ZZ, r)
    b, pi = p(PB, r), a(PP, r)
    cross = p(PA, r) * b
    common = p(PL, r) * trace - cross * pi
    s = p(PS, r)
    s2 = 2.0 * s
    return {
        XX: common + s2 * a(XX, r),
        YY: common + s2 * a(YY, r),
        ZZ: common + s2 * a(ZZ, r),
        YZ: s * a(YZ, r),
        XZ: s * a(XZ, r),
        XY: s * a(XY, r),
        PP: cross * trace - b * pi,
    }


def adjoint_edge(tile, q, a, p, r, low, high):
    forces, slopes = momentum(tile, q, r, low, high)
    h, k = p(PH, r), p(PK, r)
    lv = [a(VX + i, r) - forces[i] for i in range(3)]
    lw = [a(WX + i, r) - slopes[i] for i in range(3)]
    sent = [q(XX, r), q(XY, r), q(XZ, r), q(PP, r)]
    sent += [h * (3.0 * lv[i] - lw[i]) for i in range(3)] + [h * (k * lw[0] - lv[0])]
    return sent, lv + lw


def send(tile, even, reach, first_rows, last_rows, a_ref, b_ref):
    ups = [w.m for w in first_rows] + tile.pack([w.h for w in first_rows], reach)
    downs = [w.m for w in last_rows] + tile.pack([w.h for w in last_rows], reach)
    for n, (up, down) in enumerate(zip(ups, downs)):
        a_ref[n] = jnp.where(even, down, up)
        b_ref[n] = jnp.where(even, up, down)


def receive(tile, axis, a_ref, b_ref, count, reach):
    total = a_ref.shape[0]
    at = lax.axis_index(axis)
    even = lax.rem(at, 2) == 0
    before, after = at > 0, at < lax.axis_size(axis) - 1
    first = [jnp.where(before, jnp.where(even, b_ref[n], a_ref[n]), 0.0) for n in range(total)]
    last = [jnp.where(after, jnp.where(even, a_ref[n], b_ref[n]), 0.0) for n in range(total)]
    sides = []
    for got in (first, last):
        sides.append([W(got[n], tile.unpack(got[count:], n, reach)) for n in range(count)])
    return sides


def start_kernel(halo, my_axis, inputs, outs, scratch):
    par_hbm, (mask_hbm, index_hbm, table_hbm), rest_hbm = inputs[:7], inputs[7:10], inputs[10:]
    p_ref, a_ref, b_ref, *rest = outs
    par_ref, mask_ref, index_ref, table_ref, sems = scratch
    fields_ref, cot_ref = rest[:2]
    copies = [pltpu.make_async_copy(src, par_ref.at[n], sems.at[n]) for n, src in enumerate(par_hbm)]
    for src, dst in zip((table_hbm, mask_hbm, index_hbm, *rest_hbm), (table_ref, mask_ref, index_ref, *rest)):
        copies.append(pltpu.make_async_copy(src, dst, sems.at[len(copies)]))
    for copy in copies:
        copy.start()
    for copy in copies[:10]:
        copy.wait()

    even = lax.rem(lax.axis_index(my_axis), 2) == 0
    rows = p_ref.shape[1]
    planes, columns = p_ref.shape[2], p_ref.shape[3]
    lane = lax.broadcasted_iota(jnp.int32, (planes, columns), 1)
    group = lane // halo
    per = columns // halo

    def at(r):
        return pl.ds(r, planes, stride=rows)

    for r in range(rows):
        density, fluid, mobility, lame, shear, modulus, coupling = [par_ref[n, 0, at(r), :] for n in range(7)]
        lookup = jnp.zeros((planes, columns), jnp.float32)
        index = index_ref[0, at(r), :]
        for n in range(table_ref.shape[1]):
            lookup = jnp.where(index == n, table_ref[0, n], lookup)
        p_ref[PH, r] = 0.25 / (3.0 * density - fluid)
        p_ref[PK, r] = density / fluid
        p_ref[PM, r] = 2.0 * mobility
        p_ref[PL, r] = 0.25 * lame
        p_ref[PS, r] = 0.25 * shear
        p_ref[PB, r] = 0.25 * modulus
        p_ref[PA, r] = coupling
        p_ref[PF, r] = 1.0 - mask_ref[0, at(r), :].astype(jnp.float32) * lookup
    sources = []
    for f in range(p_ref.shape[0]):
        for r in range(rows):
            sources.append(lambda f=f, r=r: p_ref[f, r])
    for ref in (fields_ref, cot_ref):
        for f in range(ref.shape[0]):
            for r in range(rows):
                sources.append(lambda ref=ref, f=f, r=r: ref[f, at(r), :])
    waited = False
    for n in range(a_ref.shape[0]):
        if (n + 1) * per > p_ref.shape[0] * rows and not waited:
            for copy in copies[10:]:
                copy.wait()
            waited = True
        left = jnp.zeros((planes, columns), jnp.float32)
        right = left
        for g in range(per):
            if n * per + g < len(sources):
                x = sources[n * per + g]()
                left = jnp.where(group == g, roll(x, halo * g, 1), left)
                right = jnp.where(group == g, roll(x, halo * g + halo, 1), right)
        a_ref[n] = jnp.where(even, right, left)
        b_ref[n] = jnp.where(even, left, right)


def inject_kernel(halo, gx_axis, gy_axis, rec_ref, cot_ref, src_ref, amp_ref, rec_out, src_out):
    for cells_ref, amounts_ref, out in ((rec_ref, cot_ref, rec_out), (src_ref, amp_ref, src_out)):
        steps, rows, planes2, columns = out.shape
        planes = planes2 // 2
        count = amounts_ref.shape[1]
        total_x, total_y = rows * lax.axis_size(gx_axis), columns * lax.axis_size(gy_axis)
        cells = cells_ref[...]
        line = lax.div(cells, jnp.full_like(cells, total_y))
        depth = lax.div(line, jnp.full_like(cells, total_x))
        col = cells - line * total_y - lax.axis_index(gy_axis) * columns
        x = line - depth * total_x - lax.axis_index(gx_axis) * rows
        row = jnp.where((x >= 0) & (x < rows), x * planes + depth, -1)
        row_at = lax.broadcasted_iota(jnp.int32, (rows * planes, count), 0)
        here = row_at == row
        lhs = jnp.concatenate([jnp.where(here, amounts_ref[t : t + 1, :], 0.0) for t in range(steps)], axis=0)
        lane = lax.broadcasted_iota(jnp.int32, (columns, count), 0)
        side = jnp.where(lane < halo, lane + columns, jnp.where(lane >= columns - halo, lane - columns, -columns))
        for half, where in enumerate((lane, side)):
            rhs = (where == col).astype(jnp.float32)
            got = lax.dot_general(
                lhs, rhs, (((1,), (1,)), ((), ())), precision=lax.Precision.HIGHEST, preferred_element_type=jnp.float32
            )
            for t in range(steps):
                for r in range(rows):
                    base = (t * rows + r) * planes
                    out[t, r, pl.ds(half * planes, planes)] = got[base : base + planes]


def spreader(halo, gy_axis, ay_ref, by_ref, rows, tile):
    at_y = lax.axis_index(gy_axis)
    even_y = lax.rem(at_y, 2) == 0
    columns = tile.columns
    per = columns // halo
    on_right = (tile.lane < halo) & (at_y < lax.axis_size(gy_axis) - 1)
    on_left = (tile.lane >= columns - halo) & (at_y > 0)

    @memo
    def packs(n):
        a, b = ay_ref[n], by_ref[n]
        return jnp.where(even_y, a, b), jnp.where(even_y, b, a)

    def side(f, r):
        n = f * rows + r
        g = n % per
        right, left = packs(n // per)
        a, b = roll(right, -halo * g, 1), roll(left, -halo * (g + 1), 1)
        return jnp.where(on_right, a, jnp.where(on_left, b, 0.0))

    return side


def place(r, depth, rows):
    if r < depth:
        return 1, r
    return (1, r - rows + 2 * depth) if r >= rows - depth else (0, r - depth)


def getter(pair, depth, rows, both=True):
    def get(f, r):
        which, at = place(r, depth, rows)
        return read(pair[which], f, at) if both else pair[which][f, at]

    return get


def putter(pair, depth, rows):
    def put(value, f, r):
        which, at = place(r, depth, rows)
        if isinstance(value, W):
            write(pair[which], value, f, at)
        else:
            pair[which][f, at] = value

    return put


STRESS = (XX, YY, ZZ, YZ, XZ, XY, PP)
SLOT = {XX: 0, XY: 1, XZ: 2, PP: 3}


def messages(tile, axis, reach, s, a, p, rows, a_msg, b_msg, part_f, part_g, part_a, with_params):
    even = lax.rem(lax.axis_index(axis), 2) == 0
    qs = memo(lambda r: adjoint_stress(p, a, r))
    q = lambda f, r: qs(r)[f]
    sides = []
    for n, (r, low, high) in enumerate(((0, False, True), (rows - 1, True, False))):
        got, new, drives = forward_edge(tile, s, s, p, r, low, high)
        more, lam = adjoint_edge(tile, q, a, p, r, low, high)
        for m in range(6):
            write(part_f, new[m], m, n)
            part_g[m, n] = drives[m].m
            write(part_a, lam[m], m, n)
        sides.append(got + more + ([p(PH, r), p(PK, r)] if with_params else []))
    send(tile, even, reach, *sides, a_msg, b_msg)


def spread_kernel(halo, gx_axis, gy_axis, fields_ref, cot_ref, pm_ref, ay_ref, by_ref, rec_ref, p_out, *outs):
    rows, planes, columns = pm_ref.shape[1:]
    tile = Tile(planes, columns, halo)
    side = spreader(halo, gy_axis, ay_ref, by_ref, rows, tile)
    base, count = p_out.shape[0], fields_ref.shape[0]
    for f in range(base):
        for r in range(rows):
            write(p_out, W(pm_ref[f, r], side(f, r)), f, r)
    put_f, put_a = putter(outs[0:2], 2, rows), putter(outs[2:4], 2, rows)
    for f in range(count):
        for r in range(rows):
            at = pl.ds(r, planes, stride=rows)
            put_f(W(fields_ref[f, at, :], side(base + f, r)), f, r)
            value = W(cot_ref[f, at, :], side(base + count + f, r))
            if f == PP:
                value = value + read(rec_ref, rec_ref.shape[0] - 1, r)
            put_a(value * read(p_out, PF, r), f, r)
    p = lambda f, r: read(p_out, f, r)
    messages(tile, gx_axis, halo, getter(outs[0:2], 2, rows), getter(outs[2:4], 2, rows), p, rows, *outs[4:], True)


def sums(ff, aa):
    fo, pu, wo, ee, gg, w_ = ff[0:3], ff[3:6], ff[6:9], ff[9:12], ff[12:15], ff[15]
    af, ag, sg, pi = aa[0:3], aa[3:6], aa[6:12], aa[12]
    tr, dd = sg[0] + sg[1] + sg[2], ee[0] + ee[1] + ee[2]
    dot = lambda x, y: x[0] * y[0] + x[1] * y[1] + x[2] * y[2]
    return [
        dot(af, fo), dot(ag, pu), dot(af, pu), dot(ag, wo),
        tr * dd, tr * w_, 2.0 * dot(sg[0:3], ee) + dot(sg[3:6], gg), pi * dd, pi * w_,
    ]


def saved_forward(refs, rows):
    vel, strain = getter(refs[0:2], 1, rows, False), getter(refs[2:4], 2, rows, False)
    return lambda r: [vel(n, r) for n in range(9)] + [strain(n, r) for n in range(7)]


def saved_adjoint(refs, rows):
    cot = getter(refs[0:2], 1, rows, False)
    return lambda r: [cot(n, r) for n in range(6)] + [refs[2][n, r] for n in range(7)]


def sums_kernel(rows, *refs):
    out, pairs = refs[-1], refs[:-1]
    for r in range(rows):
        acc = [0.0] * 9
        for n in range(0, len(pairs), 7):
            ff, aa = saved_forward(pairs[n : n + 4], rows), saved_adjoint(pairs[n + 4 : n + 7], rows)
            acc = [x + y for x, y in zip(acc, sums(ff(r), aa(r)))]
        for n, x in enumerate(acc):
            out[n, r] = x


def gradients(acc, p, r):
    a1, a2, a3, a4, b1, b2, b3, b4, b5 = acc
    h, k, b, al = [p(n, r).m for n in (PH, PK, PB, PA)]
    h4 = 4.0 * h
    return [
        h4 * (a3 - 3.0 * a1),
        h4 * (a1 + a2 - k * (3.0 * a2 + a3)),
        -2.0 * a4,
        0.25 * b1,
        0.25 * b3,
        0.25 * (al * (b2 - b4) - b5),
        b * (b2 - b4),
    ]


def strains(tile, v, r):
    e = [dx(v, VX, r), tile.dy(v(VY, r)), tile.dz(v(VZ, r))]
    g = [
        tile.dz(v(VY, r)) + tile.dy(v(VZ, r)),
        tile.dz(v(VX, r)) + dx(v, VZ, r),
        tile.dy(v(VX, r)) + dx(v, VY, r),
    ]
    return e, g, dx(v, WX, r) + tile.dy(v(WY, r)) + tile.dz(v(WZ, r))


def new_fields(p, old, v, e, g, dw, source, r):
    dv = e[0] + e[1] + e[2]
    sh, b = p(PS, r), p(PB, r)
    ab = p(PA, r) * b
    common = p(PL, r) * dv + ab * dw
    new = {f: v(f, r) for f in range(6)}
    for i in range(3):
        new[XX + i] = old(XX + i, r) + (common + 2.0 * (sh * e[i]))
        new[YZ + i] = old(YZ + i, r) + sh * g[i]
    new[PP] = old(PP, r) - (ab * dv + b * dw) + source
    factor = p(PF, r)
    return {f: value * factor for f, value in new.items()}


def back_fields(tile, lam, c, vel, r):
    out = dict(vel)
    out[XX] = lam(XX, r) - dx(c, 0, r)
    out[YY] = lam(YY, r) - tile.dy(c(1, r))
    out[ZZ] = lam(ZZ, r) - tile.dz(c(2, r))
    out[YZ] = lam(YZ, r) - (tile.dz(c(1, r)) + tile.dy(c(2, r)))
    out[XZ] = lam(XZ, r) - (tile.dz(c(0, r)) + dx(c, 2, r))
    out[XY] = lam(XY, r) - (tile.dy(c(0, r)) + dx(c, 1, r))
    out[PP] = lam(PP, r) + (dx(c, 3, r) + tile.dy(c(4, r)) + tile.dz(c(5, r)))
    return out


def push_cots(p, r, lv, lw):
    h, k, m = p(PH, r), p(PK, r), p(PM, r)
    cf = [h * (3.0 * lv[i] - lw[i]) for i in range(3)]
    cg = [h * (k * lw[i] - lv[i]) for i in range(3)]
    vel = {VX + i: lv[i] for i in range(3)} | {WX + i: lw[i] - m * cg[i] for i in range(3)}
    return cf + cg, vel


def near(rows):
    return (1, 2, rows - 3, rows - 2)


def interior_kernel(halo, j, steps, *refs):
    refs = list(refs)
    take = lambda n: [refs.pop(0) for _ in range(n)]
    final = j == steps - 1
    f_pair, a_pair, (p_ref,) = take(2), take(2), take(1)
    if final:
        old_f, old_a, (acc_ref,) = take(4), take(3), take(1)
        grad_out, par_out, vel_near = take(3)
    else:
        src_ref, rec_ref, f_out, a_out, save_vel, save_str, save_cot, save_sig = take(8)
    v_near, c_near, l_near = take(3)
    assert not refs
    rows, planes, columns = p_ref.shape[1], p_ref.shape[2] // 2, p_ref.shape[3]
    tile = Tile(planes, columns, halo)
    p = lambda f, r: read(p_ref, f, r)
    old, lam = getter(f_pair, 2, rows), getter(a_pair, 2, rows)

    @memo
    def velocity(r):
        _, new, drives = forward_edge(tile, old, old, p, r, True, True)
        return new, [x.m for x in drives] + [old(WX + i, r).m for i in range(3)]

    qs = memo(lambda r: adjoint_stress(p, lam, r))
    q = lambda f, r: qs(r)[f]

    @memo
    def cots(r):
        forces, slopes = momentum(tile, q, r)
        return push_cots(
            p, r, [lam(VX + i, r) - forces[i] for i in range(3)], [lam(WX + i, r) - slopes[i] for i in range(3)]
        )

    v = lambda f, r: velocity(r)[0][f]
    c = lambda i, r: cots(r)[0][i]
    for r in range(1, rows - 1):
        if r in near(rows):
            at = near(rows).index(r)
            for n in range(6):
                write(v_near, v(n, r), n, at)
                write(c_near, c(n, r), n, at)
                write(l_near, cots(r)[1][n], n, at)
        inner = 2 <= r < rows - 2
        if not final:
            for n, x in enumerate(velocity(r)[1]):
                save_vel[n, r - 1] = x
            for n in range(6):
                save_cot[n, r - 1] = c(n, r).m
        elif not inner:
            for n, x in enumerate(velocity(r)[1]):
                vel_near[n, 0 if r == 1 else 1] = x
        if not inner:
            continue
        e, g, dw = strains(tile, v, r)
        strain = [x.m for x in e + g] + [dw.m]
        back = back_fields(tile, lam, c, cots(r)[1], r)
        if final:
            ff = velocity(r)[1] + strain
            aa = [c(n, r).m for n in range(6)] + [lam(f, r).m for f in STRESS]
            one = sums(ff, saved_adjoint(old_a, rows)(r))
            two = sums(saved_forward(old_f, rows)(r), aa)
            acc = [acc_ref[n, r] + (x + y) for n, (x, y) in enumerate(zip(one, two))]
            for n, x in enumerate(gradients(acc, p, r)):
                par_out[n, r - 2] = x
            for f, value in back.items():
                grad_out[f, r - 2] = value.m
            continue
        for n, x in enumerate(strain):
            save_str[n, r - 2] = x
        for f, value in new_fields(p, old, v, e, g, dw, read(src_ref, j, r), r).items():
            write(f_out, value, f, r - 2)
        back[PP] = back[PP] + read(rec_ref, steps - 2 - j, r)
        for f, value in back.items():
            write(a_out, value * p(PF, r), f, r - 2)
    if not final:
        for r in range(rows):
            for n, f in enumerate(STRESS):
                save_sig[n, r] = lam(f, r).m


def edge_kernel(gx_axis, halo, j, steps, *refs):
    refs = list(refs)
    take = lambda n: [refs.pop(0) for _ in range(n)]
    first, final = j == 0, j == steps - 1
    f_ref, a_ref, p_ref, am_ref, bm_ref, part_f, part_g, part_a, v_near, c_near, l_near = take(11)
    if not first:
        (hk_ref,) = take(1)
    if final:
        old_f, old_a, (acc_ref, grad_mid, par_mid, vel_near, grad_out, par_out) = take(4), take(3), take(6)
    else:
        src_ref, rec_ref, f_out, a_out, save_vel, save_str, save_cot = take(7)
        outs = take(5)
    if first:
        (hk_out,) = take(1)
    assert not refs
    rows, planes, columns = p_ref.shape[1], p_ref.shape[2] // 2, p_ref.shape[3]
    tile = Tile(planes, columns, halo)
    sides = receive(tile, gx_axis, am_ref, bm_ref, 2 * EDGE + (2 if first else 0), halo - 2 * j)
    p = lambda f, r: read(p_ref, f, r)
    old, lam = getter((None, f_ref), 2, rows), getter((None, a_ref), 2, rows)
    hk = []
    for n in range(2):
        if first:
            pair = sides[n][2 * EDGE :]
            for m in range(2):
                write(hk_out, pair[m], n, m)
        else:
            pair = [read(hk_ref, n, m) for m in range(2)]
        hk.append(pair)

    def add_forward(base, h, k, values):
        xx, xy, xz, pp = [h * x for x in values]
        adds = [3.0 * xx + pp, 3.0 * xy, 3.0 * xz, -(k * pp + xx), -xy, -xz]
        return [x + y for x, y in zip(base, adds)]

    velocities, drives, cots, vels = {}, {}, {}, {}
    qs = memo(lambda r: adjoint_stress(p, lam, r))
    for n, r, out in ((0, 0, -1), (1, rows - 1, rows)):
        h, k = p(PH, r), p(PK, r)
        near_s, near_v = sides[n][0:4], sides[n][4:8]
        velocities[r] = add_forward([read(part_f, m, n) for m in range(6)], -h if n == 0 else h, k, near_s)
        own = [old(f, r) for f in SLOT]
        h2, k2 = hk[n]
        velocities[out] = add_forward(near_v, h2 if n == 0 else -h2, k2, own)
        sign = -1.0 if n == 0 else 1.0
        xx, xy, xz, pp = [sign * x.m for x in near_s]
        part = [part_g[m, n] for m in range(6)]
        drives[r] = [part[0] + xx, part[1] + xy, part[2] + xz, part[3] - pp, part[4], part[5]]
        drives[r] += [old(WX + i, r).m for i in range(3)]
        near_q, near_c = sides[n][EDGE : EDGE + 4], sides[n][EDGE + 4 : EDGE + 8]
        base = [read(part_a, m, n) for m in range(6)]
        for m in range(4):
            base[m] = base[m] - sign * near_q[m]
        cots[r], vels[r] = push_cots(p, r, base[0:3], base[3:6])
        t = -h2 if n == 0 else h2
        xx, xy, xz, pp = [t * qs(r)[f] for f in SLOT]
        cots[out] = [near_c[0] + (3.0 * xx - pp), near_c[1] + 3.0 * xy, near_c[2] + 3.0 * xz, near_c[3] + (k2 * pp - xx)]
    for at, r in enumerate(near(rows)):
        velocities[r] = [read(v_near, n, at) for n in range(6)]
        cots[r] = [read(c_near, n, at) for n in range(6)]
        vels[r] = {n: read(l_near, n, at) for n in range(6)}
    v = lambda f, r: velocities[r][f]
    c = lambda i, r: cots[r][i]
    new_f, new_a = {}, {}
    for r in (0, rows - 1, 1, rows - 2):
        e, g, dw = strains(tile, v, r)
        strain = [x.m for x in e + g] + [dw.m]
        back = back_fields(tile, lam, c, vels[r], r)
        at = place(r, 2, rows)[1]
        outer = r in (0, rows - 1)
        side = 0 if r < 2 else 1
        if final:
            drive = drives[r] if outer else [vel_near[n, side] for n in range(9)]
            aa = [c(n, r).m for n in range(6)] + [lam(f, r).m for f in STRESS]
            one = sums(drive + strain, saved_adjoint(old_a, rows)(r))
            two = sums(saved_forward(old_f, rows)(r), aa)
            acc = [acc_ref[n, r] + (x + y) for n, (x, y) in enumerate(zip(one, two))]
            for n, x in enumerate(gradients(acc, p, r)):
                par_out[n, pl.ds(r, planes, stride=rows), :] = x
            for f, value in back.items():
                grad_out[f, pl.ds(r, planes, stride=rows), :] = value.m
            continue
        if outer:
            for n, x in enumerate(drives[r]):
                save_vel[n, side] = x
            for n in range(6):
                save_cot[n, side] = c(n, r).m
        for n, x in enumerate(strain):
            save_str[n, at] = x
        new_f[r] = new_fields(p, old, v, e, g, dw, read(src_ref, j, r), r)
        back[PP] = back[PP] + read(rec_ref, steps - 2 - j, r)
        new_a[r] = {f: value * p(PF, r) for f, value in back.items()}
        for f in range(f_out.shape[0]):
            write(f_out, new_f[r][f], f, at)
            write(a_out, new_a[r][f], f, at)
    if final:
        for r in range(2, rows - 2):
            for n in range(par_mid.shape[0]):
                par_out[n, pl.ds(r, planes, stride=rows), :] = par_mid[n, r - 2]
            for f in range(grad_mid.shape[0]):
                grad_out[f, pl.ds(r, planes, stride=rows), :] = grad_mid[f, r - 2]
        return
    messages(
        tile, gx_axis, halo - 2 * (j + 1), getter((None, f_out), 2, rows), getter((None, a_out), 2, rows), p, rows, *outs, False
    )


def swaps(axis, odd):
    nx, ny = lax.axis_size("gx"), lax.axis_size("gy")
    count, other = (nx, ny) if axis == "gx" else (ny, nx)
    place = (lambda i, k: i * ny + k) if axis == "gx" else (lambda i, k: k * ny + i)
    out, met = [], set()
    for i in range(odd, count - 1, 2):
        met |= {i, i + 1}
        for k in range(other):
            out += [(place(i, k), place(i + 1, k)), (place(i + 1, k), place(i, k))]
    for i in set(range(count)) - met:
        for k in range(0, other - 1, 2):
            out += [(place(i, k), place(i, k + 1)), (place(i, k + 1), place(i, k))]
    return sorted(out)


def exchange(axis, a, b):
    mesh = ("gx", "gy")
    b = lax.ppermute(b, mesh, swaps(axis, 1))
    a = lax.ppermute(a, mesh, swaps(axis, 0))
    return a, b


def call(kernel, outs, *args):
    shapes = [o if isinstance(o, jax.ShapeDtypeStruct) else jax.ShapeDtypeStruct(o, jnp.float32) for o in outs]
    return pl.pallas_call(
        kernel,
        out_shape=shapes,
        in_specs=[pl.BlockSpec(memory_space=pltpu.VMEM)] * len(args),
        out_specs=[pl.BlockSpec(memory_space=pltpu.VMEM)] * len(outs),
        compiler_params=pltpu.CompilerParams(vmem_limit_bytes=48 << 20),
    )(*args)


def per_device(
    fields, density, fluid_density, mobility, lame_lambda, shear_modulus, biot_modulus, biot_coef,
    region_mask, profile_index, profile_table, source_cells, source_amp, receiver_cells, field_cot, receiver_cot,
):
    planes, rows, columns = region_mask.shape
    steps = source_amp.shape[0]
    count = fields.shape[0]
    halo = 2 * steps
    assert steps > 2 and planes == 8 and columns == 128 and columns % (2 * halo) == 0 and rows > 1
    flat = lambda x: x.reshape(-1, planes * rows, columns)
    fields, field_cot = flat(fields), flat(field_cot)
    raw = [flat(x) for x in (density, fluid_density, mobility, lame_lambda, shear_modulus, biot_modulus, biot_coef)]
    packs = -(-(2 * count + 8) * rows * halo // columns)
    own, wide = (rows, planes, columns), (rows, 2 * planes, columns)

    table = profile_table[None]
    small = [receiver_cells[None], receiver_cot, source_cells[None], source_amp]
    inputs = [*raw, table, flat(region_mask), flat(profile_index), fields, field_cot, *small]
    whole = [fields, field_cot, *small]
    plane = (planes * rows, columns)

    def start(*refs):
        refs = list(refs)
        hbm = refs[:7] + refs[8:10] + refs[7:8] + refs[10:16]
        start_kernel(halo, "gy", hbm, refs[16:25], refs[25:])

    p_own, ay, by, fields, field_cot, *small = pl.pallas_call(
        start,
        out_shape=[jax.ShapeDtypeStruct(s, jnp.float32) for s in [(8, *own)] + [(packs, planes, columns)] * 2]
        + [jax.ShapeDtypeStruct(x.shape, x.dtype) for x in whole],
        in_specs=[pl.BlockSpec(memory_space=pltpu.HBM)] * 16,
        out_specs=[pl.BlockSpec(memory_space=pltpu.VMEM)] * 9,
        scratch_shapes=[
            pltpu.VMEM((7, 1, *plane), jnp.float32), pltpu.VMEM((1, *plane), jnp.int32),
            pltpu.VMEM((1, *plane), jnp.int32), pltpu.SMEM(table.shape, jnp.float32),
            pltpu.SemaphoreType.DMA((16,)),
        ],
        compiler_params=pltpu.CompilerParams(vmem_limit_bytes=48 << 20),
    )(*[pltpu.with_memory_space_constraint(x, pltpu.HBM) for x in inputs])
    ay, by = exchange("gy", ay, by)
    rec, src = call(functools.partial(inject_kernel, halo, "gx", "gy"), [(steps, *wide)] * 2, *small)
    def tiles(n, reach):
        return n + -(-n // (columns // (2 * reach))), planes, columns

    assert rows >= 6
    part = lambda k, r, shape: (k, r, *shape[1:])
    w, m = wide, own
    parts = [part(6, 2, w), part(6, 2, m), part(6, 2, w)]
    mid, end = part(count, rows - 4, w), part(count, 4, w)
    p, fm, fe, am, ae, ma, mb, *part_refs = call(
        functools.partial(spread_kernel, halo, "gx", "gy"),
        [(8, *wide), mid, end, mid, end] + [tiles(2 * EDGE + 2, halo)] * 2 + parts,
        fields, field_cot, p_own, ay, by, rec,
    )
    saved_f, saved_a, hk, acc = [], [], [], []
    nears = [part(6, 4, w)] * 3
    for j in range(steps - 1):
        ma, mb = exchange("gx", ma, mb)
        outs = [mid, mid, part(9, rows - 2, m), part(7, rows - 4, m), part(6, rows - 2, m), (7, *own)] + nears
        nfm, nam, vel, strain, cot, sig, *near_refs = call(
            functools.partial(interior_kernel, halo, j, steps), outs, fm, fe, am, ae, p, src, rec
        )
        outs = [end, end, part(9, 2, m), part(7, 4, m), part(6, 2, m)] + [tiles(2 * EDGE, halo - 2 * (j + 1))] * 2 + parts
        outs += [] if j else [(2, 2, 2 * planes, columns)]
        fe, ae, vel2, strain2, cot2, ma, mb, *rest = call(
            functools.partial(edge_kernel, "gx", halo, j, steps), outs,
            fe, ae, p, ma, mb, *part_refs, *near_refs, *hk, src, rec,
        )
        fm, am, part_refs = nfm, nam, rest[:3]
        hk = hk or rest[3:]
        saved_f.append([vel, vel2, strain, strain2])
        saved_a.append([cot, cot2, sig])
    ma, mb = exchange("gx", ma, mb)
    middle = [x for t in range(1, steps - 1) for x in saved_f[t] + saved_a[steps - 1 - t]]
    (acc,) = call(functools.partial(sums_kernel, rows), [(9, *own)], *middle)
    outs = [part(count, rows - 4, m), part(7, rows - 4, m), part(9, 2, m)] + nears
    grad_mid, par_mid, vel_near, *near_refs = call(
        functools.partial(interior_kernel, halo, steps - 1, steps), outs, fm, fe, am, ae, p, *saved_f[0], *saved_a[0], acc
    )
    grad, par = call(
        functools.partial(edge_kernel, "gx", halo, steps - 1, steps), [(count, *plane), (7, *plane)],
        fe, ae, p, ma, mb, *part_refs, *near_refs, *hk, *saved_f[0], *saved_a[0], acc, grad_mid, par_mid, vel_near,
    )
    return grad.reshape(count, planes, rows, columns), par.reshape(7, planes, rows, columns)


def solution(mesh):
    plane, field = P(None, "gx", "gy"), P(None, None, "gx", "gy")
    in_specs = (field,) + (plane,) * 9 + (P(),) * 4 + (field, P())
    return jax.shard_map(per_device, mesh=mesh, in_specs=in_specs, out_specs=(field, field), check_vma=False)
```

time: 38.9 us -> 36.6 us (0.941)
  starting transfers between devices: 19.4 us -> 9.51 us
  waiting for transfers between devices: 8.64 us -> 17.3 us
  Pallas kernels: 10 us -> 8.97 us
    ppermute x9 -> x5, waiting for transfers between devices: 1.14 us -> 8.4 us  [exchange(): a = lax.ppermute(a, mesh, swaps(axis, 0))]
    ppermute x9 -> x5, starting transfers between devices: 9.95 us -> 4.82 us  [exchange(): a = lax.ppermute(a, mesh, swaps(axis, 0))]
    ppermute x9 -> x5, starting transfers between devices: 9.46 us -> 4.69 us  [exchange(): b = lax.ppermute(b, mesh, swaps(axis, 1))]
    ppermute x9 -> x5, waiting for transfers between devices: 7.5 us -> 8.86 us  [exchange(): b = lax.ppermute(b, mesh, swaps(axis, 1))]
    pallas_call x12 -> x11, Pallas kernels: 8.05 us -> 7.02 us  [call(): pl.pallas_call(kernel, out_shape=shapes, in_specs=[pl.BlockSpec(memory_sp...]
  transfers between devices with their start and end apart: 18 -> 10, of which waited for: 8 -> 9; matrix products, arithmetic and copies ran while one was open for 0% -> 0% of each run, Pallas kernels for 16% -> 10%
where the time goes in v4:
time: 36.6 us; the launch traced here: 36.5 us
  waiting for transfers between devices  17.3 us (47%)
  starting transfers between devices  9.51 us (26%)
  Pallas kernels  8.97 us (25%)
  between operations  0.72 us (2%)
    ppermute x5, waiting for transfers between devices, exchange(): b = lax.ppermute(b, mesh, swaps(axis, 1))  8.86 us
    ppermute x5, waiting for transfers between devices, exchange(): a = lax.ppermute(a, mesh, swaps(axis, 0))  8.4 us
    pallas_call x11, Pallas kernels, call(): pl.pallas_call(kernel, out_shape=shapes, in_specs=[pl.BlockSpec(memory_sp...  7.02 us
    ppermute x5, starting transfers between devices, exchange(): a = lax.ppermute(a, mesh, swaps(axis, 0))  4.82 us
    ppermute x5, starting transfers between devices, exchange(): b = lax.ppermute(b, mesh, swaps(axis, 1))  4.69 us
    pallas_call x1, Pallas kernels, per_device(): pl.pallas_call(start, out_shape=[jax.ShapeDtypeStruct(s, jnp.float32) for...  1.95 us
  transfers between devices with their start and end apart: 10, of which 9 were waited for; matrix products, arithmetic and copies ran while one was open for 0% of the time, Pallas kernels for 10%

profile of v4, /device:TPU:16, one launch (start us, length us, event | category | flops | bytes accessed | tf_op | source)
XLA Modules:
  0.0 36.5 jit_solution(17833160193854336676)
XLA Ops:
  0.6 1.9 %shard_map.167 = (f32[8,8,8,128]{3,2,1,0:T(8,128)S(1)}, f32[17,8,128]{2,1,0:T(8,128)S(1)}, f32[17,8,128]{2,1,0:T(8,128)S(1)}, f32[13,64,128]{2,1,0:T(8,128)S(1)}...) custom-call(f32[1,64,128]{2,1,0:T(8,128)} %bitcast.18, ...), custom_call_target="tpu_custom_call" | custom-call | tf_op jit(solution)/shard_map/pallas_call | solution.py:699
  2.6 0.1 collective-permute-start
  2.7 1.6 %collective-permute-start.1 = (f32[17,8,128]{2,1,0:T(8,128)S(1)}, f32[17,8,128]{2,1,0:T(8,128)S(1)}, u32[]{:S(2)}, u32[]{:S(2)}) collective-permute-start(f32[17,8,128]{2,1,0:T(8,128)S(1)} %get-tuple-element.93), channel_id=1, source_target_pairs={{0,4},{1,2},{2,1},{3,7},{4,0},{5,6},{6,5},{7,3},{8,12},{9,10},{10,... | collective-permute-start | bytes 208904 | tf_op jit(solution)/shard_map/ppermute | solution.py:657
  4.2 1.2 %shard_map.168 = (f32[4,8,16,128]{3,2,1,0:T(8,128)S(1)}, f32[4,8,16,128]{3,2,1,0:T(8,128)S(1)}) custom-call(s32[1,512]{1,0:T(1,128)S(1)} %get-tuple-element.94.rec_ref, f32[4,512]{1,0:T(4,128)S(1)} %get-tuple-element.95.cot_ref, s32[1,64]{1,0:T(1,128)S(1)} %get-tuple-element.96.src_ref, f32[4,64]{1,0:T(4,128)S(1)} %get-tuple-element.97.amp_ref), custom_call_target="tpu_custom_call" | custom-call | tf_op jit(solution)/shard_map/pallas_call | solution.py:664
  5.4 0.0 collective-permute-done.ay_ref
  5.4 1.6 %collective-permute-done.1.by_ref = f32[17,8,128]{2,1,0:T(8,128)S(1)} collective-permute-done((f32[17,8,128]{2,1,0:T(8,128)S(1)}, f32[17,8,128]{2,1,0:T(8,128)S(1)}, u32[]{:S(2)}, u32[]{:S(2)}) %collective-permute-start.1) | collective-permute-done | bytes 69664 | tf_op jit(solution)/shard_map/ppermute | solution.py:657
  7.0 0.8 %shard_map.169 = (f32[8,8,16,128]{3,2,1,0:T(8,128)S(1)}, f32[13,4,16,128]{3,2,1,0:T(8,128)S(1)}, f32[13,4,16,128]{3,2,1,0:T(8,128)S(1)}, f32[13,4,16,128]{3,2,1,...) custom-call(f32[13,64,128]{2,1,0:T(8,128)S(1)} %get-tuple-element.89, ...), custom_call_target="tpu_custom_call" | custom-call | tf_op jit(solution)/shard_map/pallas_call | solution.py:664
  7.9 1.6 %collective-permute-start.2 = (f32[21,8,128]{2,1,0:T(8,128)S(1)}, f32[21,8,128]{2,1,0:T(8,128)S(1)}, u32[]{:S(2)}, u32[]{:S(2)}) collective-permute-start(f32[21,8,128]{2,1,0:T(8,128)S(1)} %get-tuple-element.102), channel_id=1, source_target_pairs={{0,4},{1,5},{2,6},{3,7},{4,0},{5,1},{6,2},{7,3},{8,12},{9,13},{10,... | collective-permute-start | bytes 258056 | tf_op jit(solution)/shard_map/ppermute | solution.py:658
  9.4 0.4 %collective-permute-start.3 = (f32[21,8,128]{2,1,0:T(8,128)S(1)}, f32[21,8,128]{2,1,0:T(8,128)S(1)}, u32[]{:S(2)}, u32[]{:S(2)}) collective-permute-start(f32[21,8,128]{2,1,0:T(8,128)S(1)} %get-tuple-element.103), channel_id=1, source_target_pairs={{0,1},{1,0},{2,3},{3,2},{4,8},{5,9},{6,10},{7,11},{8,4},{9,5},{10,... | collective-permute-start | bytes 258056 | tf_op jit(solution)/shard_map/ppermute | solution.py:657
  9.8 0.6 %shard_map.170 = (f32[13,4,16,128]{3,2,1,0:T(8,128)S(1)}, f32[13,4,16,128]{3,2,1,0:T(8,128)S(1)}, f32[9,6,8,128]{3,2,1,0:T(8,128)S(1)}, f32[7,4,8,128]{3,2,1,0:T...) custom-call(f32[13,4,16,128]{3,2,1,0:T(8,128)S(1)} %get-tuple-elemen, ...), custom_call_target="tpu_custom_call" | custom-call | tf_op jit(solution)/shard_map/pallas_call | solution.py:664
  10.4 3.0 %collective-permute-done.2.refs_3_ = f32[21,8,128]{2,1,0:T(8,128)S(1)} collective-permute-done((f32[21,8,128]{2,1,0:T(8,128)S(1)}, f32[21,8,128]{2,1,0:T(8,128)S(1)}, u32[]{:S(2)}, u32[]{:S(2)}) %collective-permute-start.2) | collective-permute-done | bytes 86048 | tf_op jit(solution)/shard_map/ppermute | solution.py:658
  13.4 1.4 %collective-permute-done.3.refs_4_ = f32[21,8,128]{2,1,0:T(8,128)S(1)} collective-permute-done((f32[21,8,128]{2,1,0:T(8,128)S(1)}, f32[21,8,128]{2,1,0:T(8,128)S(1)}, u32[]{:S(2)}, u32[]{:S(2)}) %collective-permute-start.3) | collective-permute-done | bytes 86048 | tf_op jit(solution)/shard_map/ppermute | solution.py:657
  14.8 0.5 %shard_map.171 = (f32[13,4,16,128]{3,2,1,0:T(8,128)S(1)}, f32[13,4,16,128]{3,2,1,0:T(8,128)S(1)}, f32[9,2,8,128]{3,2,1,0:T(8,128)S(1)}, f32[7,4,8,128]{3,2,1,0:T...) custom-call(f32[13,4,16,128]{3,2,1,0:T(8,128)S(1)} %get-tuple-elemen, ...), custom_call_target="tpu_custom_call" | custom-call | tf_op jit(solution)/shard_map/pallas_call | solution.py:664
  15.3 1.1 %collective-permute-start.4 = (f32[18,8,128]{2,1,0:T(8,128)S(1)}, f32[18,8,128]{2,1,0:T(8,128)S(1)}, u32[]{:S(2)}, u32[]{:S(2)}) collective-permute-start(f32[18,8,128]{2,1,0:T(8,128)S(1)} %get-tuple-element.115), channel_id=1, source_target_pairs={{0,4},{1,5},{2,6},{3,7},{4,0},{5,1},{6,2},{7,3},{8,12},{9,13},{10,... | collective-permute-start | bytes 221192 | tf_op jit(solution)/shard_map/ppermute | solution.py:658
  16.4 0.9 %collective-permute-start.5 = (f32[18,8,128]{2,1,0:T(8,128)S(1)}, f32[18,8,128]{2,1,0:T(8,128)S(1)}, u32[]{:S(2)}, u32[]{:S(2)}) collective-permute-start(f32[18,8,128]{2,1,0:T(8,128)S(1)} %get-tuple-element.116), channel_id=1, source_target_pairs={{0,1},{1,0},{2,3},{3,2},{4,8},{5,9},{6,10},{7,11},{8,4},{9,5},{10,... | collective-permute-start | bytes 221192 | tf_op jit(solution)/shard_map/ppermute | solution.py:657
  17.3 0.6 %shard_map.172 = (f32[13,4,16,128]{3,2,1,0:T(8,128)S(1)}, f32[13,4,16,128]{3,2,1,0:T(8,128)S(1)}, f32[9,6,8,128]{3,2,1,0:T(8,128)S(1)}, f32[7,4,8,128]{3,2,1,0:T...) custom-call(f32[13,4,16,128]{3,2,1,0:T(8,128)S(1)} %get-tuple-elemen, ...), custom_call_target="tpu_custom_call" | custom-call | tf_op jit(solution)/shard_map/pallas_call | solution.py:664
  17.9 1.9 %collective-permute-done.4.refs_3_ = f32[18,8,128]{2,1,0:T(8,128)S(1)} collective-permute-done((f32[18,8,128]{2,1,0:T(8,128)S(1)}, f32[18,8,128]{2,1,0:T(8,128)S(1)}, u32[]{:S(2)}, u32[]{:S(2)}) %collective-permute-start.4) | collective-permute-done | bytes 73760 | tf_op jit(solution)/shard_map/ppermute | solution.py:658
  19.7 1.9 %collective-permute-done.5.refs_4_ = f32[18,8,128]{2,1,0:T(8,128)S(1)} collective-permute-done((f32[18,8,128]{2,1,0:T(8,128)S(1)}, f32[18,8,128]{2,1,0:T(8,128)S(1)}, u32[]{:S(2)}, u32[]{:S(2)}) %collective-permute-start.5) | collective-permute-done | bytes 73760 | tf_op jit(solution)/shard_map/ppermute | solution.py:657
  21.7 0.5 %shard_map.173 = (f32[13,4,16,128]{3,2,1,0:T(8,128)S(1)}, f32[13,4,16,128]{3,2,1,0:T(8,128)S(1)}, f32[9,2,8,128]{3,2,1,0:T(8,128)S(1)}, f32[7,4,8,128]{3,2,1,0:T...) custom-call(f32[13,4,16,128]{3,2,1,0:T(8,128)S(1)} %get-tuple-elemen, ...), custom_call_target="tpu_custom_call" | custom-call | tf_op jit(solution)/shard_map/pallas_call | solution.py:664
  22.1 1.1 %collective-permute-start.6 = (f32[17,8,128]{2,1,0:T(8,128)S(1)}, f32[17,8,128]{2,1,0:T(8,128)S(1)}, u32[]{:S(2)}, u32[]{:S(2)}) collective-permute-start(f32[17,8,128]{2,1,0:T(8,128)S(1)} %get-tuple-element.128), channel_id=1, source_target_pairs={{0,4},{1,5},{2,6},{3,7},{4,0},{5,1},{6,2},{7,3},{8,12},{9,13},{10,... | collective-permute-start | bytes 208904 | tf_op jit(solution)/shard_map/ppermute | solution.py:658
  23.2 0.9 %collective-permute-start.7 = (f32[17,8,128]{2,1,0:T(8,128)S(1)}, f32[17,8,128]{2,1,0:T(8,128)S(1)}, u32[]{:S(2)}, u32[]{:S(2)}) collective-permute-start(f32[17,8,128]{2,1,0:T(8,128)S(1)} %get-tuple-element.129), channel_id=1, source_target_pairs={{0,1},{1,0},{2,3},{3,2},{4,8},{5,9},{6,10},{7,11},{8,4},{9,5},{10,... | collective-permute-start | bytes 208904 | tf_op jit(solution)/shard_map/ppermute | solution.py:657
  24.1 0.5 %shard_map.174 = (f32[13,4,16,128]{3,2,1,0:T(8,128)S(1)}, f32[13,4,16,128]{3,2,1,0:T(8,128)S(1)}, f32[9,6,8,128]{3,2,1,0:T(8,128)S(1)}, f32[7,4,8,128]{3,2,1,0:T...) custom-call(f32[13,4,16,128]{3,2,1,0:T(8,128)S(1)} %get-tuple-elemen, ...), custom_call_target="tpu_custom_call" | custom-call | tf_op jit(solution)/shard_map/pallas_call | solution.py:664
  24.7 1.8 %collective-permute-done.6.refs_3_ = f32[17,8,128]{2,1,0:T(8,128)S(1)} collective-permute-done((f32[17,8,128]{2,1,0:T(8,128)S(1)}, f32[17,8,128]{2,1,0:T(8,128)S(1)}, u32[]{:S(2)}, u32[]{:S(2)}) %collective-permute-start.6) | collective-permute-done | bytes 69664 | tf_op jit(solution)/shard_map/ppermute | solution.py:658
  26.5 2.0 %collective-permute-done.7.refs_4_ = f32[17,8,128]{2,1,0:T(8,128)S(1)} collective-permute-done((f32[17,8,128]{2,1,0:T(8,128)S(1)}, f32[17,8,128]{2,1,0:T(8,128)S(1)}, u32[]{:S(2)}, u32[]{:S(2)}) %collective-permute-start.7) | collective-permute-done | bytes 69664 | tf_op jit(solution)/shard_map/ppermute | solution.py:657
  28.5 0.5 %shard_map.175 = (f32[13,4,16,128]{3,2,1,0:T(8,128)S(1)}, f32[13,4,16,128]{3,2,1,0:T(8,128)S(1)}, f32[9,2,8,128]{3,2,1,0:T(8,128)S(1)}, f32[7,4,8,128]{3,2,1,0:T...) custom-call(f32[13,4,16,128]{3,2,1,0:T(8,128)S(1)} %get-tuple-elemen, ...), custom_call_target="tpu_custom_call" | custom-call | tf_op jit(solution)/shard_map/pallas_call | solution.py:664
  29.0 1.0 %collective-permute-start.8 = (f32[17,8,128]{2,1,0:T(8,128)S(1)}, f32[17,8,128]{2,1,0:T(8,128)S(1)}, u32[]{:S(2)}, u32[]{:S(2)}) collective-permute-start(f32[17,8,128]{2,1,0:T(8,128)S(1)} %get-tuple-element.140), channel_id=1, source_target_pairs={{0,4},{1,5},{2,6},{3,7},{4,0},{5,1},{6,2},{7,3},{8,12},{9,13},{10,... | collective-permute-start | bytes 208904 | tf_op jit(solution)/shard_map/ppermute | solution.py:658
  30.1 0.9 %collective-permute-start.9 = (f32[17,8,128]{2,1,0:T(8,128)S(1)}, f32[17,8,128]{2,1,0:T(8,128)S(1)}, u32[]{:S(2)}, u32[]{:S(2)}) collective-permute-start(f32[17,8,128]{2,1,0:T(8,128)S(1)} %get-tuple-element.141), channel_id=1, source_target_pairs={{0,1},{1,0},{2,3},{3,2},{4,8},{5,9},{6,10},{7,11},{8,4},{9,5},{10,... | collective-permute-start | bytes 208904 | tf_op jit(solution)/shard_map/ppermute | solution.py:657
  31.0 0.2 shard_map.176.refs_12_.refs_19_
  31.1 0.5 %shard_map.177 = (f32[13,4,8,128]{3,2,1,0:T(8,128)S(1)}, f32[7,4,8,128]{3,2,1,0:T(8,128)S(1)}, f32[9,2,8,128]{3,2,1,0:T(8,128)S(1)}, f32[6,4,16,128]{3,2,1,0:T(8...) custom-call(f32[13,4,16,128]{3,2,1,0:T(8,128)S(1)} %get-tuple-element.145.refs_0_, ...), custom_call_target="tpu_custom_call" | custom-call | tf_op jit(solution)/shard_map/pallas_call | solution.py:664
  31.7 1.7 %collective-permute-done.8.refs_3_ = f32[17,8,128]{2,1,0:T(8,128)S(1)} collective-permute-done((f32[17,8,128]{2,1,0:T(8,128)S(1)}, f32[17,8,128]{2,1,0:T(8,128)S(1)}, u32[]{:S(2)}, u32[]{:S(2)}) %collective-permute-start.8) | collective-permute-done | bytes 69664 | tf_op jit(solution)/shard_map/ppermute | solution.py:658
  33.4 1.9 %collective-permute-done.9.refs_4_ = f32[17,8,128]{2,1,0:T(8,128)S(1)} collective-permute-done((f32[17,8,128]{2,1,0:T(8,128)S(1)}, f32[17,8,128]{2,1,0:T(8,128)S(1)}, u32[]{:S(2)}, u32[]{:S(2)}) %collective-permute-start.9) | collective-permute-done | bytes 69664 | tf_op jit(solution)/shard_map/ppermute | solution.py:657
  35.3 1.2 %shard_map.178 = (f32[13,64,128]{2,1,0:T(8,128)}, f32[7,64,128]{2,1,0:T(8,128)}) custom-call(f32[13,4,16,128]{3,2,1,0:T(8,128)S(1)} %get-tuple-element.138.refs_1_.refs_0_, f32[13,4,16,128]{3,2,1,0:T(8,128)S(1)} %get-tuple-element.139.refs_3_.refs_1_, f32[8,8,16,128]{3,2,1,0:T(8,128)S(1)} %get-tuple-element.101.refs_4_.refs_2_, ...), custom_call_target="tpu_custom_call" | custom-call | tf_op jit(solution)/shard_map/pallas_call | solution.py:664
Async XLA Ops:
  2.6 2.8 %collective-permute-start = (f32[17,8,128]{2,1,0:T(8,128)S(1)}, f32[17,8,128]{2,1,0:T(8,128)S(1)}, u32[]{:S(2)}, u32[]{:S(2)}) collective-permute-start(f32[17,8,128]{2,1,0:T(8,128)S(1)} %get-tuple-element.92), channel_id=1, source_target_pairs={{0,1},{1,0},{2,3},{3,2},{4,5},{5,4},{6,7},{7,6},{8,9},{9,8},{10,11... | collective-permute-start | bytes 208904 | tf_op jit(solution)/shard_map/ppermute | solution.py:658
  2.7 4.4 %collective-permute-start.1 = (f32[17,8,128]{2,1,0:T(8,128)S(1)}, f32[17,8,128]{2,1,0:T(8,128)S(1)}, u32[]{:S(2)}, u32[]{:S(2)}) collective-permute-start(f32[17,8,128]{2,1,0:T(8,128)S(1)} %get-tuple-element.93), channel_id=1, source_target_pairs={{0,4},{1,2},{2,1},{3,7},{4,0},{5,6},{6,5},{7,3},{8,12},{9,10},{10,... | collective-permute-start | bytes 208904 | tf_op jit(solution)/shard_map/ppermute | solution.py:657
  7.9 5.5 %collective-permute-start.2 = (f32[21,8,128]{2,1,0:T(8,128)S(1)}, f32[21,8,128]{2,1,0:T(8,128)S(1)}, u32[]{:S(2)}, u32[]{:S(2)}) collective-permute-start(f32[21,8,128]{2,1,0:T(8,128)S(1)} %get-tuple-element.102), channel_id=1, source_target_pairs={{0,4},{1,5},{2,6},{3,7},{4,0},{5,1},{6,2},{7,3},{8,12},{9,13},{10,... | collective-permute-start | bytes 258056 | tf_op jit(solution)/shard_map/ppermute | solution.py:658
  9.4 5.4 %collective-permute-start.3 = (f32[21,8,128]{2,1,0:T(8,128)S(1)}, f32[21,8,128]{2,1,0:T(8,128)S(1)}, u32[]{:S(2)}, u32[]{:S(2)}) collective-permute-start(f32[21,8,128]{2,1,0:T(8,128)S(1)} %get-tuple-element.103), channel_id=1, source_target_pairs={{0,1},{1,0},{2,3},{3,2},{4,8},{5,9},{6,10},{7,11},{8,4},{9,5},{10,... | collective-permute-start | bytes 258056 | tf_op jit(solution)/shard_map/ppermute | solution.py:657
  15.3 4.4 %collective-permute-start.4 = (f32[18,8,128]{2,1,0:T(8,128)S(1)}, f32[18,8,128]{2,1,0:T(8,128)S(1)}, u32[]{:S(2)}, u32[]{:S(2)}) collective-permute-start(f32[18,8,128]{2,1,0:T(8,128)S(1)} %get-tuple-element.115), channel_id=1, source_target_pairs={{0,4},{1,5},{2,6},{3,7},{4,0},{5,1},{6,2},{7,3},{8,12},{9,13},{10,... | collective-permute-start | bytes 221192 | tf_op jit(solution)/shard_map/ppermute | solution.py:658
  16.4 5.3 %collective-permute-start.5 = (f32[18,8,128]{2,1,0:T(8,128)S(1)}, f32[18,8,128]{2,1,0:T(8,128)S(1)}, u32[]{:S(2)}, u32[]{:S(2)}) collective-permute-start(f32[18,8,128]{2,1,0:T(8,128)S(1)} %get-tuple-element.116), channel_id=1, source_target_pairs={{0,1},{1,0},{2,3},{3,2},{4,8},{5,9},{6,10},{7,11},{8,4},{9,5},{10,... | collective-permute-start | bytes 221192 | tf_op jit(solution)/shard_map/ppermute | solution.py:657
  22.1 4.4 %collective-permute-start.6 = (f32[17,8,128]{2,1,0:T(8,128)S(1)}, f32[17,8,128]{2,1,0:T(8,128)S(1)}, u32[]{:S(2)}, u32[]{:S(2)}) collective-permute-start(f32[17,8,128]{2,1,0:T(8,128)S(1)} %get-tuple-element.128), channel_id=1, source_target_pairs={{0,4},{1,5},{2,6},{3,7},{4,0},{5,1},{6,2},{7,3},{8,12},{9,13},{10,... | collective-permute-start | bytes 208904 | tf_op jit(solution)/shard_map/ppermute | solution.py:658
  23.2 5.3 %collective-permute-start.7 = (f32[17,8,128]{2,1,0:T(8,128)S(1)}, f32[17,8,128]{2,1,0:T(8,128)S(1)}, u32[]{:S(2)}, u32[]{:S(2)}) collective-permute-start(f32[17,8,128]{2,1,0:T(8,128)S(1)} %get-tuple-element.129), channel_id=1, source_target_pairs={{0,1},{1,0},{2,3},{3,2},{4,8},{5,9},{6,10},{7,11},{8,4},{9,5},{10,... | collective-permute-start | bytes 208904 | tf_op jit(solution)/shard_map/ppermute | solution.py:657
  29.0 4.4 %collective-permute-start.8 = (f32[17,8,128]{2,1,0:T(8,128)S(1)}, f32[17,8,128]{2,1,0:T(8,128)S(1)}, u32[]{:S(2)}, u32[]{:S(2)}) collective-permute-start(f32[17,8,128]{2,1,0:T(8,128)S(1)} %get-tuple-element.140), channel_id=1, source_target_pairs={{0,4},{1,5},{2,6},{3,7},{4,0},{5,1},{6,2},{7,3},{8,12},{9,13},{10,... | collective-permute-start | bytes 208904 | tf_op jit(solution)/shard_map/ppermute | solution.py:658
  30.1 5.2 %collective-permute-start.9 = (f32[17,8,128]{2,1,0:T(8,128)S(1)}, f32[17,8,128]{2,1,0:T(8,128)S(1)}, u32[]{:S(2)}, u32[]{:S(2)}) collective-permute-start(f32[17,8,128]{2,1,0:T(8,128)S(1)} %get-tuple-element.141), channel_id=1, source_target_pairs={{0,1},{1,0},{2,3},{3,2},{4,8},{5,9},{6,10},{7,11},{8,4},{9,5},{10,... | collective-permute-start | bytes 208904 | tf_op jit(solution)/shard_map/ppermute | solution.py:657

commit v5 on v4

--- a/solution.py
+++ b/solution.py
@@ -42,7 +42,8 @@
 
 
 class Tile:
-    def __init__(self, planes, columns, halo):
+    def __init__(self, planes, columns, halo, flip=None):
+        self.flip = flip
         self.shape = (planes, columns)
         self.planes, self.columns, self.halo = planes, columns, halo
         self.lane = lax.broadcasted_iota(jnp.int32, self.shape, 1)
@@ -50,6 +51,13 @@
         self.first, self.last = self.lane == 0, self.lane == columns - 1
         self.bottom, self.top = sub == 0, sub == planes - 1
         self.zero = jnp.zeros(self.shape, jnp.float32)
+
+    def dx(self, get, name, r, low=True, high=True):
+        if low and high:
+            d = get(name, r + 1) - get(name, r - 1)
+        else:
+            d = get(name, r + 1) if high else -get(name, r - 1)
+        return d if self.flip is None else self.flip * d
 
     def dy(self, w):
         a, b = roll(w.m, -1, 1), roll(w.h, -1, 1)
@@ -83,12 +91,6 @@
         return roll(tiles[index // per], -(reach + width * (index % per)), 1)
 
 
-def dx(get, name, r, low=True, high=True):
-    if low and high:
-        return get(name, r + 1) - get(name, r - 1)
-    return get(name, r + 1) if high else -get(name, r - 1)
-
-
 def read(ref, *at):
     planes = ref.shape[-2] // 2
     return W(ref[(*at, pl.ds(0, planes))], ref[(*at, pl.ds(planes, planes))])
@@ -106,11 +108,11 @@
 
 def momentum(tile, s, r, low=True, high=True):
     forces = [
-        dx(s, XX, r, low, high) + tile.dy(s(XY, r)) + tile.dz(s(XZ, r)),
-        dx(s, XY, r, low, high) + tile.dy(s(YY, r)) + tile.dz(s(YZ, r)),
-        dx(s, XZ, r, low, high) + tile.dy(s(YZ, r)) + tile.dz(s(ZZ, r)),
+        tile.dx(s, XX, r, low, high) + tile.dy(s(XY, r)) + tile.dz(s(XZ, r)),
+        tile.dx(s, XY, r, low, high) + tile.dy(s(YY, r)) + tile.dz(s(YZ, r)),
+        tile.dx(s, XZ, r, low, high) + tile.dy(s(YZ, r)) + tile.dz(s(ZZ, r)),
     ]
-    slopes = [dx(s, PP, r, low, high), tile.dy(s(PP, r)), tile.dz(s(PP, r))]
+    slopes = [tile.dx(s, PP, r, low, high), tile.dy(s(PP, r)), tile.dz(s(PP, r))]
     return forces, slopes
 
 
@@ -156,25 +158,25 @@
     return sent, lv + lw
 
 
-def send(tile, even, reach, first_rows, last_rows, a_ref, b_ref):
-    ups = [w.m for w in first_rows] + tile.pack([w.h for w in first_rows], reach)
-    downs = [w.m for w in last_rows] + tile.pack([w.h for w in last_rows], reach)
-    for n, (up, down) in enumerate(zip(ups, downs)):
-        a_ref[n] = jnp.where(even, down, up)
-        b_ref[n] = jnp.where(even, up, down)
-
-
-def receive(tile, axis, a_ref, b_ref, count, reach):
-    total = a_ref.shape[0]
-    at = lax.axis_index(axis)
-    even = lax.rem(at, 2) == 0
-    before, after = at > 0, at < lax.axis_size(axis) - 1
-    first = [jnp.where(before, jnp.where(even, b_ref[n], a_ref[n]), 0.0) for n in range(total)]
-    last = [jnp.where(after, jnp.where(even, a_ref[n], b_ref[n]), 0.0) for n in range(total)]
-    sides = []
-    for got in (first, last):
-        sides.append([W(got[n], tile.unpack(got[count:], n, reach)) for n in range(count)])
-    return sides
+class Side:
+    def __init__(self, axis, swap, rows):
+        at, size = lax.axis_index(axis), lax.axis_size(axis)
+        self.last = lax.rem(at, 2) == swap
+        self.met = jnp.where(self.last, at < size - 1, at > 0)
+        self.base = jnp.where(self.last, rows - 1, 0)
+        self.step = jnp.where(self.last, -1, 1)
+        self.flip = jnp.where(self.last, -1.0, 1.0)
+
+    def row(self, r):
+        return self.base + self.step * r
+
+    def near(self, r):
+        return jnp.where(self.last, 4 - r, r - 1)
+
+
+def receive(tile, side, msg, count, reach):
+    tiles = [jnp.where(side.met, msg[n], 0.0) for n in range(msg.shape[0])]
+    return [W(tiles[n], tile.unpack(tiles[count:], n, reach)) for n in range(count)]
 
 
 def start_kernel(halo, my_axis, inputs, outs, scratch):
@@ -290,52 +292,42 @@
     return side
 
 
-def place(r, depth, rows):
-    if r < depth:
-        return 1, r
-    return (1, r - rows + 2 * depth) if r >= rows - depth else (0, r - depth)
-
-
-def getter(pair, depth, rows, both=True):
-    def get(f, r):
-        which, at = place(r, depth, rows)
-        return read(pair[which], f, at) if both else pair[which][f, at]
-
-    return get
-
-
-def putter(pair, depth, rows):
-    def put(value, f, r):
-        which, at = place(r, depth, rows)
-        if isinstance(value, W):
-            write(pair[which], value, f, at)
-        else:
-            pair[which][f, at] = value
-
-    return put
-
-
 STRESS = (XX, YY, ZZ, YZ, XZ, XY, PP)
 SLOT = {XX: 0, XY: 1, XZ: 2, PP: 3}
 
 
-def messages(tile, axis, reach, s, a, p, rows, a_msg, b_msg, part_f, part_g, part_a, with_params):
-    even = lax.rem(lax.axis_index(axis), 2) == 0
+def whole(mid, ends, axis, rows):
+    last = lax.rem(lax.axis_index(axis), 2) == 0
+
+    @memo
+    def get(f, r):
+        if 2 <= r < rows - 2:
+            return read(mid, f, r - 2)
+        top = r >= rows - 2
+        at = rows - 1 - r if top else r
+        a, b = read(ends[0], f, at), read(ends[1], f, at)
+        if not top:
+            a, b = b, a
+        return W(jnp.where(last, a.m, b.m), jnp.where(last, a.h, b.h))
+
+    return get
+
+
+def message(tile, side, reach, s, a, p, msg, part_f, part_g, part_a, with_params):
     qs = memo(lambda r: adjoint_stress(p, a, r))
     q = lambda f, r: qs(r)[f]
-    sides = []
-    for n, (r, low, high) in enumerate(((0, False, True), (rows - 1, True, False))):
-        got, new, drives = forward_edge(tile, s, s, p, r, low, high)
-        more, lam = adjoint_edge(tile, q, a, p, r, low, high)
-        for m in range(6):
-            write(part_f, new[m], m, n)
-            part_g[m, n] = drives[m].m
-            write(part_a, lam[m], m, n)
-        sides.append(got + more + ([p(PH, r), p(PK, r)] if with_params else []))
-    send(tile, even, reach, *sides, a_msg, b_msg)
-
-
-def spread_kernel(halo, gx_axis, gy_axis, fields_ref, cot_ref, pm_ref, ay_ref, by_ref, rec_ref, p_out, *outs):
+    got, new, drives = forward_edge(tile, s, s, p, 0, False, True)
+    more, lam = adjoint_edge(tile, q, a, p, 0, False, True)
+    for m in range(6):
+        write(part_f, new[m], m)
+        part_g[m] = drives[m].m
+        write(part_a, lam[m], m)
+    got = got + more + ([p(PH, 0), p(PK, 0)] if with_params else [])
+    for n, x in enumerate([w.m for w in got] + tile.pack([w.h for w in got], reach)):
+        msg[n] = x
+
+
+def spread_kernel(halo, gx_axis, gy_axis, fields_ref, cot_ref, pm_ref, ay_ref, by_ref, rec_ref, p_out, f_mid, a_mid, *outs):
     rows, planes, columns = pm_ref.shape[1:]
     tile = Tile(planes, columns, halo)
     side = spreader(halo, gy_axis, ay_ref, by_ref, rows, tile)
@@ -343,17 +335,31 @@
     for f in range(base):
         for r in range(rows):
             write(p_out, W(pm_ref[f, r], side(f, r)), f, r)
-    put_f, put_a = putter(outs[0:2], 2, rows), putter(outs[2:4], 2, rows)
+    ends = [Side(gx_axis, swap, rows) for swap in (0, 1)]
+    groups = outs[:6], outs[6:]
     for f in range(count):
-        for r in range(rows):
-            at = pl.ds(r, planes, stride=rows)
-            put_f(W(fields_ref[f, at, :], side(base + f, r)), f, r)
-            value = W(cot_ref[f, at, :], side(base + count + f, r))
-            if f == PP:
-                value = value + read(rec_ref, rec_ref.shape[0] - 1, r)
-            put_a(value * read(p_out, PF, r), f, r)
-    p = lambda f, r: read(p_out, f, r)
-    messages(tile, gx_axis, halo, getter(outs[0:2], 2, rows), getter(outs[2:4], 2, rows), p, rows, *outs[4:], True)
+        for which, mid in enumerate((f_mid, a_mid)):
+            values = []
+            for r in range(rows):
+                at = pl.ds(r, planes, stride=rows)
+                if which:
+                    value = W(cot_ref[f, at, :], side(base + count + f, r))
+                    if f == PP:
+                        value = value + read(rec_ref, rec_ref.shape[0] - 1, r)
+                    values.append(value * read(p_out, PF, r))
+                else:
+                    values.append(W(fields_ref[f, at, :], side(base + f, r)))
+            for r in range(2, rows - 2):
+                write(mid, values[r], f, r - 2)
+            for end, group in zip(ends, groups):
+                for r in range(2):
+                    x, y = values[rows - 1 - r], values[r]
+                    write(group[which], W(jnp.where(end.last, x.m, y.m), jnp.where(end.last, x.h, y.h)), f, r)
+    for end, group in zip(ends, groups):
+        local = Tile(planes, columns, halo, end.flip)
+        s, a = (lambda f, r, ref=ref: read(ref, f, r) for ref in group[:2])
+        p = lambda f, r, end=end: read(p_out, f, end.row(r))
+        message(local, end, halo, s, a, p, *group[2:], True)
 
 
 def sums(ff, aa):
@@ -367,25 +373,42 @@
     ]
 
 
-def saved_forward(refs, rows):
-    vel, strain = getter(refs[0:2], 1, rows, False), getter(refs[2:4], 2, rows, False)
-    return lambda r: [vel(n, r) for n in range(9)] + [strain(n, r) for n in range(7)]
-
-
-def saved_adjoint(refs, rows):
-    cot = getter(refs[0:2], 1, rows, False)
-    return lambda r: [cot(n, r) for n in range(6)] + [refs[2][n, r] for n in range(7)]
-
-
-def sums_kernel(rows, *refs):
-    out, pairs = refs[-1], refs[:-1]
-    for r in range(rows):
+def kept_rows(refs, rows, r):
+    vel, strain, cot, sig = refs
+    return (
+        [vel[n, r - 1] for n in range(9)] + [strain[n, r - 2] for n in range(7)],
+        [cot[n, r - 1] for n in range(6)] + [sig[n, r] for n in range(7)],
+    )
+
+
+def kept_end(refs, end_refs, side, r):
+    vel, _, cot, sig = refs
+    vel_end, strain_end, cot_end = end_refs
+    at = side.row(r)
+    first, third = (vel_end, cot_end) if r == 0 else (vel, cot)
+    where = (lambda n, ref: ref[n]) if r == 0 else (lambda n, ref: ref[n, at - 1])
+    return (
+        [where(n, first) for n in range(9)] + [strain_end[n, r] for n in range(7)],
+        [where(n, third) for n in range(6)] + [sig[n, at] for n in range(7)],
+    )
+
+
+def sums_kernel(axis, rows, count, *refs):
+    out_mid, out_a, out_b = refs[-3:]
+    pairs = [(refs[n : n + 10], refs[n + 10 : n + 20]) for n in range(0, 20 * count, 20)]
+    def total(pick):
         acc = [0.0] * 9
-        for n in range(0, len(pairs), 7):
-            ff, aa = saved_forward(pairs[n : n + 4], rows), saved_adjoint(pairs[n + 4 : n + 7], rows)
-            acc = [x + y for x, y in zip(acc, sums(ff(r), aa(r)))]
-        for n, x in enumerate(acc):
-            out[n, r] = x
+        for fwd, adj in pairs:
+            acc = [x + y for x, y in zip(acc, sums(pick(fwd)[0], pick(adj)[1]))]
+        return acc
+    for r in range(2, rows - 2):
+        for n, x in enumerate(total(lambda refs: kept_rows(refs[:4], rows, r))):
+            out_mid[n, r - 2] = x
+    for swap, out in enumerate((out_a, out_b)):
+        side = Side(axis, swap, rows)
+        for r in range(2):
+            for n, x in enumerate(total(lambda refs: kept_end(refs[:4], refs[4 + 3 * swap : 7 + 3 * swap], side, r))):
+                out[n, r] = x
 
 
 def gradients(acc, p, r):
@@ -404,13 +427,13 @@
 
 
 def strains(tile, v, r):
-    e = [dx(v, VX, r), tile.dy(v(VY, r)), tile.dz(v(VZ, r))]
+    e = [tile.dx(v, VX, r), tile.dy(v(VY, r)), tile.dz(v(VZ, r))]
     g = [
         tile.dz(v(VY, r)) + tile.dy(v(VZ, r)),
-        tile.dz(v(VX, r)) + dx(v, VZ, r),
-        tile.dy(v(VX, r)) + dx(v, VY, r),
+        tile.dz(v(VX, r)) + tile.dx(v, VZ, r),
+        tile.dy(v(VX, r)) + tile.dx(v, VY, r),
     ]
-    return e, g, dx(v, WX, r) + tile.dy(v(WY, r)) + tile.dz(v(WZ, r))
+    return e, g, tile.dx(v, WX, r) + tile.dy(v(WY, r)) + tile.dz(v(WZ, r))
 
 
 def new_fields(p, old, v, e, g, dw, source, r):
@@ -429,13 +452,13 @@
 
 def back_fields(tile, lam, c, vel, r):
     out = dict(vel)
-    out[XX] = lam(XX, r) - dx(c, 0, r)
+    out[XX] = lam(XX, r) - tile.dx(c, 0, r)
     out[YY] = lam(YY, r) - tile.dy(c(1, r))
     out[ZZ] = lam(ZZ, r) - tile.dz(c(2, r))
     out[YZ] = lam(YZ, r) - (tile.dz(c(1, r)) + tile.dy(c(2, r)))
-    out[XZ] = lam(XZ, r) - (tile.dz(c(0, r)) + dx(c, 2, r))
-    out[XY] = lam(XY, r) - (tile.dy(c(0, r)) + dx(c, 1, r))
-    out[PP] = lam(PP, r) + (dx(c, 3, r) + tile.dy(c(4, r)) + tile.dz(c(5, r)))
+    out[XZ] = lam(XZ, r) - (tile.dz(c(0, r)) + tile.dx(c, 2, r))
+    out[XY] = lam(XY, r) - (tile.dy(c(0, r)) + tile.dx(c, 1, r))
+    out[PP] = lam(PP, r) + (tile.dx(c, 3, r) + tile.dy(c(4, r)) + tile.dz(c(5, r)))
     return out
 
 
@@ -451,22 +474,23 @@
     return (1, 2, rows - 3, rows - 2)
 
 
-def interior_kernel(halo, j, steps, *refs):
+def interior_kernel(gx_axis, halo, j, steps, *refs):
     refs = list(refs)
     take = lambda n: [refs.pop(0) for _ in range(n)]
     final = j == steps - 1
-    f_pair, a_pair, (p_ref,) = take(2), take(2), take(1)
+    f_mid, fa, fb, a_mid, aa, ab, p_ref = take(7)
     if final:
-        old_f, old_a, (acc_ref,) = take(4), take(3), take(1)
-        grad_out, par_out, vel_near = take(3)
+        kept, (acc_ref,) = take(4), take(1)
+        grad_out, par_out = take(2)
     else:
-        src_ref, rec_ref, f_out, a_out, save_vel, save_str, save_cot, save_sig = take(8)
+        src_ref, rec_ref, f_out, a_out = take(4)
+    save_vel, save_str, save_cot, save_sig = take(4)
     v_near, c_near, l_near = take(3)
     assert not refs
     rows, planes, columns = p_ref.shape[1], p_ref.shape[2] // 2, p_ref.shape[3]
     tile = Tile(planes, columns, halo)
     p = lambda f, r: read(p_ref, f, r)
-    old, lam = getter(f_pair, 2, rows), getter(a_pair, 2, rows)
+    old, lam = whole(f_mid, (fa, fb), gx_axis, rows), whole(a_mid, (aa, ab), gx_axis, rows)
 
     @memo
     def velocity(r):
@@ -492,26 +516,20 @@
                 write(v_near, v(n, r), n, at)
                 write(c_near, c(n, r), n, at)
                 write(l_near, cots(r)[1][n], n, at)
-        inner = 2 <= r < rows - 2
-        if not final:
-            for n, x in enumerate(velocity(r)[1]):
-                save_vel[n, r - 1] = x
-            for n in range(6):
-                save_cot[n, r - 1] = c(n, r).m
-        elif not inner:
-            for n, x in enumerate(velocity(r)[1]):
-                vel_near[n, 0 if r == 1 else 1] = x
-        if not inner:
+        for n, x in enumerate(velocity(r)[1]):
+            save_vel[n, r - 1] = x
+        for n in range(6):
+            save_cot[n, r - 1] = c(n, r).m
+        if not 2 <= r < rows - 2:
             continue
         e, g, dw = strains(tile, v, r)
         strain = [x.m for x in e + g] + [dw.m]
         back = back_fields(tile, lam, c, cots(r)[1], r)
         if final:
             ff = velocity(r)[1] + strain
-            aa = [c(n, r).m for n in range(6)] + [lam(f, r).m for f in STRESS]
-            one = sums(ff, saved_adjoint(old_a, rows)(r))
-            two = sums(saved_forward(old_f, rows)(r), aa)
-            acc = [acc_ref[n, r] + (x + y) for n, (x, y) in enumerate(zip(one, two))]
+            cc = [c(n, r).m for n in range(6)] + [lam(f, r).m for f in STRESS]
+            kept_f, kept_a = kept_rows(kept, rows, r)
+            acc = [acc_ref[n, r - 2] + (x + y) for n, (x, y) in enumerate(zip(sums(ff, kept_a), sums(kept_f, cc)))]
             for n, x in enumerate(gradients(acc, p, r)):
                 par_out[n, r - 2] = x
             for f, value in back.items():
@@ -524,117 +542,113 @@
         back[PP] = back[PP] + read(rec_ref, steps - 2 - j, r)
         for f, value in back.items():
             write(a_out, value * p(PF, r), f, r - 2)
-    if not final:
-        for r in range(rows):
-            for n, f in enumerate(STRESS):
-                save_sig[n, r] = lam(f, r).m
-
-
-def edge_kernel(gx_axis, halo, j, steps, *refs):
+    for r in range(rows):
+        for n, f in enumerate(STRESS):
+            save_sig[n, r] = lam(f, r).m
+
+
+def end_kernel(gx_axis, swap, halo, j, steps, *refs):
     refs = list(refs)
     take = lambda n: [refs.pop(0) for _ in range(n)]
     first, final = j == 0, j == steps - 1
-    f_ref, a_ref, p_ref, am_ref, bm_ref, part_f, part_g, part_a, v_near, c_near, l_near = take(11)
+    f_ref, a_ref, p_ref, msg_ref, part_f, part_g, part_a, v_near, c_near, l_near = take(10)
     if not first:
         (hk_ref,) = take(1)
     if final:
-        old_f, old_a, (acc_ref, grad_mid, par_mid, vel_near, grad_out, par_out) = take(4), take(3), take(6)
+        kept, kept_ends, (acc_ref, now_vel) = take(4), take(3), take(2)
+        if swap:
+            grad_mid, par_mid, grad_other, par_other = take(4)
+        grad_out, par_out = take(2)
     else:
         src_ref, rec_ref, f_out, a_out, save_vel, save_str, save_cot = take(7)
-        outs = take(5)
+        outs = take(4)
     if first:
         (hk_out,) = take(1)
     assert not refs
     rows, planes, columns = p_ref.shape[1], p_ref.shape[2] // 2, p_ref.shape[3]
-    tile = Tile(planes, columns, halo)
-    sides = receive(tile, gx_axis, am_ref, bm_ref, 2 * EDGE + (2 if first else 0), halo - 2 * j)
-    p = lambda f, r: read(p_ref, f, r)
-    old, lam = getter((None, f_ref), 2, rows), getter((None, a_ref), 2, rows)
-    hk = []
-    for n in range(2):
-        if first:
-            pair = sides[n][2 * EDGE :]
-            for m in range(2):
-                write(hk_out, pair[m], n, m)
-        else:
-            pair = [read(hk_ref, n, m) for m in range(2)]
-        hk.append(pair)
+    side = Side(gx_axis, swap, rows)
+    tile = Tile(planes, columns, halo, side.flip)
+    got = receive(tile, side, msg_ref, 2 * EDGE + (2 if first else 0), halo - 2 * j)
+    p = lambda f, r: read(p_ref, f, side.row(r))
+    old, lam = (lambda f, r: read(f_ref, f, r)), (lambda f, r: read(a_ref, f, r))
+    if first:
+        h2, k2 = got[2 * EDGE :]
+        write(hk_out, h2, 0)
+        write(hk_out, k2, 1)
+    else:
+        h2, k2 = read(hk_ref, 0), read(hk_ref, 1)
 
     def add_forward(base, h, k, values):
         xx, xy, xz, pp = [h * x for x in values]
         adds = [3.0 * xx + pp, 3.0 * xy, 3.0 * xz, -(k * pp + xx), -xy, -xz]
         return [x + y for x, y in zip(base, adds)]
 
-    velocities, drives, cots, vels = {}, {}, {}, {}
     qs = memo(lambda r: adjoint_stress(p, lam, r))
-    for n, r, out in ((0, 0, -1), (1, rows - 1, rows)):
-        h, k = p(PH, r), p(PK, r)
-        near_s, near_v = sides[n][0:4], sides[n][4:8]
-        velocities[r] = add_forward([read(part_f, m, n) for m in range(6)], -h if n == 0 else h, k, near_s)
-        own = [old(f, r) for f in SLOT]
-        h2, k2 = hk[n]
-        velocities[out] = add_forward(near_v, h2 if n == 0 else -h2, k2, own)
-        sign = -1.0 if n == 0 else 1.0
-        xx, xy, xz, pp = [sign * x.m for x in near_s]
-        part = [part_g[m, n] for m in range(6)]
-        drives[r] = [part[0] + xx, part[1] + xy, part[2] + xz, part[3] - pp, part[4], part[5]]
-        drives[r] += [old(WX + i, r).m for i in range(3)]
-        near_q, near_c = sides[n][EDGE : EDGE + 4], sides[n][EDGE + 4 : EDGE + 8]
-        base = [read(part_a, m, n) for m in range(6)]
-        for m in range(4):
-            base[m] = base[m] - sign * near_q[m]
-        cots[r], vels[r] = push_cots(p, r, base[0:3], base[3:6])
-        t = -h2 if n == 0 else h2
-        xx, xy, xz, pp = [t * qs(r)[f] for f in SLOT]
-        cots[out] = [near_c[0] + (3.0 * xx - pp), near_c[1] + 3.0 * xy, near_c[2] + 3.0 * xz, near_c[3] + (k2 * pp - xx)]
-    for at, r in enumerate(near(rows)):
+    near_s, near_v, near_q, near_c = [got[n : n + 4] for n in range(0, 16, 4)]
+    velocities, cots, vels = {}, {}, {}
+    sign = -side.flip
+    velocities[0] = add_forward([read(part_f, m) for m in range(6)], p(PH, 0) * sign, p(PK, 0), near_s)
+    velocities[-1] = add_forward(near_v, h2 * side.flip, k2, [old(f, 0) for f in SLOT])
+    xx, xy, xz, pp = [x.m * sign for x in near_s]
+    drives = [part_g[0] + xx, part_g[1] + xy, part_g[2] + xz, part_g[3] - pp, part_g[4], part_g[5]]
+    drives += [old(WX + i, 0).m for i in range(3)]
+    base = [read(part_a, m) for m in range(6)]
+    for m in range(4):
+        base[m] = base[m] - near_q[m] * sign
+    cots[0], vels[0] = push_cots(p, 0, base[0:3], base[3:6])
+    t = h2 * sign
+    xx, xy, xz, pp = [t * qs(0)[f] for f in SLOT]
+    cots[-1] = [near_c[0] + (3.0 * xx - pp), near_c[1] + 3.0 * xy, near_c[2] + 3.0 * xz, near_c[3] + (k2 * pp - xx)]
+    for r in (1, 2):
+        at = side.near(r)
         velocities[r] = [read(v_near, n, at) for n in range(6)]
         cots[r] = [read(c_near, n, at) for n in range(6)]
         vels[r] = {n: read(l_near, n, at) for n in range(6)}
     v = lambda f, r: velocities[r][f]
     c = lambda i, r: cots[r][i]
-    new_f, new_a = {}, {}
-    for r in (0, rows - 1, 1, rows - 2):
+    finals = []
+    for r in range(2):
         e, g, dw = strains(tile, v, r)
         strain = [x.m for x in e + g] + [dw.m]
         back = back_fields(tile, lam, c, vels[r], r)
-        at = place(r, 2, rows)[1]
-        outer = r in (0, rows - 1)
-        side = 0 if r < 2 else 1
         if final:
-            drive = drives[r] if outer else [vel_near[n, side] for n in range(9)]
-            aa = [c(n, r).m for n in range(6)] + [lam(f, r).m for f in STRESS]
-            one = sums(drive + strain, saved_adjoint(old_a, rows)(r))
-            two = sums(saved_forward(old_f, rows)(r), aa)
-            acc = [acc_ref[n, r] + (x + y) for n, (x, y) in enumerate(zip(one, two))]
-            for n, x in enumerate(gradients(acc, p, r)):
-                par_out[n, pl.ds(r, planes, stride=rows), :] = x
-            for f, value in back.items():
-                grad_out[f, pl.ds(r, planes, stride=rows), :] = value.m
+            drive = drives if r == 0 else [now_vel[n, side.row(r) - 1] for n in range(9)]
+            cc = [c(n, r).m for n in range(6)] + [lam(f, r).m for f in STRESS]
+            kept_f, kept_a = kept_end(kept, kept_ends, side, r)
+            adds = zip(sums(drive + strain, kept_a), sums(kept_f, cc))
+            acc = [acc_ref[n, r] + (x + y) for n, (x, y) in enumerate(adds)]
+            finals.append(([back[f].m for f in range(len(back))], gradients(acc, p, r)))
             continue
-        if outer:
-            for n, x in enumerate(drives[r]):
-                save_vel[n, side] = x
+        if r == 0:
+            for n, x in enumerate(drives):
+                save_vel[n] = x
             for n in range(6):
-                save_cot[n, side] = c(n, r).m
+                save_cot[n] = c(n, 0).m
         for n, x in enumerate(strain):
-            save_str[n, at] = x
-        new_f[r] = new_fields(p, old, v, e, g, dw, read(src_ref, j, r), r)
-        back[PP] = back[PP] + read(rec_ref, steps - 2 - j, r)
-        new_a[r] = {f: value * p(PF, r) for f, value in back.items()}
+            save_str[n, r] = x
+        new = new_fields(p, old, v, e, g, dw, read(src_ref, j, side.row(r)), r)
+        back[PP] = back[PP] + read(rec_ref, steps - 2 - j, side.row(r))
+        factor = p(PF, r)
         for f in range(f_out.shape[0]):
-            write(f_out, new_f[r][f], f, at)
-            write(a_out, new_a[r][f], f, at)
-    if final:
-        for r in range(2, rows - 2):
-            for n in range(par_mid.shape[0]):
-                par_out[n, pl.ds(r, planes, stride=rows), :] = par_mid[n, r - 2]
-            for f in range(grad_mid.shape[0]):
-                grad_out[f, pl.ds(r, planes, stride=rows), :] = grad_mid[f, r - 2]
+            write(f_out, new[f], f, r)
+            write(a_out, back[f] * factor, f, r)
+    if not final:
+        s, a = (lambda f, r: read(f_out, f, r)), (lambda f, r: read(a_out, f, r))
+        message(tile, side, halo - 2 * (j + 1), s, a, p, *outs, False)
         return
-    messages(
-        tile, gx_axis, halo - 2 * (j + 1), getter((None, f_out), 2, rows), getter((None, a_out), 2, rows), p, rows, *outs, False
-    )
+    for which, out in enumerate((grad_out, par_out)):
+        for n in range(out.shape[0]):
+            if not swap:
+                for r in range(2):
+                    out[n, r] = finals[r][which][n]
+                continue
+            mid, other = ((grad_mid, grad_other), (par_mid, par_other))[which]
+            for r in range(2):
+                mine, its = finals[r][which][n], other[n, r]
+                out[n, pl.ds(r, planes, stride=rows), :] = jnp.where(side.last, its, mine)
+                out[n, pl.ds(rows - 1 - r, planes, stride=rows), :] = jnp.where(side.last, mine, its)
+            for r in range(2, rows - 2):
+                out[n, pl.ds(r, planes, stride=rows), :] = mid[n, r - 2]
 
 
 def swaps(axis, odd):
@@ -652,11 +666,8 @@
     return sorted(out)
 
 
-def exchange(axis, a, b):
-    mesh = ("gx", "gy")
-    b = lax.ppermute(b, mesh, swaps(axis, 1))
-    a = lax.ppermute(a, mesh, swaps(axis, 0))
-    return a, b
+def swap_rows(axis, number, message):
+    return lax.ppermute(message, ("gx", "gy"), swaps(axis, number))
 
 
 def call(kernel, outs, *args):
@@ -709,51 +720,63 @@
         ],
         compiler_params=pltpu.CompilerParams(vmem_limit_bytes=48 << 20),
     )(*[pltpu.with_memory_space_constraint(x, pltpu.HBM) for x in inputs])
-    ay, by = exchange("gy", ay, by)
+    ay, by = swap_rows("gy", 0, ay), swap_rows("gy", 1, by)
     rec, src = call(functools.partial(inject_kernel, halo, "gx", "gy"), [(steps, *wide)] * 2, *small)
     def tiles(n, reach):
         return n + -(-n // (columns // (2 * reach))), planes, columns
 
     assert rows >= 6
-    part = lambda k, r, shape: (k, r, *shape[1:])
-    w, m = wide, own
-    parts = [part(6, 2, w), part(6, 2, m), part(6, 2, w)]
-    mid, end = part(count, rows - 4, w), part(count, 4, w)
-    p, fm, fe, am, ae, ma, mb, *part_refs = call(
-        functools.partial(spread_kernel, halo, "gx", "gy"),
-        [(8, *wide), mid, end, mid, end] + [tiles(2 * EDGE + 2, halo)] * 2 + parts,
+    w, m = wide[1:], own[1:]
+    parts = [(6, *w), (6, *m), (6, *w)]
+    mid, end = (count, rows - 4, *w), (count, 2, *w)
+    group = [end, end, tiles(2 * EDGE + 2, halo)] + parts
+    p, fm, am, *rest = call(
+        functools.partial(spread_kernel, halo, "gx", "gy"), [(8, *wide), mid, mid] + group * 2,
         fields, field_cot, p_own, ay, by, rec,
     )
-    saved_f, saved_a, hk, acc = [], [], [], []
-    nears = [part(6, 4, w)] * 3
+    ends = [rest[:6], rest[6:]]
+    coming = [swap_rows("gx", swap, ends[swap][2]) for swap in (0, 1)]
+    hk, kept = [[], []], []
+    saves = [(9, rows - 2, *m), (7, rows - 4, *m), (6, rows - 2, *m), (7, *own)]
+    nears = [(6, 4, *w)] * 3
     for j in range(steps - 1):
-        ma, mb = exchange("gx", ma, mb)
-        outs = [mid, mid, part(9, rows - 2, m), part(7, rows - 4, m), part(6, rows - 2, m), (7, *own)] + nears
-        nfm, nam, vel, strain, cot, sig, *near_refs = call(
-            functools.partial(interior_kernel, halo, j, steps), outs, fm, fe, am, ae, p, src, rec
+        fm, am, *rest = call(
+            functools.partial(interior_kernel, "gx", halo, j, steps), [mid, mid] + saves + nears,
+            fm, ends[0][0], ends[1][0], am, ends[0][1], ends[1][1], p, src, rec,
         )
-        outs = [end, end, part(9, 2, m), part(7, 4, m), part(6, 2, m)] + [tiles(2 * EDGE, halo - 2 * (j + 1))] * 2 + parts
-        outs += [] if j else [(2, 2, 2 * planes, columns)]
-        fe, ae, vel2, strain2, cot2, ma, mb, *rest = call(
-            functools.partial(edge_kernel, "gx", halo, j, steps), outs,
-            fe, ae, p, ma, mb, *part_refs, *near_refs, *hk, src, rec,
+        kept.append(rest[:4])
+        near_refs = rest[4:]
+        for swap in (0, 1):
+            f, a, _, *part_refs = ends[swap]
+            outs = [end, end, (9, *m), (7, 2, *m), (6, *m), tiles(2 * EDGE, halo - 2 * (j + 1))] + parts
+            outs += [] if j else [(2, *w)]
+            f, a, vel, strain, cot, message_out, *rest = call(
+                functools.partial(end_kernel, "gx", swap, halo, j, steps), outs,
+                f, a, p, coming[swap], *part_refs, *near_refs, *hk[swap], src, rec,
+            )
+            ends[swap] = [f, a, message_out, *rest[:3]]
+            coming[swap] = swap_rows("gx", swap, message_out)
+            hk[swap] = hk[swap] or rest[3:]
+            kept[j] = kept[j] + [vel, strain, cot]
+    middle = [x for t in range(1, steps - 1) for x in kept[t] + kept[steps - 1 - t]]
+    accs = call(
+        functools.partial(sums_kernel, "gx", rows, steps - 2), [(9, rows - 4, *m), (9, 2, *m), (9, 2, *m)], *middle
+    )
+    grad_mid, par_mid, vel, _, _, _, *near_refs = call(
+        functools.partial(interior_kernel, "gx", halo, steps - 1, steps),
+        [(count, rows - 4, *m), (7, rows - 4, *m)] + saves + nears,
+        fm, ends[0][0], ends[1][0], am, ends[0][1], ends[1][1], p, *kept[0][:4], accs[0],
+    )
+    done = []
+    for swap in (0, 1):
+        f, a, _, *part_refs = ends[swap]
+        outs = [(count, *plane), (7, *plane)] if swap else [(count, 2, *m), (7, 2, *m)]
+        done = call(
+            functools.partial(end_kernel, "gx", swap, halo, steps - 1, steps), outs,
+            f, a, p, coming[swap], *part_refs, *near_refs, *hk[swap], *kept[0][:4],
+            *kept[0][4 + 3 * swap : 7 + 3 * swap], accs[1 + swap], vel, *([grad_mid, par_mid] * swap), *done,
         )
-        fm, am, part_refs = nfm, nam, rest[:3]
-        hk = hk or rest[3:]
-        saved_f.append([vel, vel2, strain, strain2])
-        saved_a.append([cot, cot2, sig])
-    ma, mb = exchange("gx", ma, mb)
-    middle = [x for t in range(1, steps - 1) for x in saved_f[t] + saved_a[steps - 1 - t]]
-    (acc,) = call(functools.partial(sums_kernel, rows), [(9, *own)], *middle)
-    outs = [part(count, rows - 4, m), part(7, rows - 4, m), part(9, 2, m)] + nears
-    grad_mid, par_mid, vel_near, *near_refs = call(
-        functools.partial(interior_kernel, halo, steps - 1, steps), outs, fm, fe, am, ae, p, *saved_f[0], *saved_a[0], acc
-    )
-    grad, par = call(
-        functools.partial(edge_kernel, "gx", halo, steps - 1, steps), [(count, *plane), (7, *plane)],
-        fe, ae, p, ma, mb, *part_refs, *near_refs, *hk, *saved_f[0], *saved_a[0], acc, grad_mid, par_mid, vel_near,
-    )
-    return grad.reshape(count, planes, rows, columns), par.reshape(7, planes, rows, columns)
+    return done[0].reshape(count, planes, rows, columns), done[1].reshape(7, planes, rows, columns)
 
 
 def solution(mesh):

time: 36.6 us -> 34.7 us (0.948)
  waiting for transfers between devices: 17.3 us -> 13.6 us
  Pallas kernels: 8.97 us -> 10.3 us
    ppermute x10, waiting for transfers between devices: 17.3 us -> 13.6 us  [swap_rows(): return lax.ppermute(message, ('gx', 'gy'), swaps(axis, number))]
    pallas_call x11 -> x15, Pallas kernels: 7.02 us -> 8.38 us  [call(): pl.pallas_call(kernel, out_shape=shapes, in_specs=[pl.BlockSpec(memory_sp...]
  transfers between devices with their start and end apart: 10 -> 10, of which waited for: 9 -> 7; matrix products, arithmetic and copies ran while one was open for 0% -> 0% of each run, Pallas kernels for 10% -> 19%
where the time goes in v5:
time: 34.7 us; the launch traced here: 34.6 us
  waiting for transfers between devices  13.6 us (39%)
  Pallas kernels  10.3 us (30%)
  starting transfers between devices  9.86 us (28%)
  between operations  0.77 us (2%)
    ppermute x10, waiting for transfers between devices, swap_rows(): return lax.ppermute(message, ('gx', 'gy'), swaps(axis, number))  13.6 us
    ppermute x10, starting transfers between devices, swap_rows(): return lax.ppermute(message, ('gx', 'gy'), swaps(axis, number))  9.86 us
    pallas_call x15, Pallas kernels, call(): pl.pallas_call(kernel, out_shape=shapes, in_specs=[pl.BlockSpec(memory_sp...  8.38 us
    pallas_call x1, Pallas kernels, per_device(): pl.pallas_call(start, out_shape=[jax.ShapeDtypeStruct(s, jnp.float32) for...  1.95 us
  transfers between devices with their start and end apart: 10, of which 7 were waited for; matrix products, arithmetic and copies ran while one was open for 0% of the time, Pallas kernels for 19%

profile of v5, /device:TPU:16, one launch (start us, length us, event | category | flops | bytes accessed | tf_op | source)
XLA Modules:
  0.0 34.6 jit_solution(12178910230226729445)
XLA Ops:
  0.6 1.9 %shard_map.167 = (f32[8,8,8,128]{3,2,1,0:T(8,128)S(1)}, f32[17,8,128]{2,1,0:T(8,128)S(1)}, f32[17,8,128]{2,1,0:T(8,128)S(1)}, f32[13,64,128]{2,1,0:T(8,128)S(1)}...) custom-call(f32[1,64,128]{2,1,0:T(8,128)} %bitcast.18, ...), custom_call_target="tpu_custom_call" | custom-call | tf_op jit(solution)/shard_map/pallas_call | solution.py:710
  2.6 0.1 collective-permute-start
  2.7 1.6 %collective-permute-start.1 = (f32[17,8,128]{2,1,0:T(8,128)S(1)}, f32[17,8,128]{2,1,0:T(8,128)S(1)}, u32[]{:S(2)}, u32[]{:S(2)}) collective-permute-start(f32[17,8,128]{2,1,0:T(8,128)S(1)} %get-tuple-element.128), channel_id=1, source_target_pairs={{0,4},{1,2},{2,1},{3,7},{4,0},{5,6},{6,5},{7,3},{8,12},{9,10},{10,... | collective-permute-start | bytes 208904 | tf_op jit(solution)/shard_map/ppermute | solution.py:670
  4.2 1.2 %shard_map.168 = (f32[4,8,16,128]{3,2,1,0:T(8,128)S(1)}, f32[4,8,16,128]{3,2,1,0:T(8,128)S(1)}) custom-call(s32[1,512]{1,0:T(1,128)S(1)} %get-tuple-element.129.rec_ref, f32[4,512]{1,0:T(4,128)S(1)} %get-tuple-element.130.cot_ref, s32[1,64]{1,0:T(1,128)S(1)} %get-tuple-element.131.src_ref, f32[4,64]{1,0:T(4,128)S(1)} %get-tuple-element.132.amp_ref), custom_call_target="tpu_custom_call" | custom-call | tf_op jit(solution)/shard_map/pallas_call | solution.py:675
  5.4 0.0 collective-permute-done.ay_ref
  5.4 1.6 %collective-permute-done.1.by_ref = f32[17,8,128]{2,1,0:T(8,128)S(1)} collective-permute-done((f32[17,8,128]{2,1,0:T(8,128)S(1)}, f32[17,8,128]{2,1,0:T(8,128)S(1)}, u32[]{:S(2)}, u32[]{:S(2)}) %collective-permute-start.1) | collective-permute-done | bytes 69664 | tf_op jit(solution)/shard_map/ppermute | solution.py:670
  7.0 0.8 %shard_map.169 = (f32[8,8,16,128]{3,2,1,0:T(8,128)S(1)}, f32[13,4,16,128]{3,2,1,0:T(8,128)S(1)}, f32[13,4,16,128]{3,2,1,0:T(8,128)S(1)}, f32[13,2,16,128]{3,2,1,...) custom-call(f32[13,64,128]{2,1,0:T(8,128)S(1)} %get-tuple-element.12, ...), custom_call_target="tpu_custom_call" | custom-call | tf_op jit(solution)/shard_map/pallas_call | solution.py:675
  7.9 1.6 %collective-permute-start.4 = (f32[21,8,128]{2,1,0:T(8,128)S(1)}, f32[21,8,128]{2,1,0:T(8,128)S(1)}, u32[]{:S(2)}, u32[]{:S(2)}) collective-permute-start(f32[21,8,128]{2,1,0:T(8,128)S(1)} %get-tuple-element.156), channel_id=1, source_target_pairs={{0,4},{1,5},{2,6},{3,7},{4,0},{5,1},{6,2},{7,3},{8,12},{9,13},{10,... | collective-permute-start | bytes 258056 | tf_op jit(solution)/shard_map/ppermute | solution.py:670
  9.4 0.4 %collective-permute-start.2 = (f32[21,8,128]{2,1,0:T(8,128)S(1)}, f32[21,8,128]{2,1,0:T(8,128)S(1)}, u32[]{:S(2)}, u32[]{:S(2)}) collective-permute-start(f32[21,8,128]{2,1,0:T(8,128)S(1)} %get-tuple-element.137), channel_id=1, source_target_pairs={{0,1},{1,0},{2,3},{3,2},{4,8},{5,9},{6,10},{7,11},{8,4},{9,5},{10,... | collective-permute-start | bytes 258056 | tf_op jit(solution)/shard_map/ppermute | solution.py:670
  9.9 0.6 %shard_map.170 = (f32[13,4,16,128]{3,2,1,0:T(8,128)S(1)}, f32[13,4,16,128]{3,2,1,0:T(8,128)S(1)}, f32[9,6,8,128]{3,2,1,0:T(8,128)S(1)}, f32[7,4,8,128]{3,2,1,0:T...) custom-call(f32[13,4,16,128]{3,2,1,0:T(8,128)S(1)} %get-tuple-elemen, ...), custom_call_target="tpu_custom_call" | custom-call | tf_op jit(solution)/shard_map/pallas_call | solution.py:675
  10.4 3.0 %collective-permute-done.4.refs_3_ = f32[21,8,128]{2,1,0:T(8,128)S(1)} collective-permute-done((f32[21,8,128]{2,1,0:T(8,128)S(1)}, f32[21,8,128]{2,1,0:T(8,128)S(1)}, u32[]{:S(2)}, u32[]{:S(2)}) %collective-permute-start.4) | collective-permute-done | bytes 86048 | tf_op jit(solution)/shard_map/ppermute | solution.py:670
  13.4 0.3 shard_map.172
  13.7 2.5 %collective-permute-start.6 = (f32[18,8,128]{2,1,0:T(8,128)S(1)}, f32[18,8,128]{2,1,0:T(8,128)S(1)}, u32[]{:S(2)}, u32[]{:S(2)}) collective-permute-start(f32[18,8,128]{2,1,0:T(8,128)S(1)} %get-tuple-element.174), channel_id=1, source_target_pairs={{0,4},{1,5},{2,6},{3,7},{4,0},{5,1},{6,2},{7,3},{8,12},{9,13},{10,... | collective-permute-start | bytes 221192 | tf_op jit(solution)/shard_map/ppermute | solution.py:670
  16.2 0.0 collective-permute-done.2.refs_3_
  16.2 0.3 shard_map.171
  16.6 0.1 collective-permute-start.3
  16.7 0.6 %shard_map.173 = (f32[13,4,16,128]{3,2,1,0:T(8,128)S(1)}, f32[13,4,16,128]{3,2,1,0:T(8,128)S(1)}, f32[9,6,8,128]{3,2,1,0:T(8,128)S(1)}, f32[7,4,8,128]{3,2,1,0:T...) custom-call(f32[13,4,16,128]{3,2,1,0:T(8,128)S(1)} %get-tuple-elemen, ...), custom_call_target="tpu_custom_call" | custom-call | tf_op jit(solution)/shard_map/pallas_call | solution.py:675
  17.2 2.2 %collective-permute-done.6.refs_3_ = f32[18,8,128]{2,1,0:T(8,128)S(1)} collective-permute-done((f32[18,8,128]{2,1,0:T(8,128)S(1)}, f32[18,8,128]{2,1,0:T(8,128)S(1)}, u32[]{:S(2)}, u32[]{:S(2)}) %collective-permute-start.6) | collective-permute-done | bytes 73760 | tf_op jit(solution)/shard_map/ppermute | solution.py:670
  19.4 0.3 shard_map.175
  19.8 1.5 %collective-permute-start.8 = (f32[17,8,128]{2,1,0:T(8,128)S(1)}, f32[17,8,128]{2,1,0:T(8,128)S(1)}, u32[]{:S(2)}, u32[]{:S(2)}) collective-permute-start(f32[17,8,128]{2,1,0:T(8,128)S(1)} %get-tuple-element.192), channel_id=1, source_target_pairs={{0,4},{1,5},{2,6},{3,7},{4,0},{5,1},{6,2},{7,3},{8,12},{9,13},{10,... | collective-permute-start | bytes 208904 | tf_op jit(solution)/shard_map/ppermute | solution.py:670
  21.3 0.6 %collective-permute-done.3.refs_3_ = f32[18,8,128]{2,1,0:T(8,128)S(1)} collective-permute-done((f32[18,8,128]{2,1,0:T(8,128)S(1)}, f32[18,8,128]{2,1,0:T(8,128)S(1)}, u32[]{:S(2)}, u32[]{:S(2)}) %collective-permute-start.3) | collective-permute-done | bytes 73760 | tf_op jit(solution)/shard_map/ppermute | solution.py:670
  21.9 0.3 shard_map.174
  22.2 0.2 collective-permute-start.5
  22.4 0.6 %shard_map.176 = (f32[13,4,16,128]{3,2,1,0:T(8,128)S(1)}, f32[13,4,16,128]{3,2,1,0:T(8,128)S(1)}, f32[9,6,8,128]{3,2,1,0:T(8,128)S(1)}, f32[7,4,8,128]{3,2,1,0:T...) custom-call(f32[13,4,16,128]{3,2,1,0:T(8,128)S(1)} %get-tuple-elemen, ...), custom_call_target="tpu_custom_call" | custom-call | tf_op jit(solution)/shard_map/pallas_call | solution.py:675
  23.0 1.8 %collective-permute-done.8.refs_3_ = f32[17,8,128]{2,1,0:T(8,128)S(1)} collective-permute-done((f32[17,8,128]{2,1,0:T(8,128)S(1)}, f32[17,8,128]{2,1,0:T(8,128)S(1)}, u32[]{:S(2)}, u32[]{:S(2)}) %collective-permute-start.8) | collective-permute-done | bytes 69664 | tf_op jit(solution)/shard_map/ppermute | solution.py:670
  24.8 0.3 shard_map.178
  25.1 1.5 %collective-permute-start.9 = (f32[17,8,128]{2,1,0:T(8,128)S(1)}, f32[17,8,128]{2,1,0:T(8,128)S(1)}, u32[]{:S(2)}, u32[]{:S(2)}) collective-permute-start(f32[17,8,128]{2,1,0:T(8,128)S(1)} %get-tuple-element.234), channel_id=1, source_target_pairs={{0,4},{1,5},{2,6},{3,7},{4,0},{5,1},{6,2},{7,3},{8,12},{9,13},{10,... | collective-permute-start | bytes 208904 | tf_op jit(solution)/shard_map/ppermute | solution.py:670
  26.6 1.3 %collective-permute-done.5.refs_3_ = f32[17,8,128]{2,1,0:T(8,128)S(1)} collective-permute-done((f32[17,8,128]{2,1,0:T(8,128)S(1)}, f32[17,8,128]{2,1,0:T(8,128)S(1)}, u32[]{:S(2)}, u32[]{:S(2)}) %collective-permute-start.5) | collective-permute-done | bytes 69664 | tf_op jit(solution)/shard_map/ppermute | solution.py:670
  27.9 0.3 shard_map.177
  28.2 0.5 %collective-permute-start.7 = (f32[17,8,128]{2,1,0:T(8,128)S(1)}, f32[17,8,128]{2,1,0:T(8,128)S(1)}, u32[]{:S(2)}, u32[]{:S(2)}) collective-permute-start(f32[17,8,128]{2,1,0:T(8,128)S(1)} %get-tuple-element.187), channel_id=1, source_target_pairs={{0,1},{1,0},{2,3},{3,2},{4,8},{5,9},{6,10},{7,11},{8,4},{9,5},{10,... | collective-permute-start | bytes 208904 | tf_op jit(solution)/shard_map/ppermute | solution.py:670
  28.7 0.2 shard_map.179
  28.9 1.3 %shard_map.180 = (f32[13,4,8,128]{3,2,1,0:T(8,128)S(1)}, f32[7,4,8,128]{3,2,1,0:T(8,128)S(1)}, f32[9,6,8,128]{3,2,1,0:T(8,128)S(1)}, f32[7,4,8,128]{3,2,1,0:T(8,...) custom-call(f32[13,4,16,128]{3,2,1,0:T(8,128)S(1)} %get-tuple-elemen, ...), custom_call_target="tpu_custom_call" | custom-call | tf_op jit(solution)/shard_map/pallas_call | solution.py:675
  30.2 0.0 collective-permute-done.9.refs_3_
  30.2 0.2 shard_map.181
  30.4 3.2 %collective-permute-done.7.refs_3_ = f32[17,8,128]{2,1,0:T(8,128)S(1)} collective-permute-done((f32[17,8,128]{2,1,0:T(8,128)S(1)}, f32[17,8,128]{2,1,0:T(8,128)S(1)}, u32[]{:S(2)}, u32[]{:S(2)}) %collective-permute-start.7) | collective-permute-done | bytes 69664 | tf_op jit(solution)/shard_map/ppermute | solution.py:670
  33.5 1.1 %shard_map.182 = (f32[13,64,128]{2,1,0:T(8,128)}, f32[7,64,128]{2,1,0:T(8,128)}) custom-call(f32[13,2,16,128]{3,2,1,0:T(8,128)S(1)} %get-tuple-element.185.refs_2_.refs_0_, f32[13,2,16,128]{3,2,1,0:T(8,128)S(1)} %get-tuple-element.186.refs_5_.refs_1_, f32[8,8,16,128]{3,2,1,0:T(8,128)S(1)} %get-tuple-element.136.refs_6_.refs_2_, ...), custom_call_target="tpu_custom_call" | custom-call | tf_op jit(solution)/shard_map/pallas_call | solution.py:675
Async XLA Ops:
  2.6 2.8 %collective-permute-start = (f32[17,8,128]{2,1,0:T(8,128)S(1)}, f32[17,8,128]{2,1,0:T(8,128)S(1)}, u32[]{:S(2)}, u32[]{:S(2)}) collective-permute-start(f32[17,8,128]{2,1,0:T(8,128)S(1)} %get-tuple-element.127), channel_id=1, source_target_pairs={{0,1},{1,0},{2,3},{3,2},{4,5},{5,4},{6,7},{7,6},{8,9},{9,8},{10,11... | collective-permute-start | bytes 208904 | tf_op jit(solution)/shard_map/ppermute | solution.py:670
  2.7 4.4 %collective-permute-start.1 = (f32[17,8,128]{2,1,0:T(8,128)S(1)}, f32[17,8,128]{2,1,0:T(8,128)S(1)}, u32[]{:S(2)}, u32[]{:S(2)}) collective-permute-start(f32[17,8,128]{2,1,0:T(8,128)S(1)} %get-tuple-element.128), channel_id=1, source_target_pairs={{0,4},{1,2},{2,1},{3,7},{4,0},{5,6},{6,5},{7,3},{8,12},{9,10},{10,... | collective-permute-start | bytes 208904 | tf_op jit(solution)/shard_map/ppermute | solution.py:670
  7.9 5.5 %collective-permute-start.4 = (f32[21,8,128]{2,1,0:T(8,128)S(1)}, f32[21,8,128]{2,1,0:T(8,128)S(1)}, u32[]{:S(2)}, u32[]{:S(2)}) collective-permute-start(f32[21,8,128]{2,1,0:T(8,128)S(1)} %get-tuple-element.156), channel_id=1, source_target_pairs={{0,4},{1,5},{2,6},{3,7},{4,0},{5,1},{6,2},{7,3},{8,12},{9,13},{10,... | collective-permute-start | bytes 258056 | tf_op jit(solution)/shard_map/ppermute | solution.py:670
  9.4 6.8 %collective-permute-start.2 = (f32[21,8,128]{2,1,0:T(8,128)S(1)}, f32[21,8,128]{2,1,0:T(8,128)S(1)}, u32[]{:S(2)}, u32[]{:S(2)}) collective-permute-start(f32[21,8,128]{2,1,0:T(8,128)S(1)} %get-tuple-element.137), channel_id=1, source_target_pairs={{0,1},{1,0},{2,3},{3,2},{4,8},{5,9},{6,10},{7,11},{8,4},{9,5},{10,... | collective-permute-start | bytes 258056 | tf_op jit(solution)/shard_map/ppermute | solution.py:670
  13.7 5.7 %collective-permute-start.6 = (f32[18,8,128]{2,1,0:T(8,128)S(1)}, f32[18,8,128]{2,1,0:T(8,128)S(1)}, u32[]{:S(2)}, u32[]{:S(2)}) collective-permute-start(f32[18,8,128]{2,1,0:T(8,128)S(1)} %get-tuple-element.174), channel_id=1, source_target_pairs={{0,4},{1,5},{2,6},{3,7},{4,0},{5,1},{6,2},{7,3},{8,12},{9,13},{10,... | collective-permute-start | bytes 221192 | tf_op jit(solution)/shard_map/ppermute | solution.py:670
  16.6 5.3 %collective-permute-start.3 = (f32[18,8,128]{2,1,0:T(8,128)S(1)}, f32[18,8,128]{2,1,0:T(8,128)S(1)}, u32[]{:S(2)}, u32[]{:S(2)}) collective-permute-start(f32[18,8,128]{2,1,0:T(8,128)S(1)} %get-tuple-element.151), channel_id=1, source_target_pairs={{0,1},{1,0},{2,3},{3,2},{4,8},{5,9},{6,10},{7,11},{8,4},{9,5},{10,... | collective-permute-start | bytes 221192 | tf_op jit(solution)/shard_map/ppermute | solution.py:670
  19.8 5.0 %collective-permute-start.8 = (f32[17,8,128]{2,1,0:T(8,128)S(1)}, f32[17,8,128]{2,1,0:T(8,128)S(1)}, u32[]{:S(2)}, u32[]{:S(2)}) collective-permute-start(f32[17,8,128]{2,1,0:T(8,128)S(1)} %get-tuple-element.192), channel_id=1, source_target_pairs={{0,4},{1,5},{2,6},{3,7},{4,0},{5,1},{6,2},{7,3},{8,12},{9,13},{10,... | collective-permute-start | bytes 208904 | tf_op jit(solution)/shard_map/ppermute | solution.py:670
  22.2 5.7 %collective-permute-start.5 = (f32[17,8,128]{2,1,0:T(8,128)S(1)}, f32[17,8,128]{2,1,0:T(8,128)S(1)}, u32[]{:S(2)}, u32[]{:S(2)}) collective-permute-start(f32[17,8,128]{2,1,0:T(8,128)S(1)} %get-tuple-element.169), channel_id=1, source_target_pairs={{0,1},{1,0},{2,3},{3,2},{4,8},{5,9},{6,10},{7,11},{8,4},{9,5},{10,... | collective-permute-start | bytes 208904 | tf_op jit(solution)/shard_map/ppermute | solution.py:670
  25.1 5.0 %collective-permute-start.9 = (f32[17,8,128]{2,1,0:T(8,128)S(1)}, f32[17,8,128]{2,1,0:T(8,128)S(1)}, u32[]{:S(2)}, u32[]{:S(2)}) collective-permute-start(f32[17,8,128]{2,1,0:T(8,128)S(1)} %get-tuple-element.234), channel_id=1, source_target_pairs={{0,4},{1,5},{2,6},{3,7},{4,0},{5,1},{6,2},{7,3},{8,12},{9,13},{10,... | collective-permute-start | bytes 208904 | tf_op jit(solution)/shard_map/ppermute | solution.py:670
  28.2 5.3 %collective-permute-start.7 = (f32[17,8,128]{2,1,0:T(8,128)S(1)}, f32[17,8,128]{2,1,0:T(8,128)S(1)}, u32[]{:S(2)}, u32[]{:S(2)}) collective-permute-start(f32[17,8,128]{2,1,0:T(8,128)S(1)} %get-tuple-element.187), channel_id=1, source_target_pairs={{0,1},{1,0},{2,3},{3,2},{4,8},{5,9},{6,10},{7,11},{8,4},{9,5},{10,... | collective-permute-start | bytes 208904 | tf_op jit(solution)/shard_map/ppermute | solution.py:670

commit v6 on v5

--- a/solution.py
+++ b/solution.py
@@ -196,8 +196,10 @@
     rows = p_ref.shape[1]
     planes, columns = p_ref.shape[2], p_ref.shape[3]
     lane = lax.broadcasted_iota(jnp.int32, (planes, columns), 1)
-    group = lane // halo
-    per = columns // halo
+    width = 2 * halo
+    group = lane // width
+    early = lax.rem(lane, width) < halo
+    per = columns // width
 
     def at(r):
         return pl.ds(r, planes, stride=rows)
@@ -224,19 +226,23 @@
         for f in range(ref.shape[0]):
             for r in range(rows):
                 sources.append(lambda ref=ref, f=f, r=r: ref[f, at(r), :])
+    zero = jnp.zeros((planes, columns), jnp.float32)
+
+    def edges(n):
+        total = zero
+        for g, source in enumerate(sources[n * per : (n + 1) * per]):
+            total = jnp.where(group == g, roll(source(), halo + width * g, 1), total)
+        return total
+
     waited = False
     for n in range(a_ref.shape[0]):
-        if (n + 1) * per > p_ref.shape[0] * rows and not waited:
+        if (n + 1) * 2 * per > p_ref.shape[0] * rows and not waited:
             for copy in copies[10:]:
                 copy.wait()
             waited = True
-        left = jnp.zeros((planes, columns), jnp.float32)
-        right = left
-        for g in range(per):
-            if n * per + g < len(sources):
-                x = sources[n * per + g]()
-                left = jnp.where(group == g, roll(x, halo * g, 1), left)
-                right = jnp.where(group == g, roll(x, halo * g + halo, 1), right)
+        x, y = edges(2 * n), edges(2 * n + 1)
+        right = jnp.where(early, x, roll(y, halo, 1))
+        left = jnp.where(early, roll(x, -halo, 1), y)
         a_ref[n] = jnp.where(even, right, left)
         b_ref[n] = jnp.where(even, left, right)
 
@@ -272,22 +278,21 @@
 def spreader(halo, gy_axis, ay_ref, by_ref, rows, tile):
     at_y = lax.axis_index(gy_axis)
     even_y = lax.rem(at_y, 2) == 0
-    columns = tile.columns
-    per = columns // halo
-    on_right = (tile.lane < halo) & (at_y < lax.axis_size(gy_axis) - 1)
-    on_left = (tile.lane >= columns - halo) & (at_y > 0)
+    columns, width = tile.columns, 2 * halo
+    per = columns // width
+    early = lax.rem(tile.lane, width) < halo
+    on = ((tile.lane < halo) & (at_y < lax.axis_size(gy_axis) - 1)) | ((tile.lane >= columns - halo) & (at_y > 0))
 
     @memo
     def packs(n):
         a, b = ay_ref[n], by_ref[n]
-        return jnp.where(even_y, a, b), jnp.where(even_y, b, a)
+        right, left = jnp.where(even_y, a, b), jnp.where(even_y, b, a)
+        return jnp.where(early, left, roll(right, halo, 1)), jnp.where(early, roll(left, -halo, 1), right)
 
     def side(f, r):
         n = f * rows + r
-        g = n % per
-        right, left = packs(n // per)
-        a, b = roll(right, -halo * g, 1), roll(left, -halo * (g + 1), 1)
-        return jnp.where(on_right, a, jnp.where(on_left, b, 0.0))
+        tiles = packs(n // (2 * per))
+        return jnp.where(on, roll(tiles[n // per % 2], -(halo + width * (n % per)), 1), 0.0)
 
     return side
 
@@ -359,7 +364,7 @@
         local = Tile(planes, columns, halo, end.flip)
         s, a = (lambda f, r, ref=ref: read(ref, f, r) for ref in group[:2])
         p = lambda f, r, end=end: read(p_out, f, end.row(r))
-        message(local, end, halo, s, a, p, *group[2:], True)
+        message(local, end, halo - 1, s, a, p, *group[2:], True)
 
 
 def sums(ff, aa):
@@ -568,7 +573,7 @@
     rows, planes, columns = p_ref.shape[1], p_ref.shape[2] // 2, p_ref.shape[3]
     side = Side(gx_axis, swap, rows)
     tile = Tile(planes, columns, halo, side.flip)
-    got = receive(tile, side, msg_ref, 2 * EDGE + (2 if first else 0), halo - 2 * j)
+    got = receive(tile, side, msg_ref, 2 * EDGE + (2 if first else 0), halo - 1 - 2 * j)
     p = lambda f, r: read(p_ref, f, side.row(r))
     old, lam = (lambda f, r: read(f_ref, f, r)), (lambda f, r: read(a_ref, f, r))
     if first:
@@ -634,7 +639,7 @@
             write(a_out, back[f] * factor, f, r)
     if not final:
         s, a = (lambda f, r: read(f_out, f, r)), (lambda f, r: read(a_out, f, r))
-        message(tile, side, halo - 2 * (j + 1), s, a, p, *outs, False)
+        message(tile, side, halo - 1 - 2 * (j + 1), s, a, p, *outs, False)
         return
     for which, out in enumerate((grad_out, par_out)):
         for n in range(out.shape[0]):
@@ -729,7 +734,7 @@
     w, m = wide[1:], own[1:]
     parts = [(6, *w), (6, *m), (6, *w)]
     mid, end = (count, rows - 4, *w), (count, 2, *w)
-    group = [end, end, tiles(2 * EDGE + 2, halo)] + parts
+    group = [end, end, tiles(2 * EDGE + 2, halo - 1)] + parts
     p, fm, am, *rest = call(
         functools.partial(spread_kernel, halo, "gx", "gy"), [(8, *wide), mid, mid] + group * 2,
         fields, field_cot, p_own, ay, by, rec,
@@ -748,7 +753,7 @@
         near_refs = rest[4:]
         for swap in (0, 1):
             f, a, _, *part_refs = ends[swap]
-            outs = [end, end, (9, *m), (7, 2, *m), (6, *m), tiles(2 * EDGE, halo - 2 * (j + 1))] + parts
+            outs = [end, end, (9, *m), (7, 2, *m), (6, *m), tiles(2 * EDGE, halo - 1 - 2 * (j + 1))] + parts
             outs += [] if j else [(2, *w)]
             f, a, vel, strain, cot, message_out, *rest = call(
                 functools.partial(end_kernel, "gx", swap, halo, j, steps), outs,

time: 34.7 us -> 35.6 us (1.026)
  Pallas kernels: 10.3 us -> 11.2 us
  waiting for transfers between devices: 13.6 us -> 14.4 us
  starting transfers between devices: 9.86 us -> 9.08 us
    ppermute x10, starting transfers between devices: 9.86 us -> 9.08 us  [swap_rows(): return lax.ppermute(message, ('gx', 'gy'), swaps(axis, number))]
    ppermute x10, waiting for transfers between devices: 13.6 us -> 14.4 us  [swap_rows(): return lax.ppermute(message, ('gx', 'gy'), swaps(axis, number))]
    pallas_call x15, Pallas kernels: 8.38 us -> 8.95 us  [call(): pl.pallas_call(kernel, out_shape=shapes, in_specs=[pl.BlockSpec(memory_sp...]
  transfers between devices with their start and end apart: 10 -> 10, of which waited for: 7 -> 7; matrix products, arithmetic and copies ran while one was open for 0% -> 0% of each run, Pallas kernels for 19% -> 18%
where the time goes in v6:
time: 35.6 us; the launch traced here: 35.4 us
  waiting for transfers between devices  14.4 us (40%)
  Pallas kernels  11.2 us (31%)
  starting transfers between devices  9.08 us (26%)
  between operations  0.77 us (2%)
    ppermute x10, waiting for transfers between devices, swap_rows(): return lax.ppermute(message, ('gx', 'gy'), swaps(axis, number))  14.4 us
    ppermute x10, starting transfers between devices, swap_rows(): return lax.ppermute(message, ('gx', 'gy'), swaps(axis, number))  9.08 us
    pallas_call x15, Pallas kernels, call(): pl.pallas_call(kernel, out_shape=shapes, in_specs=[pl.BlockSpec(memory_sp...  8.95 us
    pallas_call x1, Pallas kernels, per_device(): pl.pallas_call(start, out_shape=[jax.ShapeDtypeStruct(s, jnp.float32) for...  2.23 us
  transfers between devices with their start and end apart: 10, of which 7 were waited for; matrix products, arithmetic and copies ran while one was open for 0% of the time, Pallas kernels for 18%

profile of v6, /device:TPU:16, one launch (start us, length us, event | category | flops | bytes accessed | tf_op | source)
XLA Modules:
  0.0 35.4 jit_solution(15536883935083314549)
XLA Ops:
  0.6 2.2 %shard_map.167 = (f32[8,8,8,128]{3,2,1,0:T(8,128)S(1)}, f32[17,8,128]{2,1,0:T(8,128)S(1)}, f32[17,8,128]{2,1,0:T(8,128)S(1)}, f32[13,64,128]{2,1,0:T(8,128)S(1)}...) custom-call(f32[1,64,128]{2,1,0:T(8,128)} %bitcast.18, ...), custom_call_target="tpu_custom_call" | custom-call | tf_op jit(solution)/shard_map/pallas_call | solution.py:715
  2.9 0.1 collective-permute-start
  3.0 1.6 %collective-permute-start.1 = (f32[17,8,128]{2,1,0:T(8,128)S(1)}, f32[17,8,128]{2,1,0:T(8,128)S(1)}, u32[]{:S(2)}, u32[]{:S(2)}) collective-permute-start(f32[17,8,128]{2,1,0:T(8,128)S(1)} %get-tuple-element.128), channel_id=1, source_target_pairs={{0,4},{1,2},{2,1},{3,7},{4,0},{5,6},{6,5},{7,3},{8,12},{9,10},{10,... | collective-permute-start | bytes 208904 | tf_op jit(solution)/shard_map/ppermute | solution.py:675
  4.5 1.2 %shard_map.168 = (f32[4,8,16,128]{3,2,1,0:T(8,128)S(1)}, f32[4,8,16,128]{3,2,1,0:T(8,128)S(1)}) custom-call(s32[1,512]{1,0:T(1,128)S(1)} %get-tuple-element.129.rec_ref, f32[4,512]{1,0:T(4,128)S(1)} %get-tuple-element.130.cot_ref, s32[1,64]{1,0:T(1,128)S(1)} %get-tuple-element.131.src_ref, f32[4,64]{1,0:T(4,128)S(1)} %get-tuple-element.132.amp_ref), custom_call_target="tpu_custom_call" | custom-call | tf_op jit(solution)/shard_map/pallas_call | solution.py:680
  5.7 0.0 collective-permute-done.ay_ref
  5.7 1.6 %collective-permute-done.1.by_ref = f32[17,8,128]{2,1,0:T(8,128)S(1)} collective-permute-done((f32[17,8,128]{2,1,0:T(8,128)S(1)}, f32[17,8,128]{2,1,0:T(8,128)S(1)}, u32[]{:S(2)}, u32[]{:S(2)}) %collective-permute-start.1) | collective-permute-done | bytes 69664 | tf_op jit(solution)/shard_map/ppermute | solution.py:675
  7.3 1.4 %shard_map.169 = (f32[8,8,16,128]{3,2,1,0:T(8,128)S(1)}, f32[13,4,16,128]{3,2,1,0:T(8,128)S(1)}, f32[13,4,16,128]{3,2,1,0:T(8,128)S(1)}, f32[13,2,16,128]{3,2,1,...) custom-call(f32[13,64,128]{2,1,0:T(8,128)S(1)} %get-tuple-element.12, ...), custom_call_target="tpu_custom_call" | custom-call | tf_op jit(solution)/shard_map/pallas_call | solution.py:680
  8.7 1.6 %collective-permute-start.4 = (f32[20,8,128]{2,1,0:T(8,128)S(1)}, f32[20,8,128]{2,1,0:T(8,128)S(1)}, u32[]{:S(2)}, u32[]{:S(2)}) collective-permute-start(f32[20,8,128]{2,1,0:T(8,128)S(1)} %get-tuple-element.156), channel_id=1, source_target_pairs={{0,4},{1,5},{2,6},{3,7},{4,0},{5,1},{6,2},{7,3},{8,12},{9,13},{10,... | collective-permute-start | bytes 245768 | tf_op jit(solution)/shard_map/ppermute | solution.py:675
  10.3 0.4 %collective-permute-start.2 = (f32[20,8,128]{2,1,0:T(8,128)S(1)}, f32[20,8,128]{2,1,0:T(8,128)S(1)}, u32[]{:S(2)}, u32[]{:S(2)}) collective-permute-start(f32[20,8,128]{2,1,0:T(8,128)S(1)} %get-tuple-element.137), channel_id=1, source_target_pairs={{0,1},{1,0},{2,3},{3,2},{4,8},{5,9},{6,10},{7,11},{8,4},{9,5},{10,... | collective-permute-start | bytes 245768 | tf_op jit(solution)/shard_map/ppermute | solution.py:675
  10.7 0.6 %shard_map.170 = (f32[13,4,16,128]{3,2,1,0:T(8,128)S(1)}, f32[13,4,16,128]{3,2,1,0:T(8,128)S(1)}, f32[9,6,8,128]{3,2,1,0:T(8,128)S(1)}, f32[7,4,8,128]{3,2,1,0:T...) custom-call(f32[13,4,16,128]{3,2,1,0:T(8,128)S(1)} %get-tuple-elemen, ...), custom_call_target="tpu_custom_call" | custom-call | tf_op jit(solution)/shard_map/pallas_call | solution.py:680
  11.3 2.8 %collective-permute-done.4.refs_3_ = f32[20,8,128]{2,1,0:T(8,128)S(1)} collective-permute-done((f32[20,8,128]{2,1,0:T(8,128)S(1)}, f32[20,8,128]{2,1,0:T(8,128)S(1)}, u32[]{:S(2)}, u32[]{:S(2)}) %collective-permute-start.4) | collective-permute-done | bytes 81952 | tf_op jit(solution)/shard_map/ppermute | solution.py:675
  14.1 0.3 shard_map.172
  14.4 2.5 %collective-permute-start.6 = (f32[18,8,128]{2,1,0:T(8,128)S(1)}, f32[18,8,128]{2,1,0:T(8,128)S(1)}, u32[]{:S(2)}, u32[]{:S(2)}) collective-permute-start(f32[18,8,128]{2,1,0:T(8,128)S(1)} %get-tuple-element.174), channel_id=1, source_target_pairs={{0,4},{1,5},{2,6},{3,7},{4,0},{5,1},{6,2},{7,3},{8,12},{9,13},{10,... | collective-permute-start | bytes 221192 | tf_op jit(solution)/shard_map/ppermute | solution.py:675
  16.9 0.0 collective-permute-done.2.refs_3_
  16.9 0.3 shard_map.171
  17.3 0.1 collective-permute-start.3
  17.4 0.6 %shard_map.173 = (f32[13,4,16,128]{3,2,1,0:T(8,128)S(1)}, f32[13,4,16,128]{3,2,1,0:T(8,128)S(1)}, f32[9,6,8,128]{3,2,1,0:T(8,128)S(1)}, f32[7,4,8,128]{3,2,1,0:T...) custom-call(f32[13,4,16,128]{3,2,1,0:T(8,128)S(1)} %get-tuple-elemen, ...), custom_call_target="tpu_custom_call" | custom-call | tf_op jit(solution)/shard_map/pallas_call | solution.py:680
  17.9 2.3 %collective-permute-done.6.refs_3_ = f32[18,8,128]{2,1,0:T(8,128)S(1)} collective-permute-done((f32[18,8,128]{2,1,0:T(8,128)S(1)}, f32[18,8,128]{2,1,0:T(8,128)S(1)}, u32[]{:S(2)}, u32[]{:S(2)}) %collective-permute-start.6) | collective-permute-done | bytes 73760 | tf_op jit(solution)/shard_map/ppermute | solution.py:675
  20.3 0.3 shard_map.175
  20.6 1.3 %collective-permute-start.8 = (f32[17,8,128]{2,1,0:T(8,128)S(1)}, f32[17,8,128]{2,1,0:T(8,128)S(1)}, u32[]{:S(2)}, u32[]{:S(2)}) collective-permute-start(f32[17,8,128]{2,1,0:T(8,128)S(1)} %get-tuple-element.192), channel_id=1, source_target_pairs={{0,4},{1,5},{2,6},{3,7},{4,0},{5,1},{6,2},{7,3},{8,12},{9,13},{10,... | collective-permute-start | bytes 208904 | tf_op jit(solution)/shard_map/ppermute | solution.py:675
  21.9 0.7 %collective-permute-done.3.refs_3_ = f32[18,8,128]{2,1,0:T(8,128)S(1)} collective-permute-done((f32[18,8,128]{2,1,0:T(8,128)S(1)}, f32[18,8,128]{2,1,0:T(8,128)S(1)}, u32[]{:S(2)}, u32[]{:S(2)}) %collective-permute-start.3) | collective-permute-done | bytes 73760 | tf_op jit(solution)/shard_map/ppermute | solution.py:675
  22.6 0.3 shard_map.174
  22.9 0.2 collective-permute-start.5
  23.1 0.6 %shard_map.176 = (f32[13,4,16,128]{3,2,1,0:T(8,128)S(1)}, f32[13,4,16,128]{3,2,1,0:T(8,128)S(1)}, f32[9,6,8,128]{3,2,1,0:T(8,128)S(1)}, f32[7,4,8,128]{3,2,1,0:T...) custom-call(f32[13,4,16,128]{3,2,1,0:T(8,128)S(1)} %get-tuple-elemen, ...), custom_call_target="tpu_custom_call" | custom-call | tf_op jit(solution)/shard_map/pallas_call | solution.py:680
  23.7 1.8 %collective-permute-done.8.refs_3_ = f32[17,8,128]{2,1,0:T(8,128)S(1)} collective-permute-done((f32[17,8,128]{2,1,0:T(8,128)S(1)}, f32[17,8,128]{2,1,0:T(8,128)S(1)}, u32[]{:S(2)}, u32[]{:S(2)}) %collective-permute-start.8) | collective-permute-done | bytes 69664 | tf_op jit(solution)/shard_map/ppermute | solution.py:675
  25.5 0.3 shard_map.178
  25.8 1.2 %collective-permute-start.9 = (f32[17,8,128]{2,1,0:T(8,128)S(1)}, f32[17,8,128]{2,1,0:T(8,128)S(1)}, u32[]{:S(2)}, u32[]{:S(2)}) collective-permute-start(f32[17,8,128]{2,1,0:T(8,128)S(1)} %get-tuple-element.234), channel_id=1, source_target_pairs={{0,4},{1,5},{2,6},{3,7},{4,0},{5,1},{6,2},{7,3},{8,12},{9,13},{10,... | collective-permute-start | bytes 208904 | tf_op jit(solution)/shard_map/ppermute | solution.py:675
  27.0 1.7 %collective-permute-done.5.refs_3_ = f32[17,8,128]{2,1,0:T(8,128)S(1)} collective-permute-done((f32[17,8,128]{2,1,0:T(8,128)S(1)}, f32[17,8,128]{2,1,0:T(8,128)S(1)}, u32[]{:S(2)}, u32[]{:S(2)}) %collective-permute-start.5) | collective-permute-done | bytes 69664 | tf_op jit(solution)/shard_map/ppermute | solution.py:675
  28.7 0.3 shard_map.177
  29.1 0.2 collective-permute-start.7
  29.3 0.2 shard_map.179
  29.5 1.3 %shard_map.180 = (f32[13,4,8,128]{3,2,1,0:T(8,128)S(1)}, f32[7,4,8,128]{3,2,1,0:T(8,128)S(1)}, f32[9,6,8,128]{3,2,1,0:T(8,128)S(1)}, f32[7,4,8,128]{3,2,1,0:T(8,...) custom-call(f32[13,4,16,128]{3,2,1,0:T(8,128)S(1)} %get-tuple-elemen, ...), custom_call_target="tpu_custom_call" | custom-call | tf_op jit(solution)/shard_map/pallas_call | solution.py:680
  30.7 0.0 collective-permute-done.9.refs_3_
  30.7 0.2 shard_map.181
  30.9 3.4 %collective-permute-done.7.refs_3_ = f32[17,8,128]{2,1,0:T(8,128)S(1)} collective-permute-done((f32[17,8,128]{2,1,0:T(8,128)S(1)}, f32[17,8,128]{2,1,0:T(8,128)S(1)}, u32[]{:S(2)}, u32[]{:S(2)}) %collective-permute-start.7) | collective-permute-done | bytes 69664 | tf_op jit(solution)/shard_map/ppermute | solution.py:675
  34.3 1.1 %shard_map.182 = (f32[13,64,128]{2,1,0:T(8,128)}, f32[7,64,128]{2,1,0:T(8,128)}) custom-call(f32[13,2,16,128]{3,2,1,0:T(8,128)S(1)} %get-tuple-element.185.refs_2_.refs_0_, f32[13,2,16,128]{3,2,1,0:T(8,128)S(1)} %get-tuple-element.186.refs_5_.refs_1_, f32[8,8,16,128]{3,2,1,0:T(8,128)S(1)} %get-tuple-element.136.refs_6_.refs_2_, ...), custom_call_target="tpu_custom_call" | custom-call | tf_op jit(solution)/shard_map/pallas_call | solution.py:680
Async XLA Ops:
  2.9 2.8 %collective-permute-start = (f32[17,8,128]{2,1,0:T(8,128)S(1)}, f32[17,8,128]{2,1,0:T(8,128)S(1)}, u32[]{:S(2)}, u32[]{:S(2)}) collective-permute-start(f32[17,8,128]{2,1,0:T(8,128)S(1)} %get-tuple-element.127), channel_id=1, source_target_pairs={{0,1},{1,0},{2,3},{3,2},{4,5},{5,4},{6,7},{7,6},{8,9},{9,8},{10,11... | collective-permute-start | bytes 208904 | tf_op jit(solution)/shard_map/ppermute | solution.py:675
  3.0 4.4 %collective-permute-start.1 = (f32[17,8,128]{2,1,0:T(8,128)S(1)}, f32[17,8,128]{2,1,0:T(8,128)S(1)}, u32[]{:S(2)}, u32[]{:S(2)}) collective-permute-start(f32[17,8,128]{2,1,0:T(8,128)S(1)} %get-tuple-element.128), channel_id=1, source_target_pairs={{0,4},{1,2},{2,1},{3,7},{4,0},{5,6},{6,5},{7,3},{8,12},{9,10},{10,... | collective-permute-start | bytes 208904 | tf_op jit(solution)/shard_map/ppermute | solution.py:675
  8.7 5.3 %collective-permute-start.4 = (f32[20,8,128]{2,1,0:T(8,128)S(1)}, f32[20,8,128]{2,1,0:T(8,128)S(1)}, u32[]{:S(2)}, u32[]{:S(2)}) collective-permute-start(f32[20,8,128]{2,1,0:T(8,128)S(1)} %get-tuple-element.156), channel_id=1, source_target_pairs={{0,4},{1,5},{2,6},{3,7},{4,0},{5,1},{6,2},{7,3},{8,12},{9,13},{10,... | collective-permute-start | bytes 245768 | tf_op jit(solution)/shard_map/ppermute | solution.py:675
  10.3 6.6 %collective-permute-start.2 = (f32[20,8,128]{2,1,0:T(8,128)S(1)}, f32[20,8,128]{2,1,0:T(8,128)S(1)}, u32[]{:S(2)}, u32[]{:S(2)}) collective-permute-start(f32[20,8,128]{2,1,0:T(8,128)S(1)} %get-tuple-element.137), channel_id=1, source_target_pairs={{0,1},{1,0},{2,3},{3,2},{4,8},{5,9},{6,10},{7,11},{8,4},{9,5},{10,... | collective-permute-start | bytes 245768 | tf_op jit(solution)/shard_map/ppermute | solution.py:675
  14.4 5.8 %collective-permute-start.6 = (f32[18,8,128]{2,1,0:T(8,128)S(1)}, f32[18,8,128]{2,1,0:T(8,128)S(1)}, u32[]{:S(2)}, u32[]{:S(2)}) collective-permute-start(f32[18,8,128]{2,1,0:T(8,128)S(1)} %get-tuple-element.174), channel_id=1, source_target_pairs={{0,4},{1,5},{2,6},{3,7},{4,0},{5,1},{6,2},{7,3},{8,12},{9,13},{10,... | collective-permute-start | bytes 221192 | tf_op jit(solution)/shard_map/ppermute | solution.py:675
  17.3 5.3 %collective-permute-start.3 = (f32[18,8,128]{2,1,0:T(8,128)S(1)}, f32[18,8,128]{2,1,0:T(8,128)S(1)}, u32[]{:S(2)}, u32[]{:S(2)}) collective-permute-start(f32[18,8,128]{2,1,0:T(8,128)S(1)} %get-tuple-element.151), channel_id=1, source_target_pairs={{0,1},{1,0},{2,3},{3,2},{4,8},{5,9},{6,10},{7,11},{8,4},{9,5},{10,... | collective-permute-start | bytes 221192 | tf_op jit(solution)/shard_map/ppermute | solution.py:675
  20.6 4.9 %collective-permute-start.8 = (f32[17,8,128]{2,1,0:T(8,128)S(1)}, f32[17,8,128]{2,1,0:T(8,128)S(1)}, u32[]{:S(2)}, u32[]{:S(2)}) collective-permute-start(f32[17,8,128]{2,1,0:T(8,128)S(1)} %get-tuple-element.192), channel_id=1, source_target_pairs={{0,4},{1,5},{2,6},{3,7},{4,0},{5,1},{6,2},{7,3},{8,12},{9,13},{10,... | collective-permute-start | bytes 208904 | tf_op jit(solution)/shard_map/ppermute | solution.py:675
  22.9 5.8 %collective-permute-start.5 = (f32[17,8,128]{2,1,0:T(8,128)S(1)}, f32[17,8,128]{2,1,0:T(8,128)S(1)}, u32[]{:S(2)}, u32[]{:S(2)}) collective-permute-start(f32[17,8,128]{2,1,0:T(8,128)S(1)} %get-tuple-element.169), channel_id=1, source_target_pairs={{0,1},{1,0},{2,3},{3,2},{4,8},{5,9},{6,10},{7,11},{8,4},{9,5},{10,... | collective-permute-start | bytes 208904 | tf_op jit(solution)/shard_map/ppermute | solution.py:675
  25.8 4.9 %collective-permute-start.9 = (f32[17,8,128]{2,1,0:T(8,128)S(1)}, f32[17,8,128]{2,1,0:T(8,128)S(1)}, u32[]{:S(2)}, u32[]{:S(2)}) collective-permute-start(f32[17,8,128]{2,1,0:T(8,128)S(1)} %get-tuple-element.234), channel_id=1, source_target_pairs={{0,4},{1,5},{2,6},{3,7},{4,0},{5,1},{6,2},{7,3},{8,12},{9,13},{10,... | collective-permute-start | bytes 208904 | tf_op jit(solution)/shard_map/ppermute | solution.py:675
  29.1 5.3 %collective-permute-start.7 = (f32[17,8,128]{2,1,0:T(8,128)S(1)}, f32[17,8,128]{2,1,0:T(8,128)S(1)}, u32[]{:S(2)}, u32[]{:S(2)}) collective-permute-start(f32[17,8,128]{2,1,0:T(8,128)S(1)} %get-tuple-element.187), channel_id=1, source_target_pairs={{0,1},{1,0},{2,3},{3,2},{4,8},{5,9},{6,10},{7,11},{8,4},{9,5},{10,... | collective-permute-start | bytes 208904 | tf_op jit(solution)/shard_map/ppermute | solution.py:675

commit v7 on v5

--- a/solution.py
+++ b/solution.py
@@ -161,7 +161,7 @@
 class Side:
     def __init__(self, axis, swap, rows):
         at, size = lax.axis_index(axis), lax.axis_size(axis)
-        self.last = lax.rem(at, 2) == swap
+        self.last = lax.rem(at, 2) != swap
         self.met = jnp.where(self.last, at < size - 1, at > 0)
         self.base = jnp.where(self.last, rows - 1, 0)
         self.step = jnp.where(self.last, -1, 1)
@@ -297,7 +297,7 @@
 
 
 def whole(mid, ends, axis, rows):
-    last = lax.rem(lax.axis_index(axis), 2) == 0
+    last = lax.rem(lax.axis_index(axis), 2) == 1
 
     @memo
     def get(f, r):
@@ -735,7 +735,7 @@
         fields, field_cot, p_own, ay, by, rec,
     )
     ends = [rest[:6], rest[6:]]
-    coming = [swap_rows("gx", swap, ends[swap][2]) for swap in (0, 1)]
+    coming = [swap_rows("gx", 1 - swap, ends[swap][2]) for swap in (0, 1)]
     hk, kept = [[], []], []
     saves = [(9, rows - 2, *m), (7, rows - 4, *m), (6, rows - 2, *m), (7, *own)]
     nears = [(6, 4, *w)] * 3
@@ -755,7 +755,7 @@
                 f, a, p, coming[swap], *part_refs, *near_refs, *hk[swap], src, rec,
             )
             ends[swap] = [f, a, message_out, *rest[:3]]
-            coming[swap] = swap_rows("gx", swap, message_out)
+            coming[swap] = swap_rows("gx", 1 - swap, message_out)
             hk[swap] = hk[swap] or rest[3:]
             kept[j] = kept[j] + [vel, strain, cot]
     middle = [x for t in range(1, steps - 1) for x in kept[t] + kept[steps - 1 - t]]

time: 34.7 us -> 33.8 us (0.974)
  the two profiles are of different devices: /device:TPU:16 before, /device:TPU:0 now
where the time goes in v7:
time: 33.8 us; the launch traced here: 33.6 us
  starting transfers between devices  15.6 us (46%)
  Pallas kernels  10.4 us (31%)
  waiting for transfers between devices  6.89 us (20%)
  between operations  0.8 us (2%)
    ppermute x10, starting transfers between devices, swap_rows(): return lax.ppermute(message, ('gx', 'gy'), swaps(axis, number))  15.6 us
    pallas_call x15, Pallas kernels, call(): pl.pallas_call(kernel, out_shape=shapes, in_specs=[pl.BlockSpec(memory_sp...  8.43 us
    ppermute x10, waiting for transfers between devices, swap_rows(): return lax.ppermute(message, ('gx', 'gy'), swaps(axis, number))  6.89 us
    pallas_call x1, Pallas kernels, per_device(): pl.pallas_call(start, out_shape=[jax.ShapeDtypeStruct(s, jnp.float32) for...  1.95 us
  transfers between devices with their start and end apart: 10, of which 5 were waited for; matrix products, arithmetic and copies ran while one was open for 0% of the time, Pallas kernels for 19%

profile of v7, /device:TPU:0, one launch (start us, length us, event | category | flops | bytes accessed | tf_op | source)
XLA Modules:
  0.0 33.6 jit_solution(12308845237403784457)
XLA Ops:
  0.6 1.9 %shard_map.167 = (f32[8,8,8,128]{3,2,1,0:T(8,128)S(1)}, f32[17,8,128]{2,1,0:T(8,128)S(1)}, f32[17,8,128]{2,1,0:T(8,128)S(1)}, f32[13,64,128]{2,1,0:T(8,128)S(1)}...) custom-call(f32[1,64,128]{2,1,0:T(8,128)} %bitcast.18, ...), custom_call_target="tpu_custom_call" | custom-call | tf_op jit(solution)/shard_map/pallas_call | solution.py:710
  2.6 0.6 %collective-permute-start = (f32[17,8,128]{2,1,0:T(8,128)S(1)}, f32[17,8,128]{2,1,0:T(8,128)S(1)}, u32[]{:S(2)}, u32[]{:S(2)}) collective-permute-start(f32[17,8,128]{2,1,0:T(8,128)S(1)} %get-tuple-element.127), channel_id=1, source_target_pairs={{0,1},{1,0},{2,3},{3,2},{4,5},{5,4},{6,7},{7,6},{8,9},{9,8},{10,11... | collective-permute-start | bytes 208904 | tf_op jit(solution)/shard_map/ppermute | solution.py:670
  3.2 2.6 %collective-permute-start.1 = (f32[17,8,128]{2,1,0:T(8,128)S(1)}, f32[17,8,128]{2,1,0:T(8,128)S(1)}, u32[]{:S(2)}, u32[]{:S(2)}) collective-permute-start(f32[17,8,128]{2,1,0:T(8,128)S(1)} %get-tuple-element.128), channel_id=1, source_target_pairs={{0,4},{1,2},{2,1},{3,7},{4,0},{5,6},{6,5},{7,3},{8,12},{9,10},{10,... | collective-permute-start | bytes 208904 | tf_op jit(solution)/shard_map/ppermute | solution.py:670
  5.7 1.2 %shard_map.168 = (f32[4,8,16,128]{3,2,1,0:T(8,128)S(1)}, f32[4,8,16,128]{3,2,1,0:T(8,128)S(1)}) custom-call(s32[1,512]{1,0:T(1,128)S(1)} %get-tuple-element.129.rec_ref, f32[4,512]{1,0:T(4,128)S(1)} %get-tuple-element.130.cot_ref, s32[1,64]{1,0:T(1,128)S(1)} %get-tuple-element.131.src_ref, f32[4,64]{1,0:T(4,128)S(1)} %get-tuple-element.132.amp_ref), custom_call_target="tpu_custom_call" | custom-call | tf_op jit(solution)/shard_map/pallas_call | solution.py:675
  6.9 0.0 collective-permute-done.ay_ref
  6.9 1.1 %collective-permute-done.1.by_ref = f32[17,8,128]{2,1,0:T(8,128)S(1)} collective-permute-done((f32[17,8,128]{2,1,0:T(8,128)S(1)}, f32[17,8,128]{2,1,0:T(8,128)S(1)}, u32[]{:S(2)}, u32[]{:S(2)}) %collective-permute-start.1) | collective-permute-done | bytes 69664 | tf_op jit(solution)/shard_map/ppermute | solution.py:670
  8.0 0.8 %shard_map.169 = (f32[8,8,16,128]{3,2,1,0:T(8,128)S(1)}, f32[13,4,16,128]{3,2,1,0:T(8,128)S(1)}, f32[13,4,16,128]{3,2,1,0:T(8,128)S(1)}, f32[13,2,16,128]{3,2,1,...) custom-call(f32[13,64,128]{2,1,0:T(8,128)S(1)} %get-tuple-element.12, ...), custom_call_target="tpu_custom_call" | custom-call | tf_op jit(solution)/shard_map/pallas_call | solution.py:675
  8.8 0.2 collective-permute-start.4
  9.0 3.5 %collective-permute-start.2 = (f32[21,8,128]{2,1,0:T(8,128)S(1)}, f32[21,8,128]{2,1,0:T(8,128)S(1)}, u32[]{:S(2)}, u32[]{:S(2)}) collective-permute-start(f32[21,8,128]{2,1,0:T(8,128)S(1)} %get-tuple-element.137), channel_id=1, source_target_pairs={{0,4},{1,5},{2,6},{3,7},{4,0},{5,1},{6,2},{7,3},{8,12},{9,13},{10,... | collective-permute-start | bytes 258056 | tf_op jit(solution)/shard_map/ppermute | solution.py:670
  12.5 0.6 %shard_map.170 = (f32[13,4,16,128]{3,2,1,0:T(8,128)S(1)}, f32[13,4,16,128]{3,2,1,0:T(8,128)S(1)}, f32[9,6,8,128]{3,2,1,0:T(8,128)S(1)}, f32[7,4,8,128]{3,2,1,0:T...) custom-call(f32[13,4,16,128]{3,2,1,0:T(8,128)S(1)} %get-tuple-elemen, ...), custom_call_target="tpu_custom_call" | custom-call | tf_op jit(solution)/shard_map/pallas_call | solution.py:675
  13.0 0.0 collective-permute-done.4.refs_3_
  13.1 0.3 %shard_map.172 = (f32[13,2,16,128]{3,2,1,0:T(8,128)S(1)}, f32[13,2,16,128]{3,2,1,0:T(8,128)S(1)}, f32[9,8,128]{2,1,0:T(8,128)S(1)}, f32[7,2,8,128]{3,2,1,0:T(8,1...) custom-call(f32[13,2,16,128]{3,2,1,0:T(8,128)S(1)} %get-tuple-elemen, ...), custom_call_target="tpu_custom_call" | custom-call | tf_op jit(solution)/shard_map/pallas_call | solution.py:675
  13.4 0.1 collective-permute-start.6
  13.5 2.2 %collective-permute-done.2.refs_3_ = f32[21,8,128]{2,1,0:T(8,128)S(1)} collective-permute-done((f32[21,8,128]{2,1,0:T(8,128)S(1)}, f32[21,8,128]{2,1,0:T(8,128)S(1)}, u32[]{:S(2)}, u32[]{:S(2)}) %collective-permute-start.2) | collective-permute-done | bytes 86048 | tf_op jit(solution)/shard_map/ppermute | solution.py:670
  15.7 0.3 shard_map.171
  16.1 2.8 %collective-permute-start.3 = (f32[18,8,128]{2,1,0:T(8,128)S(1)}, f32[18,8,128]{2,1,0:T(8,128)S(1)}, u32[]{:S(2)}, u32[]{:S(2)}) collective-permute-start(f32[18,8,128]{2,1,0:T(8,128)S(1)} %get-tuple-element.151), channel_id=1, source_target_pairs={{0,4},{1,5},{2,6},{3,7},{4,0},{5,1},{6,2},{7,3},{8,12},{9,13},{10,... | collective-permute-start | bytes 221192 | tf_op jit(solution)/shard_map/ppermute | solution.py:670
  18.8 0.6 %shard_map.173 = (f32[13,4,16,128]{3,2,1,0:T(8,128)S(1)}, f32[13,4,16,128]{3,2,1,0:T(8,128)S(1)}, f32[9,6,8,128]{3,2,1,0:T(8,128)S(1)}, f32[7,4,8,128]{3,2,1,0:T...) custom-call(f32[13,4,16,128]{3,2,1,0:T(8,128)S(1)} %get-tuple-elemen, ...), custom_call_target="tpu_custom_call" | custom-call | tf_op jit(solution)/shard_map/pallas_call | solution.py:675
  19.4 0.0 collective-permute-done.6.refs_3_
  19.4 0.3 %shard_map.175 = (f32[13,2,16,128]{3,2,1,0:T(8,128)S(1)}, f32[13,2,16,128]{3,2,1,0:T(8,128)S(1)}, f32[9,8,128]{2,1,0:T(8,128)S(1)}, f32[7,2,8,128]{3,2,1,0:T(8,1...) custom-call(f32[13,2,16,128]{3,2,1,0:T(8,128)S(1)} %get-tuple-elemen, ...), custom_call_target="tpu_custom_call" | custom-call | tf_op jit(solution)/shard_map/pallas_call | solution.py:675
  19.8 0.1 collective-permute-start.8
  19.8 1.3 %collective-permute-done.3.refs_3_ = f32[18,8,128]{2,1,0:T(8,128)S(1)} collective-permute-done((f32[18,8,128]{2,1,0:T(8,128)S(1)}, f32[18,8,128]{2,1,0:T(8,128)S(1)}, u32[]{:S(2)}, u32[]{:S(2)}) %collective-permute-start.3) | collective-permute-done | bytes 73760 | tf_op jit(solution)/shard_map/ppermute | solution.py:670
  21.2 0.3 shard_map.174
  21.5 3.1 %collective-permute-start.5 = (f32[17,8,128]{2,1,0:T(8,128)S(1)}, f32[17,8,128]{2,1,0:T(8,128)S(1)}, u32[]{:S(2)}, u32[]{:S(2)}) collective-permute-start(f32[17,8,128]{2,1,0:T(8,128)S(1)} %get-tuple-element.169), channel_id=1, source_target_pairs={{0,4},{1,5},{2,6},{3,7},{4,0},{5,1},{6,2},{7,3},{8,12},{9,13},{10,... | collective-permute-start | bytes 208904 | tf_op jit(solution)/shard_map/ppermute | solution.py:670
  24.6 0.6 %shard_map.176 = (f32[13,4,16,128]{3,2,1,0:T(8,128)S(1)}, f32[13,4,16,128]{3,2,1,0:T(8,128)S(1)}, f32[9,6,8,128]{3,2,1,0:T(8,128)S(1)}, f32[7,4,8,128]{3,2,1,0:T...) custom-call(f32[13,4,16,128]{3,2,1,0:T(8,128)S(1)} %get-tuple-elemen, ...), custom_call_target="tpu_custom_call" | custom-call | tf_op jit(solution)/shard_map/pallas_call | solution.py:675
  25.2 0.0 collective-permute-done.8.refs_3_
  25.2 0.3 %shard_map.178 = (f32[13,2,16,128]{3,2,1,0:T(8,128)S(1)}, f32[13,2,16,128]{3,2,1,0:T(8,128)S(1)}, f32[9,8,128]{2,1,0:T(8,128)S(1)}, f32[7,2,8,128]{3,2,1,0:T(8,1...) custom-call(f32[13,2,16,128]{3,2,1,0:T(8,128)S(1)} %get-tuple-elemen, ...), custom_call_target="tpu_custom_call" | custom-call | tf_op jit(solution)/shard_map/pallas_call | solution.py:675
  25.5 0.1 collective-permute-start.9
  25.6 1.6 %collective-permute-done.5.refs_3_ = f32[17,8,128]{2,1,0:T(8,128)S(1)} collective-permute-done((f32[17,8,128]{2,1,0:T(8,128)S(1)}, f32[17,8,128]{2,1,0:T(8,128)S(1)}, u32[]{:S(2)}, u32[]{:S(2)}) %collective-permute-start.5) | collective-permute-done | bytes 69664 | tf_op jit(solution)/shard_map/ppermute | solution.py:670
  27.2 0.3 shard_map.177
  27.5 2.8 %collective-permute-start.7 = (f32[17,8,128]{2,1,0:T(8,128)S(1)}, f32[17,8,128]{2,1,0:T(8,128)S(1)}, u32[]{:S(2)}, u32[]{:S(2)}) collective-permute-start(f32[17,8,128]{2,1,0:T(8,128)S(1)} %get-tuple-element.187), channel_id=1, source_target_pairs={{0,4},{1,5},{2,6},{3,7},{4,0},{5,1},{6,2},{7,3},{8,12},{9,13},{10,... | collective-permute-start | bytes 208904 | tf_op jit(solution)/shard_map/ppermute | solution.py:670
  30.3 0.2 shard_map.179
  30.5 1.3 %shard_map.180 = (f32[13,4,8,128]{3,2,1,0:T(8,128)S(1)}, f32[7,4,8,128]{3,2,1,0:T(8,128)S(1)}, f32[9,6,8,128]{3,2,1,0:T(8,128)S(1)}, f32[7,4,8,128]{3,2,1,0:T(8,...) custom-call(f32[13,4,16,128]{3,2,1,0:T(8,128)S(1)} %get-tuple-elemen, ...), custom_call_target="tpu_custom_call" | custom-call | tf_op jit(solution)/shard_map/pallas_call | solution.py:675
  31.7 0.0 collective-permute-done.9.refs_3_
  31.7 0.2 shard_map.181
  31.9 0.7 %collective-permute-done.7.refs_3_ = f32[17,8,128]{2,1,0:T(8,128)S(1)} collective-permute-done((f32[17,8,128]{2,1,0:T(8,128)S(1)}, f32[17,8,128]{2,1,0:T(8,128)S(1)}, u32[]{:S(2)}, u32[]{:S(2)}) %collective-permute-start.7) | collective-permute-done | bytes 69664 | tf_op jit(solution)/shard_map/ppermute | solution.py:670
  32.6 1.1 %shard_map.182 = (f32[13,64,128]{2,1,0:T(8,128)}, f32[7,64,128]{2,1,0:T(8,128)}) custom-call(f32[13,2,16,128]{3,2,1,0:T(8,128)S(1)} %get-tuple-element.185.refs_2_.refs_0_, f32[13,2,16,128]{3,2,1,0:T(8,128)S(1)} %get-tuple-element.186.refs_5_.refs_1_, f32[8,8,16,128]{3,2,1,0:T(8,128)S(1)} %get-tuple-element.136.refs_6_.refs_2_, ...), custom_call_target="tpu_custom_call" | custom-call | tf_op jit(solution)/shard_map/pallas_call | solution.py:675
Async XLA Ops:
  2.6 4.3 %collective-permute-start = (f32[17,8,128]{2,1,0:T(8,128)S(1)}, f32[17,8,128]{2,1,0:T(8,128)S(1)}, u32[]{:S(2)}, u32[]{:S(2)}) collective-permute-start(f32[17,8,128]{2,1,0:T(8,128)S(1)} %get-tuple-element.127), channel_id=1, source_target_pairs={{0,1},{1,0},{2,3},{3,2},{4,5},{5,4},{6,7},{7,6},{8,9},{9,8},{10,11... | collective-permute-start | bytes 208904 | tf_op jit(solution)/shard_map/ppermute | solution.py:670
  3.2 4.8 %collective-permute-start.1 = (f32[17,8,128]{2,1,0:T(8,128)S(1)}, f32[17,8,128]{2,1,0:T(8,128)S(1)}, u32[]{:S(2)}, u32[]{:S(2)}) collective-permute-start(f32[17,8,128]{2,1,0:T(8,128)S(1)} %get-tuple-element.128), channel_id=1, source_target_pairs={{0,4},{1,2},{2,1},{3,7},{4,0},{5,6},{6,5},{7,3},{8,12},{9,10},{10,... | collective-permute-start | bytes 208904 | tf_op jit(solution)/shard_map/ppermute | solution.py:670
  8.8 4.2 %collective-permute-start.4 = (f32[21,8,128]{2,1,0:T(8,128)S(1)}, f32[21,8,128]{2,1,0:T(8,128)S(1)}, u32[]{:S(2)}, u32[]{:S(2)}) collective-permute-start(f32[21,8,128]{2,1,0:T(8,128)S(1)} %get-tuple-element.156), channel_id=1, source_target_pairs={{0,1},{1,0},{2,3},{3,2},{4,8},{5,9},{6,10},{7,11},{8,4},{9,5},{10,... | collective-permute-start | bytes 258056 | tf_op jit(solution)/shard_map/ppermute | solution.py:670
  9.0 6.7 %collective-permute-start.2 = (f32[21,8,128]{2,1,0:T(8,128)S(1)}, f32[21,8,128]{2,1,0:T(8,128)S(1)}, u32[]{:S(2)}, u32[]{:S(2)}) collective-permute-start(f32[21,8,128]{2,1,0:T(8,128)S(1)} %get-tuple-element.137), channel_id=1, source_target_pairs={{0,4},{1,5},{2,6},{3,7},{4,0},{5,1},{6,2},{7,3},{8,12},{9,13},{10,... | collective-permute-start | bytes 258056 | tf_op jit(solution)/shard_map/ppermute | solution.py:670
  13.4 6.0 %collective-permute-start.6 = (f32[18,8,128]{2,1,0:T(8,128)S(1)}, f32[18,8,128]{2,1,0:T(8,128)S(1)}, u32[]{:S(2)}, u32[]{:S(2)}) collective-permute-start(f32[18,8,128]{2,1,0:T(8,128)S(1)} %get-tuple-element.174), channel_id=1, source_target_pairs={{0,1},{1,0},{2,3},{3,2},{4,8},{5,9},{6,10},{7,11},{8,4},{9,5},{10,... | collective-permute-start | bytes 221192 | tf_op jit(solution)/shard_map/ppermute | solution.py:670
  16.1 5.1 %collective-permute-start.3 = (f32[18,8,128]{2,1,0:T(8,128)S(1)}, f32[18,8,128]{2,1,0:T(8,128)S(1)}, u32[]{:S(2)}, u32[]{:S(2)}) collective-permute-start(f32[18,8,128]{2,1,0:T(8,128)S(1)} %get-tuple-element.151), channel_id=1, source_target_pairs={{0,4},{1,5},{2,6},{3,7},{4,0},{5,1},{6,2},{7,3},{8,12},{9,13},{10,... | collective-permute-start | bytes 221192 | tf_op jit(solution)/shard_map/ppermute | solution.py:670
  19.8 5.4 %collective-permute-start.8 = (f32[17,8,128]{2,1,0:T(8,128)S(1)}, f32[17,8,128]{2,1,0:T(8,128)S(1)}, u32[]{:S(2)}, u32[]{:S(2)}) collective-permute-start(f32[17,8,128]{2,1,0:T(8,128)S(1)} %get-tuple-element.192), channel_id=1, source_target_pairs={{0,1},{1,0},{2,3},{3,2},{4,8},{5,9},{6,10},{7,11},{8,4},{9,5},{10,... | collective-permute-start | bytes 208904 | tf_op jit(solution)/shard_map/ppermute | solution.py:670
  21.5 5.7 %collective-permute-start.5 = (f32[17,8,128]{2,1,0:T(8,128)S(1)}, f32[17,8,128]{2,1,0:T(8,128)S(1)}, u32[]{:S(2)}, u32[]{:S(2)}) collective-permute-start(f32[17,8,128]{2,1,0:T(8,128)S(1)} %get-tuple-element.169), channel_id=1, source_target_pairs={{0,4},{1,5},{2,6},{3,7},{4,0},{5,1},{6,2},{7,3},{8,12},{9,13},{10,... | collective-permute-start | bytes 208904 | tf_op jit(solution)/shard_map/ppermute | solution.py:670
  25.5 6.2 %collective-permute-start.9 = (f32[17,8,128]{2,1,0:T(8,128)S(1)}, f32[17,8,128]{2,1,0:T(8,128)S(1)}, u32[]{:S(2)}, u32[]{:S(2)}) collective-permute-start(f32[17,8,128]{2,1,0:T(8,128)S(1)} %get-tuple-element.234), channel_id=1, source_target_pairs={{0,1},{1,0},{2,3},{3,2},{4,8},{5,9},{6,10},{7,11},{8,4},{9,5},{10,... | collective-permute-start | bytes 208904 | tf_op jit(solution)/shard_map/ppermute | solution.py:670
  27.5 5.1 %collective-permute-start.7 = (f32[17,8,128]{2,1,0:T(8,128)S(1)}, f32[17,8,128]{2,1,0:T(8,128)S(1)}, u32[]{:S(2)}, u32[]{:S(2)}) collective-permute-start(f32[17,8,128]{2,1,0:T(8,128)S(1)} %get-tuple-element.187), channel_id=1, source_target_pairs={{0,4},{1,5},{2,6},{3,7},{4,0},{5,1},{6,2},{7,3},{8,12},{9,13},{10,... | collective-permute-start | bytes 208904 | tf_op jit(solution)/shard_map/ppermute | solution.py:670

commit v8 on v7

--- a/solution.py
+++ b/solution.py
@@ -359,7 +359,7 @@
         local = Tile(planes, columns, halo, end.flip)
         s, a = (lambda f, r, ref=ref: read(ref, f, r) for ref in group[:2])
         p = lambda f, r, end=end: read(p_out, f, end.row(r))
-        message(local, end, halo, s, a, p, *group[2:], True)
+        message(local, end, halo - 1, s, a, p, *group[2:], True)
 
 
 def sums(ff, aa):
@@ -568,7 +568,7 @@
     rows, planes, columns = p_ref.shape[1], p_ref.shape[2] // 2, p_ref.shape[3]
     side = Side(gx_axis, swap, rows)
     tile = Tile(planes, columns, halo, side.flip)
-    got = receive(tile, side, msg_ref, 2 * EDGE + (2 if first else 0), halo - 2 * j)
+    got = receive(tile, side, msg_ref, 2 * EDGE + (2 if first else 0), halo - 1 - 2 * j)
     p = lambda f, r: read(p_ref, f, side.row(r))
     old, lam = (lambda f, r: read(f_ref, f, r)), (lambda f, r: read(a_ref, f, r))
     if first:
@@ -634,7 +634,7 @@
             write(a_out, back[f] * factor, f, r)
     if not final:
         s, a = (lambda f, r: read(f_out, f, r)), (lambda f, r: read(a_out, f, r))
-        message(tile, side, halo - 2 * (j + 1), s, a, p, *outs, False)
+        message(tile, side, halo - 1 - 2 * (j + 1), s, a, p, *outs, False)
         return
     for which, out in enumerate((grad_out, par_out)):
         for n in range(out.shape[0]):
@@ -729,7 +729,7 @@
     w, m = wide[1:], own[1:]
     parts = [(6, *w), (6, *m), (6, *w)]
     mid, end = (count, rows - 4, *w), (count, 2, *w)
-    group = [end, end, tiles(2 * EDGE + 2, halo)] + parts
+    group = [end, end, tiles(2 * EDGE + 2, halo - 1)] + parts
     p, fm, am, *rest = call(
         functools.partial(spread_kernel, halo, "gx", "gy"), [(8, *wide), mid, mid] + group * 2,
         fields, field_cot, p_own, ay, by, rec,
@@ -748,7 +748,7 @@
         near_refs = rest[4:]
         for swap in (0, 1):
             f, a, _, *part_refs = ends[swap]
-            outs = [end, end, (9, *m), (7, 2, *m), (6, *m), tiles(2 * EDGE, halo - 2 * (j + 1))] + parts
+            outs = [end, end, (9, *m), (7, 2, *m), (6, *m), tiles(2 * EDGE, halo - 1 - 2 * (j + 1))] + parts
             outs += [] if j else [(2, *w)]
             f, a, vel, strain, cot, message_out, *rest = call(
                 functools.partial(end_kernel, "gx", swap, halo, j, steps), outs,

time: 33.8 us -> 33.6 us (level)
  transfers between devices with their start and end apart: 10 -> 10, of which waited for: 5 -> 5; matrix products, arithmetic and copies ran while one was open for 0% -> 0% of each run, Pallas kernels for 19% -> 20%
where the time goes in v8:
time: 33.6 us; the launch traced here: 33.5 us
  starting transfers between devices  15.6 us (46%)
  Pallas kernels  10.4 us (31%)
  waiting for transfers between devices  6.71 us (20%)
  between operations  0.79 us (2%)
    ppermute x10, starting transfers between devices, swap_rows(): return lax.ppermute(message, ('gx', 'gy'), swaps(axis, number))  15.6 us
    pallas_call x15, Pallas kernels, call(): pl.pallas_call(kernel, out_shape=shapes, in_specs=[pl.BlockSpec(memory_sp...  8.44 us
    ppermute x10, waiting for transfers between devices, swap_rows(): return lax.ppermute(message, ('gx', 'gy'), swaps(axis, number))  6.71 us
    pallas_call x1, Pallas kernels, per_device(): pl.pallas_call(start, out_shape=[jax.ShapeDtypeStruct(s, jnp.float32) for...  1.95 us
  transfers between devices with their start and end apart: 10, of which 5 were waited for; matrix products, arithmetic and copies ran while one was open for 0% of the time, Pallas kernels for 20%

profile of v8, /device:TPU:0, one launch (start us, length us, event | category | flops | bytes accessed | tf_op | source)
XLA Modules:
  0.0 33.5 jit_solution(11440283283802096678)
XLA Ops:
  0.6 1.9 %shard_map.167 = (f32[8,8,8,128]{3,2,1,0:T(8,128)S(1)}, f32[17,8,128]{2,1,0:T(8,128)S(1)}, f32[17,8,128]{2,1,0:T(8,128)S(1)}, f32[13,64,128]{2,1,0:T(8,128)S(1)}...) custom-call(f32[1,64,128]{2,1,0:T(8,128)} %bitcast.18, ...), custom_call_target="tpu_custom_call" | custom-call | tf_op jit(solution)/shard_map/pallas_call | solution.py:710
  2.6 0.6 %collective-permute-start = (f32[17,8,128]{2,1,0:T(8,128)S(1)}, f32[17,8,128]{2,1,0:T(8,128)S(1)}, u32[]{:S(2)}, u32[]{:S(2)}) collective-permute-start(f32[17,8,128]{2,1,0:T(8,128)S(1)} %get-tuple-element.127), channel_id=1, source_target_pairs={{0,1},{1,0},{2,3},{3,2},{4,5},{5,4},{6,7},{7,6},{8,9},{9,8},{10,11... | collective-permute-start | bytes 208904 | tf_op jit(solution)/shard_map/ppermute | solution.py:670
  3.2 2.6 %collective-permute-start.1 = (f32[17,8,128]{2,1,0:T(8,128)S(1)}, f32[17,8,128]{2,1,0:T(8,128)S(1)}, u32[]{:S(2)}, u32[]{:S(2)}) collective-permute-start(f32[17,8,128]{2,1,0:T(8,128)S(1)} %get-tuple-element.128), channel_id=1, source_target_pairs={{0,4},{1,2},{2,1},{3,7},{4,0},{5,6},{6,5},{7,3},{8,12},{9,10},{10,... | collective-permute-start | bytes 208904 | tf_op jit(solution)/shard_map/ppermute | solution.py:670
  5.7 1.2 %shard_map.168 = (f32[4,8,16,128]{3,2,1,0:T(8,128)S(1)}, f32[4,8,16,128]{3,2,1,0:T(8,128)S(1)}) custom-call(s32[1,512]{1,0:T(1,128)S(1)} %get-tuple-element.129.rec_ref, f32[4,512]{1,0:T(4,128)S(1)} %get-tuple-element.130.cot_ref, s32[1,64]{1,0:T(1,128)S(1)} %get-tuple-element.131.src_ref, f32[4,64]{1,0:T(4,128)S(1)} %get-tuple-element.132.amp_ref), custom_call_target="tpu_custom_call" | custom-call | tf_op jit(solution)/shard_map/pallas_call | solution.py:675
  6.9 0.0 collective-permute-done.ay_ref
  6.9 1.1 %collective-permute-done.1.by_ref = f32[17,8,128]{2,1,0:T(8,128)S(1)} collective-permute-done((f32[17,8,128]{2,1,0:T(8,128)S(1)}, f32[17,8,128]{2,1,0:T(8,128)S(1)}, u32[]{:S(2)}, u32[]{:S(2)}) %collective-permute-start.1) | collective-permute-done | bytes 69664 | tf_op jit(solution)/shard_map/ppermute | solution.py:670
  8.0 0.8 %shard_map.169 = (f32[8,8,16,128]{3,2,1,0:T(8,128)S(1)}, f32[13,4,16,128]{3,2,1,0:T(8,128)S(1)}, f32[13,4,16,128]{3,2,1,0:T(8,128)S(1)}, f32[13,2,16,128]{3,2,1,...) custom-call(f32[13,64,128]{2,1,0:T(8,128)S(1)} %get-tuple-element.12, ...), custom_call_target="tpu_custom_call" | custom-call | tf_op jit(solution)/shard_map/pallas_call | solution.py:675
  8.8 0.2 collective-permute-start.4
  9.0 3.5 %collective-permute-start.2 = (f32[20,8,128]{2,1,0:T(8,128)S(1)}, f32[20,8,128]{2,1,0:T(8,128)S(1)}, u32[]{:S(2)}, u32[]{:S(2)}) collective-permute-start(f32[20,8,128]{2,1,0:T(8,128)S(1)} %get-tuple-element.137), channel_id=1, source_target_pairs={{0,4},{1,5},{2,6},{3,7},{4,0},{5,1},{6,2},{7,3},{8,12},{9,13},{10,... | collective-permute-start | bytes 245768 | tf_op jit(solution)/shard_map/ppermute | solution.py:670
  12.5 0.6 %shard_map.170 = (f32[13,4,16,128]{3,2,1,0:T(8,128)S(1)}, f32[13,4,16,128]{3,2,1,0:T(8,128)S(1)}, f32[9,6,8,128]{3,2,1,0:T(8,128)S(1)}, f32[7,4,8,128]{3,2,1,0:T...) custom-call(f32[13,4,16,128]{3,2,1,0:T(8,128)S(1)} %get-tuple-elemen, ...), custom_call_target="tpu_custom_call" | custom-call | tf_op jit(solution)/shard_map/pallas_call | solution.py:675
  13.0 0.0 collective-permute-done.4.refs_3_
  13.1 0.4 %shard_map.172 = (f32[13,2,16,128]{3,2,1,0:T(8,128)S(1)}, f32[13,2,16,128]{3,2,1,0:T(8,128)S(1)}, f32[9,8,128]{2,1,0:T(8,128)S(1)}, f32[7,2,8,128]{3,2,1,0:T(8,1...) custom-call(f32[13,2,16,128]{3,2,1,0:T(8,128)S(1)} %get-tuple-elemen, ...), custom_call_target="tpu_custom_call" | custom-call | tf_op jit(solution)/shard_map/pallas_call | solution.py:675
  13.4 0.1 collective-permute-start.6
  13.5 2.1 %collective-permute-done.2.refs_3_ = f32[20,8,128]{2,1,0:T(8,128)S(1)} collective-permute-done((f32[20,8,128]{2,1,0:T(8,128)S(1)}, f32[20,8,128]{2,1,0:T(8,128)S(1)}, u32[]{:S(2)}, u32[]{:S(2)}) %collective-permute-start.2) | collective-permute-done | bytes 81952 | tf_op jit(solution)/shard_map/ppermute | solution.py:670
  15.6 0.3 shard_map.171
  15.9 2.9 %collective-permute-start.3 = (f32[18,8,128]{2,1,0:T(8,128)S(1)}, f32[18,8,128]{2,1,0:T(8,128)S(1)}, u32[]{:S(2)}, u32[]{:S(2)}) collective-permute-start(f32[18,8,128]{2,1,0:T(8,128)S(1)} %get-tuple-element.151), channel_id=1, source_target_pairs={{0,4},{1,5},{2,6},{3,7},{4,0},{5,1},{6,2},{7,3},{8,12},{9,13},{10,... | collective-permute-start | bytes 221192 | tf_op jit(solution)/shard_map/ppermute | solution.py:670
  18.8 0.6 %shard_map.173 = (f32[13,4,16,128]{3,2,1,0:T(8,128)S(1)}, f32[13,4,16,128]{3,2,1,0:T(8,128)S(1)}, f32[9,6,8,128]{3,2,1,0:T(8,128)S(1)}, f32[7,4,8,128]{3,2,1,0:T...) custom-call(f32[13,4,16,128]{3,2,1,0:T(8,128)S(1)} %get-tuple-elemen, ...), custom_call_target="tpu_custom_call" | custom-call | tf_op jit(solution)/shard_map/pallas_call | solution.py:675
  19.3 0.0 collective-permute-done.6.refs_3_
  19.3 0.3 %shard_map.175 = (f32[13,2,16,128]{3,2,1,0:T(8,128)S(1)}, f32[13,2,16,128]{3,2,1,0:T(8,128)S(1)}, f32[9,8,128]{2,1,0:T(8,128)S(1)}, f32[7,2,8,128]{3,2,1,0:T(8,1...) custom-call(f32[13,2,16,128]{3,2,1,0:T(8,128)S(1)} %get-tuple-elemen, ...), custom_call_target="tpu_custom_call" | custom-call | tf_op jit(solution)/shard_map/pallas_call | solution.py:675
  19.7 0.1 collective-permute-start.8
  19.8 1.3 %collective-permute-done.3.refs_3_ = f32[18,8,128]{2,1,0:T(8,128)S(1)} collective-permute-done((f32[18,8,128]{2,1,0:T(8,128)S(1)}, f32[18,8,128]{2,1,0:T(8,128)S(1)}, u32[]{:S(2)}, u32[]{:S(2)}) %collective-permute-start.3) | collective-permute-done | bytes 73760 | tf_op jit(solution)/shard_map/ppermute | solution.py:670
  21.1 0.3 shard_map.174
  21.4 3.1 %collective-permute-start.5 = (f32[17,8,128]{2,1,0:T(8,128)S(1)}, f32[17,8,128]{2,1,0:T(8,128)S(1)}, u32[]{:S(2)}, u32[]{:S(2)}) collective-permute-start(f32[17,8,128]{2,1,0:T(8,128)S(1)} %get-tuple-element.169), channel_id=1, source_target_pairs={{0,4},{1,5},{2,6},{3,7},{4,0},{5,1},{6,2},{7,3},{8,12},{9,13},{10,... | collective-permute-start | bytes 208904 | tf_op jit(solution)/shard_map/ppermute | solution.py:670
  24.5 0.6 %shard_map.176 = (f32[13,4,16,128]{3,2,1,0:T(8,128)S(1)}, f32[13,4,16,128]{3,2,1,0:T(8,128)S(1)}, f32[9,6,8,128]{3,2,1,0:T(8,128)S(1)}, f32[7,4,8,128]{3,2,1,0:T...) custom-call(f32[13,4,16,128]{3,2,1,0:T(8,128)S(1)} %get-tuple-elemen, ...), custom_call_target="tpu_custom_call" | custom-call | tf_op jit(solution)/shard_map/pallas_call | solution.py:675
  25.1 0.0 collective-permute-done.8.refs_3_
  25.1 0.3 %shard_map.178 = (f32[13,2,16,128]{3,2,1,0:T(8,128)S(1)}, f32[13,2,16,128]{3,2,1,0:T(8,128)S(1)}, f32[9,8,128]{2,1,0:T(8,128)S(1)}, f32[7,2,8,128]{3,2,1,0:T(8,1...) custom-call(f32[13,2,16,128]{3,2,1,0:T(8,128)S(1)} %get-tuple-elemen, ...), custom_call_target="tpu_custom_call" | custom-call | tf_op jit(solution)/shard_map/pallas_call | solution.py:675
  25.4 0.1 collective-permute-start.9
  25.5 1.6 %collective-permute-done.5.refs_3_ = f32[17,8,128]{2,1,0:T(8,128)S(1)} collective-permute-done((f32[17,8,128]{2,1,0:T(8,128)S(1)}, f32[17,8,128]{2,1,0:T(8,128)S(1)}, u32[]{:S(2)}, u32[]{:S(2)}) %collective-permute-start.5) | collective-permute-done | bytes 69664 | tf_op jit(solution)/shard_map/ppermute | solution.py:670
  27.1 0.3 shard_map.177
  27.4 2.7 %collective-permute-start.7 = (f32[17,8,128]{2,1,0:T(8,128)S(1)}, f32[17,8,128]{2,1,0:T(8,128)S(1)}, u32[]{:S(2)}, u32[]{:S(2)}) collective-permute-start(f32[17,8,128]{2,1,0:T(8,128)S(1)} %get-tuple-element.187), channel_id=1, source_target_pairs={{0,4},{1,5},{2,6},{3,7},{4,0},{5,1},{6,2},{7,3},{8,12},{9,13},{10,... | collective-permute-start | bytes 208904 | tf_op jit(solution)/shard_map/ppermute | solution.py:670
  30.1 0.2 shard_map.179
  30.3 1.3 %shard_map.180 = (f32[13,4,8,128]{3,2,1,0:T(8,128)S(1)}, f32[7,4,8,128]{3,2,1,0:T(8,128)S(1)}, f32[9,6,8,128]{3,2,1,0:T(8,128)S(1)}, f32[7,4,8,128]{3,2,1,0:T(8,...) custom-call(f32[13,4,16,128]{3,2,1,0:T(8,128)S(1)} %get-tuple-elemen, ...), custom_call_target="tpu_custom_call" | custom-call | tf_op jit(solution)/shard_map/pallas_call | solution.py:675
  31.5 0.0 collective-permute-done.9.refs_3_
  31.5 0.2 shard_map.181
  31.7 0.7 %collective-permute-done.7.refs_3_ = f32[17,8,128]{2,1,0:T(8,128)S(1)} collective-permute-done((f32[17,8,128]{2,1,0:T(8,128)S(1)}, f32[17,8,128]{2,1,0:T(8,128)S(1)}, u32[]{:S(2)}, u32[]{:S(2)}) %collective-permute-start.7) | collective-permute-done | bytes 69664 | tf_op jit(solution)/shard_map/ppermute | solution.py:670
  32.4 1.1 %shard_map.182 = (f32[13,64,128]{2,1,0:T(8,128)}, f32[7,64,128]{2,1,0:T(8,128)}) custom-call(f32[13,2,16,128]{3,2,1,0:T(8,128)S(1)} %get-tuple-element.185.refs_2_.refs_0_, f32[13,2,16,128]{3,2,1,0:T(8,128)S(1)} %get-tuple-element.186.refs_5_.refs_1_, f32[8,8,16,128]{3,2,1,0:T(8,128)S(1)} %get-tuple-element.136.refs_6_.refs_2_, ...), custom_call_target="tpu_custom_call" | custom-call | tf_op jit(solution)/shard_map/pallas_call | solution.py:675
Async XLA Ops:
  2.6 4.3 %collective-permute-start = (f32[17,8,128]{2,1,0:T(8,128)S(1)}, f32[17,8,128]{2,1,0:T(8,128)S(1)}, u32[]{:S(2)}, u32[]{:S(2)}) collective-permute-start(f32[17,8,128]{2,1,0:T(8,128)S(1)} %get-tuple-element.127), channel_id=1, source_target_pairs={{0,1},{1,0},{2,3},{3,2},{4,5},{5,4},{6,7},{7,6},{8,9},{9,8},{10,11... | collective-permute-start | bytes 208904 | tf_op jit(solution)/shard_map/ppermute | solution.py:670
  3.2 4.8 %collective-permute-start.1 = (f32[17,8,128]{2,1,0:T(8,128)S(1)}, f32[17,8,128]{2,1,0:T(8,128)S(1)}, u32[]{:S(2)}, u32[]{:S(2)}) collective-permute-start(f32[17,8,128]{2,1,0:T(8,128)S(1)} %get-tuple-element.128), channel_id=1, source_target_pairs={{0,4},{1,2},{2,1},{3,7},{4,0},{5,6},{6,5},{7,3},{8,12},{9,10},{10,... | collective-permute-start | bytes 208904 | tf_op jit(solution)/shard_map/ppermute | solution.py:670
  8.8 4.2 %collective-permute-start.4 = (f32[20,8,128]{2,1,0:T(8,128)S(1)}, f32[20,8,128]{2,1,0:T(8,128)S(1)}, u32[]{:S(2)}, u32[]{:S(2)}) collective-permute-start(f32[20,8,128]{2,1,0:T(8,128)S(1)} %get-tuple-element.156), channel_id=1, source_target_pairs={{0,1},{1,0},{2,3},{3,2},{4,8},{5,9},{6,10},{7,11},{8,4},{9,5},{10,... | collective-permute-start | bytes 245768 | tf_op jit(solution)/shard_map/ppermute | solution.py:670
  9.0 6.5 %collective-permute-start.2 = (f32[20,8,128]{2,1,0:T(8,128)S(1)}, f32[20,8,128]{2,1,0:T(8,128)S(1)}, u32[]{:S(2)}, u32[]{:S(2)}) collective-permute-start(f32[20,8,128]{2,1,0:T(8,128)S(1)} %get-tuple-element.137), channel_id=1, source_target_pairs={{0,4},{1,5},{2,6},{3,7},{4,0},{5,1},{6,2},{7,3},{8,12},{9,13},{10,... | collective-permute-start | bytes 245768 | tf_op jit(solution)/shard_map/ppermute | solution.py:670
  13.4 5.9 %collective-permute-start.6 = (f32[18,8,128]{2,1,0:T(8,128)S(1)}, f32[18,8,128]{2,1,0:T(8,128)S(1)}, u32[]{:S(2)}, u32[]{:S(2)}) collective-permute-start(f32[18,8,128]{2,1,0:T(8,128)S(1)} %get-tuple-element.174), channel_id=1, source_target_pairs={{0,1},{1,0},{2,3},{3,2},{4,8},{5,9},{6,10},{7,11},{8,4},{9,5},{10,... | collective-permute-start | bytes 221192 | tf_op jit(solution)/shard_map/ppermute | solution.py:670
  15.9 5.2 %collective-permute-start.3 = (f32[18,8,128]{2,1,0:T(8,128)S(1)}, f32[18,8,128]{2,1,0:T(8,128)S(1)}, u32[]{:S(2)}, u32[]{:S(2)}) collective-permute-start(f32[18,8,128]{2,1,0:T(8,128)S(1)} %get-tuple-element.151), channel_id=1, source_target_pairs={{0,4},{1,5},{2,6},{3,7},{4,0},{5,1},{6,2},{7,3},{8,12},{9,13},{10,... | collective-permute-start | bytes 221192 | tf_op jit(solution)/shard_map/ppermute | solution.py:670
  19.7 5.4 %collective-permute-start.8 = (f32[17,8,128]{2,1,0:T(8,128)S(1)}, f32[17,8,128]{2,1,0:T(8,128)S(1)}, u32[]{:S(2)}, u32[]{:S(2)}) collective-permute-start(f32[17,8,128]{2,1,0:T(8,128)S(1)} %get-tuple-element.192), channel_id=1, source_target_pairs={{0,1},{1,0},{2,3},{3,2},{4,8},{5,9},{6,10},{7,11},{8,4},{9,5},{10,... | collective-permute-start | bytes 208904 | tf_op jit(solution)/shard_map/ppermute | solution.py:670
  21.4 5.7 %collective-permute-start.5 = (f32[17,8,128]{2,1,0:T(8,128)S(1)}, f32[17,8,128]{2,1,0:T(8,128)S(1)}, u32[]{:S(2)}, u32[]{:S(2)}) collective-permute-start(f32[17,8,128]{2,1,0:T(8,128)S(1)} %get-tuple-element.169), channel_id=1, source_target_pairs={{0,4},{1,5},{2,6},{3,7},{4,0},{5,1},{6,2},{7,3},{8,12},{9,13},{10,... | collective-permute-start | bytes 208904 | tf_op jit(solution)/shard_map/ppermute | solution.py:670
  25.4 6.1 %collective-permute-start.9 = (f32[17,8,128]{2,1,0:T(8,128)S(1)}, f32[17,8,128]{2,1,0:T(8,128)S(1)}, u32[]{:S(2)}, u32[]{:S(2)}) collective-permute-start(f32[17,8,128]{2,1,0:T(8,128)S(1)} %get-tuple-element.234), channel_id=1, source_target_pairs={{0,1},{1,0},{2,3},{3,2},{4,8},{5,9},{6,10},{7,11},{8,4},{9,5},{10,... | collective-permute-start | bytes 208904 | tf_op jit(solution)/shard_map/ppermute | solution.py:670
  27.4 5.0 %collective-permute-start.7 = (f32[17,8,128]{2,1,0:T(8,128)S(1)}, f32[17,8,128]{2,1,0:T(8,128)S(1)}, u32[]{:S(2)}, u32[]{:S(2)}) collective-permute-start(f32[17,8,128]{2,1,0:T(8,128)S(1)} %get-tuple-element.187), channel_id=1, source_target_pairs={{0,4},{1,5},{2,6},{3,7},{4,0},{5,1},{6,2},{7,3},{8,12},{9,13},{10,... | collective-permute-start | bytes 208904 | tf_op jit(solution)/shard_map/ppermute | solution.py:670
